TPU v7x, 32 devices: a whole 2x2x4 slice. The times are simulated.
32 devices in a mesh: gx: 4 (over z), gy: 4 (over x, core), gz: 2 (over y).
Axes of the slice: x: 2, y: 2, z: 4, core: 2. Of those that a mesh axis runs over, the one named last changes fastest.
Arguments:
- pressure: float32 [128, 128, 256], P('gx', 'gy', 'gz'), may hold values from -2.5 to 2.5
- source: float32 [128, 128, 256], P('gx', 'gy', 'gz'), may hold values from -40 to 40
- saturation: float32 [128, 128, 256], P('gx', 'gy', 'gz'), may hold values from 0.1 to 0.9
- permeability: float32 [128, 128, 256], P('gx', 'gy', 'gz'), may hold values from 0.1 to 10
- compress: float32 [128, 128, 256], P('gx', 'gy', 'gz'), may hold values from 0.1 to 1
- porosity: float32 [128, 128, 256], P('gx', 'gy', 'gz'), may hold values from 0.1 to 0.3
- rock_type: int32 [128, 128, 256], P('gx', 'gy', 'gz'), may hold values from 0 to 7
- well_mask: int32 [128, 128, 256], P('gx', 'gy', 'gz'), may hold values 0 or 1
- oil_factor: float32 [8], replicated, may hold values from 0.3 to 3
Outputs:
- pressure_new: float32 [128, 128, 256], P('gx', 'gy', 'gz')
- residual_new: float32 [128, 128, 256], P('gx', 'gy', 'gz')
- saturation_new: float32 [128, 128, 256], P('gx', 'gy', 'gz')
All inputs are finite; a program needn't handle non-finite values. No bound on the sum of `well_mask` on one device may be relied on, other than what follows from the above.
Results may differ from a plain program's by a relative error of at most 0.0003.
Values sent between devices are 32-bit elements; how exact they have to be, the bound alone decides.
No kernel may reach another device: no remote copies, remote signals or barrier semaphores. Data moves between devices by JAX's collectives and lax.ppermute only.
A program may use at most 64 MiB of HBM per device.

v0:
```python
import functools
import math

import jax
import jax.numpy as jnp
import numpy as np
from jax import lax
from jax.experimental import pallas as pl
from jax.experimental.pallas import tpu as pltpu
from jax.sharding import PartitionSpec as P

INTERSECTION = 8
NEWTON = 3

WELL_INDEX = 4.0
INJECT_RATE = 2.0
TIME_STEP = 0.05

AXES = ("gx", "gy", "gz")
F32 = jnp.float32
HIGH = lax.Precision.HIGHEST
MSG_ROWS = 16


def sine_basis(length):
    points = np.arange(length) + 1
    angles = np.outer(points, points) % (2 * (length + 1)) * (math.pi / (length + 1))
    table = math.sqrt(2.0 / (length + 1)) * np.sin(angles)
    eigen = 2.0 - 2.0 * np.cos(points * (math.pi / (length + 1)))
    return table, eigen


def sweep_factors(count, eigen_y, eigen_z):
    shift = 2.0 + eigen_y[:, None] + eigen_z[None, :]
    factors = []
    last = np.zeros_like(shift)
    for _ in range(count):
        last = 1.0 / (shift - last)
        factors.append(last)
    return np.stack(factors), 1.0 / (1.0 - last * last)


def pairs(count, periodic, parity):
    if periodic and count % 2:
        step = 1 if parity == 0 else -1
        return [(i, (i + step) % count) for i in range(count)]
    out = []
    for i in range(parity, count, 2):
        j = i + 1
        if periodic:
            j = j % count
        if j < count:
            out += [(i, j), (j, i)]
    return out


def harmonic(one, two):
    return 2.0 * one * two / (one + two)


def dot(one, two, dims=((1,), (0,))):
    return lax.dot_general(
        one, two, (dims, ((), ())), precision=HIGH, preferred_element_type=F32
    )


def rows_of(shape):
    return lax.broadcasted_iota(jnp.int32, shape, 0)


def lanes_of(shape):
    return lax.broadcasted_iota(jnp.int32, shape, 1)


def back(value, axis):
    return pltpu.roll(value, value.shape[axis] - 1, axis)


def ahead(value, axis):
    return pltpu.roll(value, 1, axis)


class Plan:
    def __init__(self, nx, ny, nz, counts):
        self.nx, self.ny, self.nz = nx, ny, nz
        self.counts = counts
        self.z_msgs = [q for q in (0, 1) if pairs(counts["gz"], False, q)]

    def perm(self, axis, which):
        return pairs(self.counts[axis], axis != "gz", which)

    def high(self, axis, which):
        if axis != "gz" and self.counts[axis] % 2:
            return (which == 0, which == 1)
        up = (lax.axis_index(axis) % 2) == which
        return (up, up)


def call(kernel, outs, args, scratch=(), aliases=None, smem=(), limit=28):
    vmem = pl.BlockSpec(memory_space=pltpu.VMEM)
    return pl.pallas_call(
        kernel,
        out_shape=[jax.ShapeDtypeStruct(s, F32) for s in outs],
        in_specs=[
            pl.BlockSpec(memory_space=pltpu.SMEM) if k in smem else vmem
            for k in range(len(args))
        ],
        out_specs=[vmem] * len(outs),
        scratch_shapes=[pltpu.VMEM(s, F32) for s in scratch],
        input_output_aliases=aliases or {},
        compiler_params=pltpu.CompilerParams(vmem_limit_bytes=limit << 20),
    )(*args)


def side(plan, axis, ref_a, ref_b, high):
    a_high = plan.high(axis, 0)[1]
    if high:
        return jnp.where(a_high, ref_a, ref_b)
    return jnp.where(a_high, ref_b, ref_a)


def pack_x(plan, ref, out_a, out_b):
    last = plan.nx - 1
    for which, out in ((0, out_a), (1, out_b)):
        out[...] = ref[jnp.where(plan.high("gx", which)[0], last, 0)]


def pack_y(plan, ref, out_a, out_b):
    low, top = ref[:, 0, :], ref[:, plan.ny - 1, :]
    for which, out in ((0, out_a), (1, out_b)):
        out[...] = jnp.where(plan.high("gy", which)[0], top, low)


def pack_z(plan, flat, outs):
    for q, out in zip(plan.z_msgs, outs):
        face = jnp.where(plan.high("gz", q)[0], plan.nz - 1, 0)
        pick = (rows_of((8, plan.nz)) == 0) & (lanes_of((8, plan.nz)) == face)
        out[...] = dot(pick.astype(F32), flat, ((1,), (1,)))


def columns(rows):
    eye = (rows_of((8, 128)) == lanes_of((8, 128))).astype(F32)
    return dot(rows, eye, ((0,), (0,)))


def stack_rows(parts):
    cells = parts[0].shape[1]
    row = rows_of((8, cells))
    out = jnp.zeros((8, cells), F32)
    for k, part in enumerate(parts):
        out = jnp.where(row == k, jnp.broadcast_to(part, (8, cells)), out)
    return out


def z_sides(plan, vals):
    low, top = jnp.zeros_like(vals[0]), jnp.zeros_like(vals[0])
    for q, val in zip(plan.z_msgs, vals):
        up = plan.high("gz", q)[1]
        low = low + jnp.where(up, 0.0, val)
        top = top + jnp.where(up, val, 0.0)
    return low, top


def mobility_kernel(
    plan, press, sat, perm, rock, oil, mob, coef, frac, xa, xb, ya, yb, total
):
    kinds = oil.shape[0]

    def layer(i, acc):
        s, kind = sat[i], rock[i]
        c = jnp.full(s.shape, oil[0], F32)
        for k in range(1, kinds):
            c = jnp.where(kind == k, oil[k], c)
        water, rest = s * s, 1.0 - s
        den = water + c * rest * rest
        m = perm[i] * den
        coef[i] = c
        mob[i] = m
        frac[i] = water / den
        return acc + m

    total[...] = lax.fori_loop(
        0, plan.nx, layer, jnp.zeros((plan.ny, plan.nz), F32), unroll=2
    )
    for k, ref in enumerate((press, mob, frac)):
        pack_x(plan, ref, xa.at[k], xb.at[k])
        pack_y(plan, ref, ya.at[k], yb.at[k])


def inner_kernel(plan, press, mob, source, compress, well, res, tx, ty, tz, diag):
    shape = (plan.ny, plan.nz)
    row, lane = rows_of(shape), lanes_of(shape)

    def layer(i, carry):
        p_last, m_last, r_last = carry
        p, m = press[i], mob[i]
        t = harmonic(m_last, m)
        tx[i] = t
        flux_x = t * (p_last - p)
        t = harmonic(jnp.where(row == 0, 0.0, ahead(m, 0)), m)
        ty[i] = t
        flux_y = t * (ahead(p, 0) - p)
        t = harmonic(jnp.where(lane == 0, 0.0, ahead(m, 1)), m)
        tz[i] = t
        flux_z = t * (ahead(p, 1) - p)
        d = compress[i] + WELL_INDEX * well[i].astype(F32) * m
        diag[i] = d
        r = source[i] - d * p + flux_x + (flux_y - back(flux_y, 0)) + (flux_z - back(flux_z, 1))
        res[jnp.maximum(i - 1, 0)] = r_last - flux_x
        return p, m, r

    zero = jnp.zeros(shape, F32)
    res[plan.nx - 1] = lax.fori_loop(0, plan.nx, layer, (zero, zero, zero), unroll=2)[2]


def rim_kernel(plan, res_in, press, mob, frac, xa, xb, ya, yb, res, *rest):
    z_outs, comp = rest[:-1], rest[-1]
    nx, ny, nz = plan.nx, plan.ny, plan.nz
    last = nx - 1
    for high, k in ((False, 0), (True, last)):
        p, m = (side(plan, "gx", xa[f], xb[f], high) for f in (0, 1))
        res[k] = res[k] + harmonic(mob[k], m) * (p - press[k])
    for high, k in ((False, 0), (True, ny - 1)):
        p, m = (side(plan, "gy", ya[f], yb[f], high) for f in (0, 1))
        res[:, k, :] = res[:, k, :] + harmonic(mob[:, k, :], m) * (p - press[:, k, :])
    lane = lanes_of((ny, nz))
    pick = (rows_of((MSG_ROWS, nz)) == lanes_of((MSG_ROWS, nz))).astype(F32)
    wide = INTERSECTION
    for q, out in zip(plan.z_msgs, z_outs):
        up = plan.high("gz", q)[0]

        def layer(i, carry):
            acc = jnp.where(
                lane < wide, jnp.where(up, pltpu.roll(res[i], wide, 1), res[i]), 0.0
            )
            for k, ref in enumerate((press, mob, frac)):
                moved = jnp.where(
                    up,
                    pltpu.roll(ref[i], wide + k + 1, 1),
                    pltpu.roll(ref[i], wide + k, 1),
                )
                acc = jnp.where(lane == wide + k, moved, acc)
            comp[pl.ds(i * ny, ny), :] = acc
            return carry

        lax.fori_loop(0, nx, layer, 0, unroll=2)
        out[...] = dot(pick, comp[...], ((1,), (1,)))


def z_flux(plan, sent, got):
    wide = INTERSECTION
    out = []
    for own, other in zip(sent, got):
        t = harmonic(own[wide + 1 : wide + 2, :], other[wide + 1 : wide + 2, :])
        q = t * (other[wide : wide + 1, :] - own[wide : wide + 1, :])
        out.append((other[wide : wide + 1, :], other[wide + 2 : wide + 3, :], t, q))
    return out


def z_kernel(plan, n_msg, res, basis, rim_low, rim_top, *rest):
    sent, got = rest[:n_msg], rest[n_msg : 2 * n_msg]
    spec, ya, yb = rest[2 * n_msg :]
    nx, ny, nz = plan.nx, plan.ny, plan.nz
    wide = INTERSECTION
    out = dot(res[...].reshape(nx * ny, nz), basis[...])
    for q, other, (_, _, _, flux) in zip(plan.z_msgs, got, z_flux(plan, sent, got)):
        up = plan.high("gz", q)[1]
        row = rows_of(other.shape)
        near = jnp.where(up, 0, wide - 1)
        flux = jnp.broadcast_to(flux, other.shape)
        mix = jnp.where(row < wide, other[...], 0.0)
        mix = jnp.where(row == near, mix - flux, mix)
        mix = jnp.where(row == wide, flux, mix)
        rim = jnp.where(up, rim_top[...], rim_low[...])
        out = out + dot(mix, rim, ((0,), (0,)))
    spec[...] = out.reshape(nx, ny, out.shape[1])
    low, top = spec[:, :wide, :], spec[:, ny - wide :, :]
    for which, ref in ((0, ya), (1, yb)):
        ref[...] = jnp.where(plan.high("gy", which)[0], top, low)


def faces_kernel(plan, n_msg, res, mob, tx_in, ty_in, tz_in, xa, xb, ya, yb, *rest):
    sent, got = rest[:n_msg], rest[n_msg : 2 * n_msg]
    full, tx, ty_low, ty_top, tz_low, tz_top, hx, hy, hz, ty_rim = rest[2 * n_msg :]
    nx, ny, nz = plan.nx, plan.ny, plan.nz
    parts = z_flux(plan, sent, got)
    split = [z_sides(plan, [part[k] for part in parts]) for k in range(4)]
    hz[...] = columns(stack_rows([v for pair in split for v in pair]))
    for k, high in ((0, False), (1, True)):
        for f, field in ((0, 0), (1, 2)):
            hx[k, f] = side(plan, "gx", xa[field], xb[field], high)
            hy[k, f] = side(plan, "gy", ya[field], yb[field], high)
    tx[0] = harmonic(mob[0], side(plan, "gx", xa[1], xb[1], False))
    tx[nx] = harmonic(mob[nx - 1], side(plan, "gx", xa[1], xb[1], True))
    ty_rim[0] = harmonic(mob[:, 0, :], side(plan, "gy", ya[1], yb[1], False))
    ty_rim[1] = harmonic(mob[:, ny - 1, :], side(plan, "gy", ya[1], yb[1], True))
    row, lane = rows_of((ny, nz)), lanes_of((ny, nz))

    def layer(i, carry):
        @pl.when(i > 0)
        def _():
            tx[i] = tx_in[i]

        ty = ty_in[i]
        ty_low[i] = jnp.where(row == 0, ty_rim[0, pl.ds(i, 1), :], ty)
        ty_top[i] = jnp.where(row == ny - 1, ty_rim[1, pl.ds(i, 1), :], back(ty, 0))
        tz = tz_in[i]
        col = hz[pl.ds(i * ny, ny), :]
        tz_low[i] = jnp.where(lane == 0, col[:, 4:5], tz)
        tz_top[i] = jnp.where(lane == nz - 1, col[:, 5:6], back(tz, 1))
        flux = jnp.where(lane == 0, col[:, 6:7], 0.0) + jnp.where(
            lane == nz - 1, col[:, 7:8], 0.0
        )
        full[i] = res[i] + flux
        return carry

    lax.fori_loop(0, nx, layer, 0, unroll=2)


def y_kernel(plan, spec, ya, yb, basis, factors, modes, xa, xb):
    nx = plan.nx
    wide = INTERSECTION

    def layer(i, carry):
        low = side(plan, "gy", ya[i], yb[i], False)
        top = side(plan, "gy", ya[i], yb[i], True)
        modes[i] = dot(basis[...], jnp.concatenate([low, spec[i], top], axis=0))
        return carry

    lax.fori_loop(0, nx, layer, 0, unroll=2)
    low = jnp.zeros(modes.shape[1:], F32)
    top = low
    for k in range(wide):
        low = (modes[wide - 1 - k] + low) * factors[k]
        top = (modes[nx - wide + k] + top) * factors[k]
    for which, out in ((0, xa), (1, xb)):
        out[...] = jnp.where(plan.high("gx", which)[0], top, low)


def solve_kernel(
    plan, modes, xa, xb, factors, middle, basis_y, basis_z, total, direction, *rest
):
    (dxa, dxb, dya, dyb), z_outs, work = rest[:4], rest[4:-1], rest[-1]
    nx, ny, nz = plan.nx, plan.ny, plan.nz
    wide = INTERSECTION
    half = nx // 2
    low = side(plan, "gx", xa[...], xb[...], False)
    top = side(plan, "gx", xa[...], xb[...], True)

    def inward(k, carry):
        low, top = carry
        c = factors[wide + k]
        low = (modes[k] + low) * c
        top = (modes[nx - 1 - k] + top) * c
        modes[k] = low
        modes[nx - 1 - k] = top
        return low, top

    low, top = lax.fori_loop(0, half, inward, (low, top), unroll=2)
    c, mid = factors[wide + half - 1], middle[...]
    low, top = (low + c * top) * mid, (top + c * low) * mid

    def put(i, value):
        work[pl.ds(i * ny, ny), :] = dot(basis_y[...], value)

    put(half - 1, low)
    put(half, top)

    def outward(k, carry):
        low, top = carry
        i = half - 2 - k
        c = factors[wide + i]
        low = modes[i] + c * low
        top = modes[nx - 1 - i] + c * top
        put(i, low)
        put(nx - 1 - i, top)
        return low, top

    lax.fori_loop(0, half - 1, outward, (low, top), unroll=2)
    mean = jnp.sum(jnp.sum(total[...], axis=0, keepdims=True), axis=1, keepdims=True) / (
        nx * ny * nz
    )
    flat = dot(work[...], basis_z[...]) / mean
    direction[...] = flat.reshape(nx, ny, nz)
    pack_x(plan, direction, dxa, dxb)
    pack_y(plan, direction, dya, dyb)
    pack_z(plan, flat, z_outs)


def image_kernel(
    plan, n_dev, direction, diag, full, tx, ty_low, ty_top, tz_low, tz_top, xa, xb, ya, yb, *rest
):
    n_msg = len(plan.z_msgs)
    got = rest[:n_msg]
    image, sums, hz, hy = rest[n_msg:]
    nx, ny, nz = plan.nx, plan.ny, plan.nz
    hz[...] = columns(stack_rows(z_sides(plan, [ref[0:1, :] for ref in got])))
    hy[0] = side(plan, "gy", ya[...], yb[...], False)
    hy[1] = side(plan, "gy", ya[...], yb[...], True)
    row, lane = rows_of((ny, nz)), lanes_of((ny, nz))

    def layer(i, carry):
        d_last, im_last, rd, da = carry
        d = direction[i]
        flux = tx[i] * (d_last - d)
        col = hz[pl.ds(i * ny, ny), :]
        y_last = jnp.where(row == 0, hy[0, pl.ds(i, 1), :], ahead(d, 0))
        y_next = jnp.where(row == ny - 1, hy[1, pl.ds(i, 1), :], back(d, 0))
        z_last = jnp.where(lane == 0, col[:, 0:1], ahead(d, 1))
        z_next = jnp.where(lane == nz - 1, col[:, 1:2], back(d, 1))
        im = (
            diag[i] * d
            - flux
            + (ty_low[i] * (d - y_last) + ty_top[i] * (d - y_next))
            + (tz_low[i] * (d - z_last) + tz_top[i] * (d - z_next))
        )
        im_last = im_last + flux
        image[jnp.maximum(i - 1, 0)] = im_last
        rd = rd + full[i] * d
        da = da + jnp.where(i > 0, d_last, 0.0) * im_last
        return d, im, rd, da

    zero = jnp.zeros((ny, nz), F32)
    low = side(plan, "gx", xa[...], xb[...], False)
    top = side(plan, "gx", xa[...], xb[...], True)
    d, im, rd, da = lax.fori_loop(0, nx, layer, (low, zero, zero, zero), unroll=2)
    im = im + tx[nx] * (d - top)
    image[nx - 1] = im
    da = da + d * im
    lane = lanes_of((n_dev, 128))
    sums[...] = jnp.where(lane < 64, jnp.sum(rd), jnp.sum(da))


def sweep(plan, first, last_sweep, refs):
    nx, ny, nz = plan.nx, plan.ny, plan.nz
    (start, now, frac, coef, poro, well, gx, gy_low, gy_top, gz_low, gz_top, outflow) = refs[:12]
    x_low, x_top, hy, col_at, new, new_frac = refs[12:]
    row, lane = rows_of((ny, nz)), lanes_of((ny, nz))

    def upwind(g, low, high):
        return g * jnp.where(g > 0.0, low, high)

    def layer(i, carry):
        f, flow = carry
        is_end = i == nx - 1
        f_next = jnp.where(is_end, x_top, frac[jnp.minimum(i + 1, nx - 1)])
        s, c = now[i], coef[i]
        flow_next = upwind(gx[i + 1], f, f_next)
        y_last = jnp.where(row == 0, hy[0, pl.ds(i, 1), :], ahead(f, 0))
        y_next = jnp.where(row == ny - 1, hy[1, pl.ds(i, 1), :], back(f, 0))
        z_low, z_top = col_at(i)
        z_last = jnp.where(lane == 0, z_low, ahead(f, 1))
        z_next = jnp.where(lane == nz - 1, z_top, back(f, 1))
        rate = poro[i] * (1.0 / TIME_STEP)
        bal = (
            (flow_next - flow)
            + (upwind(gy_top[i], f, y_next) - upwind(gy_low[i], y_last, f))
            + (upwind(gz_top[i], f, z_next) - upwind(gz_low[i], z_last, f))
            - INJECT_RATE * well[i].astype(F32)
        )
        if not first:
            bal = bal + rate * (s - start[i])
        rest = 1.0 - s
        den = s * s + c * rest * rest
        slope = 2.0 * c * s * rest / (den * den)
        s = s - bal / (rate + outflow[i] * jnp.abs(slope))
        new[i] = s
        if not last_sweep:
            water, rest = s * s, 1.0 - s
            new_frac[i] = water / (water + c * rest * rest)
        return f_next, flow_next

    f0 = frac[0]
    lax.fori_loop(0, nx, layer, (f0, upwind(gx[0], x_low, f0)), unroll=2)


def pack_all(plan, ref, outs):
    xa, xb, ya, yb = outs[:4]
    pack_x(plan, ref, xa, xb)
    pack_y(plan, ref, ya, yb)
    pack_z(plan, ref[...].reshape(plan.nx * plan.ny, plan.nz), outs[4:])


def step_kernel(plan, *refs):
    n_msg = len(plan.z_msgs)
    (sums, press, direction, full, image, tx, ty_low, ty_top, tz_low, tz_top) = refs[:10]
    (hx, hy, hz, dxa, dxb, dya, dyb, dhz, sat, frac, coef, poro, well) = refs[10:23]
    (p_new, r_new, s_new, f_new, gx, gy_low, gy_top, gz_low, gz_top, outflow) = refs[23:33]
    packs = refs[33 : 37 + n_msg]
    ph, fh = refs[37 + n_msg :]
    nx, ny, nz = plan.nx, plan.ny, plan.nz
    all_sums = jnp.sum(sums[...], axis=0, keepdims=True)
    step = all_sums[:, 0:1] / all_sums[:, 64:65]
    x_low = hx[0, 0] + step * side(plan, "gx", dxa[...], dxb[...], False)
    x_top = hx[1, 0] + step * side(plan, "gx", dxa[...], dxb[...], True)
    ph[0] = hy[0, 0] + step * side(plan, "gy", dya[...], dyb[...], False)
    ph[1] = hy[1, 0] + step * side(plan, "gy", dya[...], dyb[...], True)
    fh[0] = hy[0, 1]
    fh[1] = hy[1, 1]
    row, lane = rows_of((ny, nz)), lanes_of((ny, nz))

    def layer(i, carry):
        p, g = carry
        p_new[i] = p
        r_new[i] = full[i] - step * image[i]
        k = jnp.minimum(i + 1, nx - 1)
        p_next = jnp.where(i == nx - 1, x_top, press[k] + step * direction[k])
        g_next = tx[i + 1] * (p - p_next)
        gx[i + 1] = g_next
        cells = pl.ds(i * ny, ny)
        zc = hz[cells, 0:2] + step * dhz[cells, 0:2]
        y_last = jnp.where(row == 0, ph[0, pl.ds(i, 1), :], ahead(p, 0))
        y_next = jnp.where(row == ny - 1, ph[1, pl.ds(i, 1), :], back(p, 0))
        z_last = jnp.where(lane == 0, zc[:, 0:1], ahead(p, 1))
        z_next = jnp.where(lane == nz - 1, zc[:, 1:2], back(p, 1))
        parts = (
            (gy_low, ty_low[i] * (y_last - p), -1.0),
            (gy_top, ty_top[i] * (p - y_next), 1.0),
            (gz_low, tz_low[i] * (z_last - p), -1.0),
            (gz_top, tz_top[i] * (p - z_next), 1.0),
        )
        total = jnp.maximum(-g, 0.0) + jnp.maximum(g_next, 0.0)
        for ref, value, sign in parts:
            ref[i] = value
            total = total + jnp.maximum(value * sign, 0.0)
        outflow[i] = total
        return p_next, g_next

    p0 = press[0] + step * direction[0]
    g0 = tx[0] * (x_low - p0)
    gx[0] = g0
    lax.fori_loop(0, nx, layer, (p0, g0), unroll=2)

    def col_at(i):
        cells = pl.ds(i * ny, ny)
        return hz[cells, 2:3], hz[cells, 3:4]

    sweep(
        plan, True, False,
        (sat, sat, frac, coef, poro, well, gx, gy_low, gy_top, gz_low, gz_top, outflow,
         hx[0, 1], hx[1, 1], fh, col_at, s_new, f_new),
    )
    pack_all(plan, f_new, packs)


def later_kernel(plan, last_sweep, *refs):
    n_msg = len(plan.z_msgs)
    fields = refs[:12]
    xa, xb, ya, yb = refs[12:16]
    got = refs[16 : 16 + n_msg]
    rest = refs[16 + n_msg :]
    if last_sweep:
        new, fh, hz = rest
        new_frac, packs = None, ()
    else:
        new, new_frac = rest[:2]
        packs = rest[2 : 6 + n_msg]
        fh, hz = rest[6 + n_msg :]
    ny = plan.ny
    hz[...] = columns(stack_rows(z_sides(plan, [ref[0:1, :] for ref in got])))
    fh[0] = side(plan, "gy", ya[...], yb[...], False)
    fh[1] = side(plan, "gy", ya[...], yb[...], True)

    def col_at(i):
        cells = pl.ds(i * ny, ny)
        return hz[cells, 0:1], hz[cells, 1:2]

    sweep(
        plan, False, last_sweep,
        fields + (side(plan, "gx", xa[...], xb[...], False), side(plan, "gx", xa[...], xb[...], True),
                  fh, col_at, new, new_frac),
    )
    if not last_sweep:
        pack_all(plan, new_frac, packs)


def per_device(
    counts, pressure, source, saturation, permeability, compress, porosity, rock_type, well_mask, oil_factor
):
    nx, ny, nz = pressure.shape
    wide = INTERSECTION
    plan = Plan(nx, ny, nz, counts)
    n_msg = len(plan.z_msgs)
    n_dev = counts["gx"] * counts["gy"] * counts["gz"]
    cells = nx * ny
    my, mz = ny + 2 * wide, nz + 2 * wide
    table_y, eigen_y = sine_basis(my)
    table_z, eigen_z = sine_basis(mz)
    factors, middle = sweep_factors(wide + nx // 2, eigen_y, eigen_z)
    const = lambda v: jnp.asarray(v, F32)
    factors, middle = const(factors), const(middle)
    rim = np.zeros((2, MSG_ROWS, mz))
    rim[0, :wide] = table_z[:wide]
    rim[0, wide] = table_z[wide]
    rim[1, :wide] = table_z[mz - wide :]
    rim[1, wide] = table_z[mz - wide - 1]

    def swap(axis, a, b):
        return (
            lax.ppermute(a, axis, plan.perm(axis, 0)),
            lax.ppermute(b, axis, plan.perm(axis, 1)),
        )

    def swap_z(msgs):
        return [lax.ppermute(v, "gz", plan.perm("gz", q)) for q, v in zip(plan.z_msgs, msgs)]

    full_shape = (nx, ny, nz)
    x_face, y_face, z_face = (ny, nz), (nx, nz), (8, cells)
    face_shapes = [x_face, x_face, y_face, y_face] + [z_face] * n_msg

    def exchange(packs):
        z = swap_z(packs[4:])
        y = swap("gy", packs[2], packs[3])
        x = swap("gx", packs[0], packs[1])
        return [*x, *y, *z]

    mob, coef, frac, xa, xb, ya, yb, total = call(
        functools.partial(mobility_kernel, plan),
        [full_shape] * 3 + [(3,) + x_face] * 2 + [(3,) + y_face] * 2 + [x_face],
        (pressure, saturation, permeability, rock_type, oil_factor),
        smem=(4,),
    )
    ya, yb = swap("gy", ya, yb)
    xa, xb = swap("gx", xa, xb)
    res, tx, ty, tz, diag = call(
        functools.partial(inner_kernel, plan),
        [full_shape] * 5,
        (pressure, mob, source, compress, well_mask),
    )
    res, *sent = call(
        functools.partial(rim_kernel, plan),
        [full_shape] + [(MSG_ROWS, cells)] * n_msg,
        (res, pressure, mob, frac, xa, xb, ya, yb),
        scratch=[(cells, nz)],
        aliases={0: 0},
    )
    got = swap_z(sent)
    spec, sa, sb = call(
        functools.partial(z_kernel, plan, n_msg),
        [(nx, ny, mz)] + [(nx, wide, mz)] * 2,
        (res, const(table_z[wide : wide + nz]), const(rim[0]), const(rim[1]), *sent, *got),
    )
    sa, sb = swap("gy", sa, sb)
    full, tx, ty_low, ty_top, tz_low, tz_top, hx, hy, hz = call(
        functools.partial(faces_kernel, plan, n_msg),
        [full_shape, (nx + 1, ny, nz)] + [full_shape] * 4
        + [(2, 2) + x_face, (2, 2) + y_face, (cells, 128)],
        (res, mob, tx, ty, tz, xa, xb, ya, yb, *sent, *got),
        scratch=[(2,) + y_face],
    )
    modes, ma, mb = call(
        functools.partial(y_kernel, plan),
        [(nx, my, mz), (my, mz), (my, mz)],
        (spec, sa, sb, const(table_y), factors),
    )
    ma, mb = swap("gx", ma, mb)
    direction, *packs = call(
        functools.partial(solve_kernel, plan),
        [full_shape] + face_shapes,
        (modes, ma, mb, factors, middle, const(table_y[wide : wide + ny]),
         const(table_z[:, wide : wide + nz]), total),
        scratch=[(cells, mz)],
    )
    dhalo = exchange(packs)
    image, sums, dhz = call(
        functools.partial(image_kernel, plan, n_dev),
        [full_shape, (n_dev, 128), (cells, 128)],
        (direction, diag, full, tx, ty_low, ty_top, tz_low, tz_top, *dhalo),
        scratch=[(2,) + y_face],
    )
    sums = lax.all_to_all(sums, AXES, 0, 0, tiled=True)
    outs = call(
        functools.partial(step_kernel, plan),
        [full_shape] * 4 + [(nx + 1, ny, nz)] + [full_shape] * 5 + face_shapes,
        (sums, pressure, direction, full, image, tx, ty_low, ty_top, tz_low, tz_top,
         hx, hy, hz, *dhalo[:4], dhz, saturation, frac, coef, porosity, well_mask),
        scratch=[(2,) + y_face] * 2,
        limit=40,
    )
    p_new, r_new, current, frac, *flows = outs[:10]
    packs = outs[10:]
    for sweep_index in range(1, NEWTON):
        halo = exchange(packs)
        last_sweep = sweep_index == NEWTON - 1
        outs = call(
            functools.partial(later_kernel, plan, last_sweep),
            [full_shape] if last_sweep else [full_shape] * 2 + face_shapes,
            (saturation, current, frac, coef, porosity, well_mask, *flows, *halo),
            scratch=[(2,) + y_face, (cells, 128)],
        )
        current = outs[0]
        if not last_sweep:
            frac, packs = outs[1], outs[2:]
    return p_new, r_new, current


def solution(mesh):
    spec = P(*AXES)
    return jax.shard_map(
        functools.partial(per_device, dict(mesh.shape)),
        mesh=mesh,
        in_specs=(spec,) * 8 + (P(),),
        out_specs=(spec,) * 3,
        check_vma=False,
    )
```

profile of v0, /device:TPU:0, one launch (start us, length us, event | category | flops | bytes accessed | tf_op | source)
XLA Modules:
  0.0 96.1 jit_solution(15426068998286079974)
XLA Ops:
  0.6 0.0 copy-start
  0.6 1.0 %copy-done = f32[32,32,128]{2,1,0:T(8,128)S(1)} copy-done((f32[32,32,128]{2,1,0:T(8,128)S(1)}, f32[32,32,128]{2,1,0:T(8,128)}, u32[]{:S(2)}) %copy-start) | copy-done | bytes 524312
  1.7 1.0 %copy-done.2 = f32[32,32,128]{2,1,0:T(8,128)S(1)} copy-done((f32[32,32,128]{2,1,0:T(8,128)S(1)}, f32[32,32,128]{2,1,0:T(8,128)}, u32[]{:S(2)}) %copy-start.2) | copy-done | bytes 524312
  2.7 1.0 %copy-done.7 = f32[32,32,128]{2,1,0:T(8,128)S(1)} copy-done((f32[32,32,128]{2,1,0:T(8,128)S(1)}, f32[32,32,128]{2,1,0:T(8,128)}, u32[]{:S(2)}) %copy-start.7) | copy-done | bytes 524312
  3.8 1.0 %copy-done.8 = s32[32,32,128]{2,1,0:T(8,128)S(1)} copy-done((s32[32,32,128]{2,1,0:T(8,128)S(1)}, s32[32,32,128]{2,1,0:T(8,128)}, u32[]{:S(2)}) %copy-start.8) | copy-done | bytes 524312
  4.8 0.7 copy-done.18
  5.5 1.2 %shard_map.184 = (f32[32,32,128]{2,1,0:T(8,128)S(1)}, f32[32,32,128]{2,1,0:T(8,128)S(1)}, f32[32,32,128]{2,1,0:T(8,128)S(1)}, f32[3,32,128]{2,1,0:T(8,128)S(1)},...) custom-call(f32[32,32,128]{2,1,0:T(8,128)S(1)} %copy-done, ...), custom_call_target="tpu_custom_call" | custom-call | tf_op jit(solution)/shard_map/pallas_call | solution.py:101
  6.7 3.1 %collective-permute-start = (f32[3,32,128]{2,1,0:T(8,128)S(1)}, f32[3,32,128]{2,1,0:T(8,128)S(1)}, u32[]{:S(2)}, u32[]{:S(2)}) collective-permute-start(f32[3,32,128]{2,1,0:T(8,128)S(1)} %get-tuple-element.67), channel_id=1, source_target_pairs={{0,8},{8,0},{16,24},{24,16},{1,9},{9,1},{17,25},{25,17},{2,10},{10... | collective-permute-start | bytes 147464 | tf_op jit(solution)/shard_map/ppermute | solution.py:600
  9.8 2.5 %collective-permute-start.1 = (f32[3,32,128]{2,1,0:T(8,128)S(1)}, f32[3,32,128]{2,1,0:T(8,128)S(1)}, u32[]{:S(2)}, u32[]{:S(2)}) collective-permute-start(f32[3,32,128]{2,1,0:T(8,128)S(1)} %get-tuple-element.68), channel_id=1, source_target_pairs={{8,16},{16,8},{24,0},{0,24},{9,17},{17,9},{25,1},{1,25},{10,18},{1... | collective-permute-start | bytes 147464 | tf_op jit(solution)/shard_map/ppermute | solution.py:601
  12.3 0.0 collective-permute-start.2
  12.3 1.6 %collective-permute-start.3 = (f32[3,32,128]{2,1,0:T(8,128)S(1)}, f32[3,32,128]{2,1,0:T(8,128)S(1)}, u32[]{:S(2)}, u32[]{:S(2)}) collective-permute-start(f32[3,32,128]{2,1,0:T(8,128)S(1)} %get-tuple-element.70), channel_id=1, source_target_pairs={{2,4},{4,2},{6,0},{0,6},{3,5},{5,3},{7,1},{1,7},{10,12},{12,10},{1... | collective-permute-start | bytes 147464 | tf_op jit(solution)/shard_map/ppermute | solution.py:601
  13.9 2.5 %shard_map.185 = (f32[32,32,128]{2,1,0:T(8,128)S(1)}, f32[32,32,128]{2,1,0:T(8,128)S(1)}, f32[32,32,128]{2,1,0:T(8,128)S(1)}, f32[32,32,128]{2,1,0:T(8,128)S(1)}, f32[32,32,128]{2,1,0:T(8,128)S(1)}) custom-call(f32[32,32,128]{2,1,0:T(8,128)S(1)} %copy-done, f32[32,32,128]{2,1,0:T(8,128)S(1)} %get-tuple-element.64.mob, f32[32,32,128]{2,1,0:T(8,128)S(1)} %copy-done.9, ...), custom_call_target="tpu_custom_call" | custom-call | tf_op jit(solution)/shard_map/pallas_call | solution.py:101
  16.4 0.0 copy-start.11
  16.4 0.0 copy-start.16
  16.4 0.0 copy-start.17
  16.4 0.0 copy-start.6
  16.5 0.0 copy-start.14
  16.5 0.0 collective-permute-done.xa
  16.5 0.0 collective-permute-done.3.yb
  16.5 2.7 %shard_map.186 = (f32[32,32,128]{2,1,0:T(8,128)S(1)}, f32[16,1024]{1,0:T(8,128)S(1)}) custom-call(f32[32,32,128]{2,1,0:T(8,128)S(1)} %get-tuple-element.65.res_in, f32[32,32,128]{2,1,0:T(8,128)S(1)} %copy-done, f32[32,32,128]{2,1,0:T(8,128)S(1)} %get-tuple-element.64.mob, ...), custom_call_target="tpu_custom_call", output_to_operand_aliasing={{0}: (0, {})} | custom-call | tf_op jit(solution)/shard_map/pallas_call | solution.py:101
  19.3 1.5 %collective-permute-start.4 = (f32[16,1024]{1,0:T(8,128)S(1)}, f32[16,1024]{1,0:T(8,128)S(1)}, u32[]{:S(2)}, u32[]{:S(2)}) collective-permute-start(f32[16,1024]{1,0:T(8,128)S(1)} %get-tuple-element.72.rest_0_), channel_id=1, source_target_pairs={{0,1},{1,0},{2,3},{3,2},{4,5},{5,4},{6,7},{7,6},{8,9},{9,8},{10,11... | collective-permute-start | bytes 196616 | tf_op jit(solution)/shard_map/ppermute | solution.py:605
  20.8 2.7 %collective-permute-done.4.rest_1_ = f32[16,1024]{1,0:T(8,128)S(1)} collective-permute-done((f32[16,1024]{1,0:T(8,128)S(1)}, f32[16,1024]{1,0:T(8,128)S(1)}, u32[]{:S(2)}, u32[]{:S(2)}) %collective-permute-start.4) | collective-permute-done | bytes 65568 | tf_op jit(solution)/shard_map/ppermute | solution.py:605
  23.6 1.9 %shard_map.187 = (f32[32,32,144]{2,1,0:T(8,128)S(1)}, f32[32,8,144]{2,1,0:T(8,128)S(1)}, f32[32,8,144]{2,1,0:T(8,128)S(1)}) custom-call(f32[32,32,128]{2,1,0:T(8,128)S(1)} %get-tuple-element.71.res, f32[128,144]{1,0:T(8,128)S(1)} %copy-done.11, f32[16,144]{1,0:T(8,128)S(1)} %copy-done.17, f32[16,144]{1,0:T(8,128)S(1)} %copy-done.16, ...), custom_call_target="tpu_custom_call" | custom-call | tf_op jit(solution)/shard_map/pallas_call | solution.py:101
  25.5 0.0 copy-start.12
  25.5 0.0 copy-start.13
  25.5 0.0 copy-start.15
  25.5 0.1 collective-permute-start.5
  25.6 1.1 %collective-permute-start.6 = (f32[32,8,144]{2,1,0:T(8,128)S(1)}, f32[32,8,144]{2,1,0:T(8,128)S(1)}, u32[]{:S(2)}, u32[]{:S(2)}) collective-permute-start(f32[32,8,144]{2,1,0:T(8,128)S(1)} %get-tuple-element.75), channel_id=1, source_target_pairs={{2,4},{4,2},{6,0},{0,6},{3,5},{5,3},{7,1},{1,7},{10,12},{12,10},{1... | collective-permute-start | bytes 442376 | tf_op jit(solution)/shard_map/ppermute | solution.py:601
  26.7 0.4 collective-permute-done.5.ya
  27.1 6.5 %collective-permute-done.6.yb = f32[32,8,144]{2,1,0:T(8,128)S(1)} collective-permute-done((f32[32,8,144]{2,1,0:T(8,128)S(1)}, f32[32,8,144]{2,1,0:T(8,128)S(1)}, u32[]{:S(2)}, u32[]{:S(2)}) %collective-permute-start.6) | collective-permute-done | bytes 147488 | tf_op jit(solution)/shard_map/ppermute | solution.py:601
  33.6 3.9 %shard_map.188 = (f32[32,48,144]{2,1,0:T(8,128)S(1)}, f32[48,144]{1,0:T(8,128)S(1)}, f32[48,144]{1,0:T(8,128)S(1)}) custom-call(f32[32,32,144]{2,1,0:T(8,128)S(1)} %get-tuple-element.73.spec, f32[32,8,144]{2,1,0:T(8,128)S(1)} %collective-permute-done.5.ya, f32[32,8,144]{2,1,0:T(8,128)S(1)} %collective-permute-done.6.yb, f32[48,48]{1,0:T(8,128)S(1)} %copy-done.14, ...), custom_call_target="tpu_custom_call" | custom-call | tf_op jit(solution)/shard_map/pallas_call | solution.py:101
  37.5 0.7 collective-permute-start.7
  38.3 1.0 %collective-permute-start.8 = (f32[48,144]{1,0:T(8,128)S(1)}, f32[48,144]{1,0:T(8,128)S(1)}, u32[]{:S(2)}, u32[]{:S(2)}) collective-permute-start(f32[48,144]{1,0:T(8,128)S(1)} %get-tuple-element.78), channel_id=1, source_target_pairs={{8,16},{16,8},{24,0},{0,24},{9,17},{17,9},{25,1},{1,25},{10,18},{1... | collective-permute-start | bytes 82952 | tf_op jit(solution)/shard_map/ppermute | solution.py:601
  39.3 2.4 %collective-permute-done.7.xa = f32[48,144]{1,0:T(8,128)S(1)} collective-permute-done((f32[48,144]{1,0:T(8,128)S(1)}, f32[48,144]{1,0:T(8,128)S(1)}, u32[]{:S(2)}, u32[]{:S(2)}) %collective-permute-start.7) | collective-permute-done | bytes 27680 | tf_op jit(solution)/shard_map/ppermute | solution.py:600
  41.7 2.5 %collective-permute-done.8.xb = f32[48,144]{1,0:T(8,128)S(1)} collective-permute-done((f32[48,144]{1,0:T(8,128)S(1)}, f32[48,144]{1,0:T(8,128)S(1)}, u32[]{:S(2)}, u32[]{:S(2)}) %collective-permute-start.8) | collective-permute-done | bytes 27680 | tf_op jit(solution)/shard_map/ppermute | solution.py:601
  44.2 4.5 %shard_map.189 = (f32[32,32,128]{2,1,0:T(8,128)S(1)}, f32[32,128]{1,0:T(8,128)S(1)}, f32[32,128]{1,0:T(8,128)S(1)}, f32[32,128]{1,0:T(8,128)S(1)}, f32[32,128]{1,0:T(8,128)S(1)}, /*index=5*/f32[8,1024]{1,0:T(8,128)S(1)}) custom-call(f32[32,48,144]{2,1,0:T(8,128)S(1)} %get-tuple-element.76.modes, f32[48,144]{1,0:T(8,128)S(1)} %collective-permute-done.7.xa, ...), custom_call_target="tpu_custom_call" | custom-call | tf_op jit(solution)/shard_map/pallas_call | solution.py:101
  48.7 1.6 %collective-permute-start.13 = (f32[8,1024]{1,0:T(8,128)S(1)}, f32[8,1024]{1,0:T(8,128)S(1)}, u32[]{:S(2)}, u32[]{:S(2)}) collective-permute-start(f32[8,1024]{1,0:T(8,128)S(1)} %get-tuple-element.95), channel_id=1, source_target_pairs={{0,1},{1,0},{2,3},{3,2},{4,5},{5,4},{6,7},{7,6},{8,9},{9,8},{10,11... | collective-permute-start | bytes 98312 | tf_op jit(solution)/shard_map/ppermute | solution.py:605
  50.3 0.6 collective-permute-start.9
  50.9 1.5 %collective-permute-start.10 = (f32[32,128]{1,0:T(8,128)S(1)}, f32[32,128]{1,0:T(8,128)S(1)}, u32[]{:S(2)}, u32[]{:S(2)}) collective-permute-start(f32[32,128]{1,0:T(8,128)S(1)} %get-tuple-element.92), channel_id=1, source_target_pairs={{8,16},{16,8},{24,0},{0,24},{9,17},{17,9},{25,1},{1,25},{10,18},{1... | collective-permute-start | bytes 49160 | tf_op jit(solution)/shard_map/ppermute | solution.py:601
  52.4 1.6 %collective-permute-start.12 = (f32[32,128]{1,0:T(8,128)S(1)}, f32[32,128]{1,0:T(8,128)S(1)}, u32[]{:S(2)}, u32[]{:S(2)}) collective-permute-start(f32[32,128]{1,0:T(8,128)S(1)} %get-tuple-element.94), channel_id=1, source_target_pairs={{2,4},{4,2},{6,0},{0,6},{3,5},{5,3},{7,1},{1,7},{10,12},{12,10},{1... | collective-permute-start | bytes 49160 | tf_op jit(solution)/shard_map/ppermute | solution.py:601
  54.0 3.8 %shard_map.190 = (f32[32,32,128]{2,1,0:T(8,128)S(1)}, f32[33,32,128]{2,1,0:T(8,128)S(1)}, f32[32,32,128]{2,1,0:T(8,128)S(1)}, f32[32,32,128]{2,1,0:T(8,128)S(1)}...) custom-call(f32[32,32,128]{2,1,0:T(8,128)S(1)} %get-tuple-element.71, ...), custom_call_target="tpu_custom_call" | custom-call | tf_op jit(solution)/shard_map/pallas_call | solution.py:101
  57.8 0.0 collective-permute-done.10.xb.refs_14_
  57.8 0.0 collective-permute-done.11.ya.refs_15_
  57.8 0.0 collective-permute-done.13.rest_0_
  57.8 0.0 copy-start.1
  57.8 0.0 copy-start.3
  57.8 0.0 copy-start.5
  57.8 2.6 %shard_map.191 = (f32[32,32,128]{2,1,0:T(8,128)S(1)}, f32[32,128]{1,0:T(8,128)S(1)}, f32[1024,128]{1,0:T(8,128)S(1)}) custom-call(f32[32,32,128]{2,1,0:T(8,128)S(1)} %get-tuple-element.80.direction.refs_2_, f32[32,32,128]{2,1,0:T(8,128)S(1)} %get-tuple-element.81.diag, f32[32,32,128]{2,1,0:T(8,128)S(1)} %get-tuple-element.85.full.refs_3_, ...), custom_call_target="tpu_custom_call" | custom-call | tf_op jit(solution)/shard_map/pallas_call | solution.py:101
  60.5 9.7 %all_to_all.11 = f32[32,1,128]{2,1,0:T(1,128)S(1)} all-to-all(f32[32,1,128]{2,1,0:T(1,128)S(1)} %bitcast.5), channel_id=1, replica_groups=mesh['gx'=4,'gy'=4,'gz'=2] {'gx','gy','gz'}, dimensions={0} | all-to-all | bytes 32768 | tf_op jit(solution)/shard_map/all_to_all | solution.py:671
  70.1 5.0 %shard_map.192 = (f32[32,32,128]{2,1,0:T(8,128)}, f32[32,32,128]{2,1,0:T(8,128)}, f32[32,32,128]{2,1,0:T(8,128)S(1)}, f32[32,32,128]{2,1,0:T(8,128)S(1)}, f32[33...) custom-call(f32[32,128]{1,0:T(8,128)S(1)} %bitcast.4, ...), custom_call_target="tpu_custom_call" | custom-call | tf_op jit(solution)/shard_map/pallas_call | solution.py:101
  75.1 0.5 collective-permute-start.18
  75.6 0.6 collective-permute-start.14
  76.2 1.5 %collective-permute-start.15 = (f32[32,128]{1,0:T(8,128)S(1)}, f32[32,128]{1,0:T(8,128)S(1)}, u32[]{:S(2)}, u32[]{:S(2)}) collective-permute-start(f32[32,128]{1,0:T(8,128)S(1)} %get-tuple-element.114), channel_id=1, source_target_pairs={{8,16},{16,8},{24,0},{0,24},{9,17},{17,9},{25,1},{1,25},{10,18},{1... | collective-permute-start | bytes 49160 | tf_op jit(solution)/shard_map/ppermute | solution.py:601
  77.7 0.7 collective-permute-start.17
  78.3 1.0 %collective-permute-done.14.refs_12_ = f32[32,128]{1,0:T(8,128)S(1)} collective-permute-done((f32[32,128]{1,0:T(8,128)S(1)}, f32[32,128]{1,0:T(8,128)S(1)}, u32[]{:S(2)}, u32[]{:S(2)}) %collective-permute-start.14) | collective-permute-done | bytes 16416 | tf_op jit(solution)/shard_map/ppermute | solution.py:600
  79.4 2.4 %collective-permute-done.15.refs_13_ = f32[32,128]{1,0:T(8,128)S(1)} collective-permute-done((f32[32,128]{1,0:T(8,128)S(1)}, f32[32,128]{1,0:T(8,128)S(1)}, u32[]{:S(2)}, u32[]{:S(2)}) %collective-permute-start.15) | collective-permute-done | bytes 16416 | tf_op jit(solution)/shard_map/ppermute | solution.py:601
  81.7 0.0 collective-permute-done.17.refs_15_
  81.8 4.0 %shard_map.193 = (f32[32,32,128]{2,1,0:T(8,128)S(1)}, f32[32,32,128]{2,1,0:T(8,128)S(1)}, f32[32,128]{1,0:T(8,128)S(1)}, f32[32,128]{1,0:T(8,128)S(1)}, f32[32,1...) custom-call(f32[32,32,128]{2,1,0:T(8,128)S(1)} %copy-done.3, ...), custom_call_target="tpu_custom_call" | custom-call | tf_op jit(solution)/shard_map/pallas_call | solution.py:101
  85.8 1.4 %collective-permute-start.23 = (f32[8,1024]{1,0:T(8,128)S(1)}, f32[8,1024]{1,0:T(8,128)S(1)}, u32[]{:S(2)}, u32[]{:S(2)}) collective-permute-start(f32[8,1024]{1,0:T(8,128)S(1)} %get-tuple-element.124), channel_id=1, source_target_pairs={{0,1},{1,0},{2,3},{3,2},{4,5},{5,4},{6,7},{7,6},{8,9},{9,8},{10,11... | collective-permute-start | bytes 98312 | tf_op jit(solution)/shard_map/ppermute | solution.py:605
  87.2 2.1 %collective-permute-start.20 = (f32[32,128]{1,0:T(8,128)S(1)}, f32[32,128]{1,0:T(8,128)S(1)}, u32[]{:S(2)}, u32[]{:S(2)}) collective-permute-start(f32[32,128]{1,0:T(8,128)S(1)} %get-tuple-element.121), channel_id=1, source_target_pairs={{8,16},{16,8},{24,0},{0,24},{9,17},{17,9},{25,1},{1,25},{10,18},{1... | collective-permute-start | bytes 49160 | tf_op jit(solution)/shard_map/ppermute | solution.py:601
  89.3 0.6 collective-permute-start.22
  90.0 1.0 %collective-permute-done.19.refs_12_ = f32[32,128]{1,0:T(8,128)S(1)} collective-permute-done((f32[32,128]{1,0:T(8,128)S(1)}, f32[32,128]{1,0:T(8,128)S(1)}, u32[]{:S(2)}, u32[]{:S(2)}) %collective-permute-start.19) | collective-permute-done | bytes 16416 | tf_op jit(solution)/shard_map/ppermute | solution.py:600
  91.0 1.8 %collective-permute-done.20.refs_13_ = f32[32,128]{1,0:T(8,128)S(1)} collective-permute-done((f32[32,128]{1,0:T(8,128)S(1)}, f32[32,128]{1,0:T(8,128)S(1)}, u32[]{:S(2)}, u32[]{:S(2)}) %collective-permute-start.20) | collective-permute-done | bytes 16416 | tf_op jit(solution)/shard_map/ppermute | solution.py:601
  92.8 3.3 %shard_map.194 = f32[32,32,128]{2,1,0:T(8,128)} custom-call(f32[32,32,128]{2,1,0:T(8,128)S(1)} %copy-done.3, f32[32,32,128]{2,1,0:T(8,128)S(1)} %get-tuple-element.118.refs_1_, f32[32,32,128]{2,1,0:T(8,128)S(1)} %get-tuple-element.119.refs_2_, f32[32,32,128]{2,1,0:T(8,128)S(1)} %get-tuple-element.102.refs_20_.refs_3_, f32[32,32,128]{2,1,0:T(8,128)S(1)} %copy-done.5, ...), custom_call_target="tpu_custom_call" | custom-call | tf_op jit(solution)/shard_map/pallas_call | solution.py:101
  (34 shorter events, 0.1 us)
Async XLA Ops:
  0.6 1.0 %copy-start = (f32[32,32,128]{2,1,0:T(8,128)S(1)}, f32[32,32,128]{2,1,0:T(8,128)}, u32[]{:S(2)}) copy-start(f32[32,32,128]{2,1,0:T(8,128)} %refs_1_.1) | copy-start | bytes 1572868
  1.7 1.0 %copy-start.2 = (f32[32,32,128]{2,1,0:T(8,128)S(1)}, f32[32,32,128]{2,1,0:T(8,128)}, u32[]{:S(2)}) copy-start(f32[32,32,128]{2,1,0:T(8,128)} %refs_0_.3) | copy-start | bytes 1572868
  2.7 1.0 %copy-start.7 = (f32[32,32,128]{2,1,0:T(8,128)S(1)}, f32[32,32,128]{2,1,0:T(8,128)}, u32[]{:S(2)}) copy-start(f32[32,32,128]{2,1,0:T(8,128)} %perm.1) | copy-start | bytes 1572868
  3.8 1.0 %copy-start.8 = (s32[32,32,128]{2,1,0:T(8,128)S(1)}, s32[32,32,128]{2,1,0:T(8,128)}, u32[]{:S(2)}) copy-start(s32[32,32,128]{2,1,0:T(8,128)} %rock.1) | copy-start | bytes 1572868
  4.8 0.7 copy-start.18
  5.5 8.4 %copy-start.4 = (s32[32,32,128]{2,1,0:T(8,128)S(1)}, s32[32,32,128]{2,1,0:T(8,128)}, u32[]{:S(2)}) copy-start(s32[32,32,128]{2,1,0:T(8,128)} %refs_5_.3) | copy-start | bytes 1572868
  5.5 8.4 %copy-start.9 = (f32[32,32,128]{2,1,0:T(8,128)S(1)}, f32[32,32,128]{2,1,0:T(8,128)}, u32[]{:S(2)}) copy-start(f32[32,32,128]{2,1,0:T(8,128)} %source.1) | copy-start | bytes 1572868
  5.5 8.4 %copy-start.10 = (f32[32,32,128]{2,1,0:T(8,128)S(1)}, f32[32,32,128]{2,1,0:T(8,128)}, u32[]{:S(2)}) copy-start(f32[32,32,128]{2,1,0:T(8,128)} %compress.1) | copy-start | bytes 1572868
  6.7 9.8 %collective-permute-start = (f32[3,32,128]{2,1,0:T(8,128)S(1)}, f32[3,32,128]{2,1,0:T(8,128)S(1)}, u32[]{:S(2)}, u32[]{:S(2)}) collective-permute-start(f32[3,32,128]{2,1,0:T(8,128)S(1)} %get-tuple-element.67), channel_id=1, source_target_pairs={{0,8},{8,0},{16,24},{24,16},{1,9},{9,1},{17,25},{25,17},{2,10},{10... | collective-permute-start | bytes 147464 | tf_op jit(solution)/shard_map/ppermute | solution.py:600
  9.8 6.7 %collective-permute-start.1 = (f32[3,32,128]{2,1,0:T(8,128)S(1)}, f32[3,32,128]{2,1,0:T(8,128)S(1)}, u32[]{:S(2)}, u32[]{:S(2)}) collective-permute-start(f32[3,32,128]{2,1,0:T(8,128)S(1)} %get-tuple-element.68), channel_id=1, source_target_pairs={{8,16},{16,8},{24,0},{0,24},{9,17},{17,9},{25,1},{1,25},{10,18},{1... | collective-permute-start | bytes 147464 | tf_op jit(solution)/shard_map/ppermute | solution.py:601
  12.3 4.2 %collective-permute-start.2 = (f32[3,32,128]{2,1,0:T(8,128)S(1)}, f32[3,32,128]{2,1,0:T(8,128)S(1)}, u32[]{:S(2)}, u32[]{:S(2)}) collective-permute-start(f32[3,32,128]{2,1,0:T(8,128)S(1)} %get-tuple-element.69), channel_id=1, source_target_pairs={{0,2},{2,0},{4,6},{6,4},{1,3},{3,1},{5,7},{7,5},{8,10},{10,8},{12,... | collective-permute-start | bytes 147464 | tf_op jit(solution)/shard_map/ppermute | solution.py:600
  12.3 4.2 %collective-permute-start.3 = (f32[3,32,128]{2,1,0:T(8,128)S(1)}, f32[3,32,128]{2,1,0:T(8,128)S(1)}, u32[]{:S(2)}, u32[]{:S(2)}) collective-permute-start(f32[3,32,128]{2,1,0:T(8,128)S(1)} %get-tuple-element.70), channel_id=1, source_target_pairs={{2,4},{4,2},{6,0},{0,6},{3,5},{5,3},{7,1},{1,7},{10,12},{12,10},{1... | collective-permute-start | bytes 147464 | tf_op jit(solution)/shard_map/ppermute | solution.py:601
  16.4 7.1 %copy-start.11 = (f32[128,144]{1,0:T(8,128)S(1)}, f32[128,144]{1,0:T(8,128)}, u32[]{:S(2)}) copy-start(f32[128,144]{1,0:T(8,128)} %constant.18.clone.basis) | copy-start | bytes 221188
  16.4 7.1 %copy-start.16 = (f32[16,144]{1,0:T(8,128)S(1)}, f32[16,144]{1,0:T(8,128)}, u32[]{:S(2)}) copy-start(f32[16,144]{1,0:T(8,128)} %constant.20.clone.rim_top) | copy-start | bytes 27652
  16.4 7.1 %copy-start.17 = (f32[16,144]{1,0:T(8,128)S(1)}, f32[16,144]{1,0:T(8,128)}, u32[]{:S(2)}) copy-start(f32[16,144]{1,0:T(8,128)} %constant.19.clone.rim_low) | copy-start | bytes 27652
  16.4 17.2 %copy-start.6 = (f32[24,48,144]{2,1,0:T(8,128)S(1)}, f32[24,48,144]{2,1,0:T(8,128)}, u32[]{:S(2)}) copy-start(f32[24,48,144]{2,1,0:T(8,128)} %constant.16.clone.factors) | copy-start | bytes 1990660
  16.5 17.2 %copy-start.14 = (f32[48,48]{1,0:T(8,128)S(1)}, f32[48,48]{1,0:T(8,128)}, u32[]{:S(2)}) copy-start(f32[48,48]{1,0:T(8,128)} %constant.21.clone.basis) | copy-start | bytes 27652
  19.3 4.3 %collective-permute-start.4 = (f32[16,1024]{1,0:T(8,128)S(1)}, f32[16,1024]{1,0:T(8,128)S(1)}, u32[]{:S(2)}, u32[]{:S(2)}) collective-permute-start(f32[16,1024]{1,0:T(8,128)S(1)} %get-tuple-element.72.rest_0_), channel_id=1, source_target_pairs={{0,1},{1,0},{2,3},{3,2},{4,5},{5,4},{6,7},{7,6},{8,9},{9,8},{10,11... | collective-permute-start | bytes 196616 | tf_op jit(solution)/shard_map/ppermute | solution.py:605
  25.5 18.7 %copy-start.12 = (f32[144,128]{1,0:T(8,128)S(1)}, f32[144,128]{1,0:T(8,128)}, u32[]{:S(2)}) copy-start(f32[144,128]{1,0:T(8,128)} %constant.23.clone.basis_z) | copy-start | bytes 221188
  25.5 18.7 %copy-start.13 = (f32[48,144]{1,0:T(8,128)S(1)}, f32[48,144]{1,0:T(8,128)}, u32[]{:S(2)}) copy-start(f32[48,144]{1,0:T(8,128)} %constant.17.clone.middle) | copy-start | bytes 82948
  25.5 18.7 %copy-start.15 = (f32[32,48]{1,0:T(8,128)S(1)}, f32[32,48]{1,0:T(8,128)}, u32[]{:S(2)}) copy-start(f32[32,48]{1,0:T(8,128)} %constant.22.clone.basis_y) | copy-start | bytes 18436
  25.5 1.6 %collective-permute-start.5 = (f32[32,8,144]{2,1,0:T(8,128)S(1)}, f32[32,8,144]{2,1,0:T(8,128)S(1)}, u32[]{:S(2)}, u32[]{:S(2)}) collective-permute-start(f32[32,8,144]{2,1,0:T(8,128)S(1)} %get-tuple-element.74), channel_id=1, source_target_pairs={{0,2},{2,0},{4,6},{6,4},{1,3},{3,1},{5,7},{7,5},{8,10},{10,8},{12,... | collective-permute-start | bytes 442376 | tf_op jit(solution)/shard_map/ppermute | solution.py:600
  25.6 8.1 %collective-permute-start.6 = (f32[32,8,144]{2,1,0:T(8,128)S(1)}, f32[32,8,144]{2,1,0:T(8,128)S(1)}, u32[]{:S(2)}, u32[]{:S(2)}) collective-permute-start(f32[32,8,144]{2,1,0:T(8,128)S(1)} %get-tuple-element.75), channel_id=1, source_target_pairs={{2,4},{4,2},{6,0},{0,6},{3,5},{5,3},{7,1},{1,7},{10,12},{12,10},{1... | collective-permute-start | bytes 442376 | tf_op jit(solution)/shard_map/ppermute | solution.py:601
  37.5 4.2 %collective-permute-start.7 = (f32[48,144]{1,0:T(8,128)S(1)}, f32[48,144]{1,0:T(8,128)S(1)}, u32[]{:S(2)}, u32[]{:S(2)}) collective-permute-start(f32[48,144]{1,0:T(8,128)S(1)} %get-tuple-element.77), channel_id=1, source_target_pairs={{0,8},{8,0},{16,24},{24,16},{1,9},{9,1},{17,25},{25,17},{2,10},{10... | collective-permute-start | bytes 82952 | tf_op jit(solution)/shard_map/ppermute | solution.py:600
  38.3 5.9 %collective-permute-start.8 = (f32[48,144]{1,0:T(8,128)S(1)}, f32[48,144]{1,0:T(8,128)S(1)}, u32[]{:S(2)}, u32[]{:S(2)}) collective-permute-start(f32[48,144]{1,0:T(8,128)S(1)} %get-tuple-element.78), channel_id=1, source_target_pairs={{8,16},{16,8},{24,0},{0,24},{9,17},{17,9},{25,1},{1,25},{10,18},{1... | collective-permute-start | bytes 82952 | tf_op jit(solution)/shard_map/ppermute | solution.py:601
  48.7 9.1 %collective-permute-start.13 = (f32[8,1024]{1,0:T(8,128)S(1)}, f32[8,1024]{1,0:T(8,128)S(1)}, u32[]{:S(2)}, u32[]{:S(2)}) collective-permute-start(f32[8,1024]{1,0:T(8,128)S(1)} %get-tuple-element.95), channel_id=1, source_target_pairs={{0,1},{1,0},{2,3},{3,2},{4,5},{5,4},{6,7},{7,6},{8,9},{9,8},{10,11... | collective-permute-start | bytes 98312 | tf_op jit(solution)/shard_map/ppermute | solution.py:605
  50.3 7.5 %collective-permute-start.9 = (f32[32,128]{1,0:T(8,128)S(1)}, f32[32,128]{1,0:T(8,128)S(1)}, u32[]{:S(2)}, u32[]{:S(2)}) collective-permute-start(f32[32,128]{1,0:T(8,128)S(1)} %get-tuple-element.91), channel_id=1, source_target_pairs={{0,8},{8,0},{16,24},{24,16},{1,9},{9,1},{17,25},{25,17},{2,10},{10... | collective-permute-start | bytes 49160 | tf_op jit(solution)/shard_map/ppermute | solution.py:600
  50.9 6.9 %collective-permute-start.10 = (f32[32,128]{1,0:T(8,128)S(1)}, f32[32,128]{1,0:T(8,128)S(1)}, u32[]{:S(2)}, u32[]{:S(2)}) collective-permute-start(f32[32,128]{1,0:T(8,128)S(1)} %get-tuple-element.92), channel_id=1, source_target_pairs={{8,16},{16,8},{24,0},{0,24},{9,17},{17,9},{25,1},{1,25},{10,18},{1... | collective-permute-start | bytes 49160 | tf_op jit(solution)/shard_map/ppermute | solution.py:601
  52.4 5.4 %collective-permute-start.11 = (f32[32,128]{1,0:T(8,128)S(1)}, f32[32,128]{1,0:T(8,128)S(1)}, u32[]{:S(2)}, u32[]{:S(2)}) collective-permute-start(f32[32,128]{1,0:T(8,128)S(1)} %get-tuple-element.93), channel_id=1, source_target_pairs={{0,2},{2,0},{4,6},{6,4},{1,3},{3,1},{5,7},{7,5},{8,10},{10,8},{12,... | collective-permute-start | bytes 49160 | tf_op jit(solution)/shard_map/ppermute | solution.py:600
  52.4 5.4 %collective-permute-start.12 = (f32[32,128]{1,0:T(8,128)S(1)}, f32[32,128]{1,0:T(8,128)S(1)}, u32[]{:S(2)}, u32[]{:S(2)}) collective-permute-start(f32[32,128]{1,0:T(8,128)S(1)} %get-tuple-element.94), channel_id=1, source_target_pairs={{2,4},{4,2},{6,0},{0,6},{3,5},{5,3},{7,1},{1,7},{10,12},{12,10},{1... | collective-permute-start | bytes 49160 | tf_op jit(solution)/shard_map/ppermute | solution.py:601
  57.8 12.3 %copy-start.1 = (f32[32,32,128]{2,1,0:T(8,128)S(1)}, f32[32,32,128]{2,1,0:T(8,128)}, u32[]{:S(2)}) copy-start(f32[32,32,128]{2,1,0:T(8,128)} %refs_1_.1) | copy-start | bytes 1572868
  57.8 12.3 %copy-start.3 = (f32[32,32,128]{2,1,0:T(8,128)S(1)}, f32[32,32,128]{2,1,0:T(8,128)}, u32[]{:S(2)}) copy-start(f32[32,32,128]{2,1,0:T(8,128)} %refs_0_.3) | copy-start | bytes 1572868
  57.8 12.3 %copy-start.5 = (f32[32,32,128]{2,1,0:T(8,128)S(1)}, f32[32,32,128]{2,1,0:T(8,128)}, u32[]{:S(2)}) copy-start(f32[32,32,128]{2,1,0:T(8,128)} %refs_4_.3) | copy-start | bytes 1572868
  75.1 6.6 %collective-permute-start.18 = (f32[8,1024]{1,0:T(8,128)S(1)}, f32[8,1024]{1,0:T(8,128)S(1)}, u32[]{:S(2)}, u32[]{:S(2)}) collective-permute-start(f32[8,1024]{1,0:T(8,128)S(1)} %get-tuple-element.117), channel_id=1, source_target_pairs={{0,1},{1,0},{2,3},{3,2},{4,5},{5,4},{6,7},{7,6},{8,9},{9,8},{10,11... | collective-permute-start | bytes 98312 | tf_op jit(solution)/shard_map/ppermute | solution.py:605
  75.6 3.7 %collective-permute-start.14 = (f32[32,128]{1,0:T(8,128)S(1)}, f32[32,128]{1,0:T(8,128)S(1)}, u32[]{:S(2)}, u32[]{:S(2)}) collective-permute-start(f32[32,128]{1,0:T(8,128)S(1)} %get-tuple-element.113), channel_id=1, source_target_pairs={{0,8},{8,0},{16,24},{24,16},{1,9},{9,1},{17,25},{25,17},{2,10},{10... | collective-permute-start | bytes 49160 | tf_op jit(solution)/shard_map/ppermute | solution.py:600
  76.2 5.5 %collective-permute-start.15 = (f32[32,128]{1,0:T(8,128)S(1)}, f32[32,128]{1,0:T(8,128)S(1)}, u32[]{:S(2)}, u32[]{:S(2)}) collective-permute-start(f32[32,128]{1,0:T(8,128)S(1)} %get-tuple-element.114), channel_id=1, source_target_pairs={{8,16},{16,8},{24,0},{0,24},{9,17},{17,9},{25,1},{1,25},{10,18},{1... | collective-permute-start | bytes 49160 | tf_op jit(solution)/shard_map/ppermute | solution.py:601
  77.7 4.1 %collective-permute-start.16 = (f32[32,128]{1,0:T(8,128)S(1)}, f32[32,128]{1,0:T(8,128)S(1)}, u32[]{:S(2)}, u32[]{:S(2)}) collective-permute-start(f32[32,128]{1,0:T(8,128)S(1)} %get-tuple-element.115), channel_id=1, source_target_pairs={{0,2},{2,0},{4,6},{6,4},{1,3},{3,1},{5,7},{7,5},{8,10},{10,8},{12,... | collective-permute-start | bytes 49160 | tf_op jit(solution)/shard_map/ppermute | solution.py:600
  77.7 4.1 %collective-permute-start.17 = (f32[32,128]{1,0:T(8,128)S(1)}, f32[32,128]{1,0:T(8,128)S(1)}, u32[]{:S(2)}, u32[]{:S(2)}) collective-permute-start(f32[32,128]{1,0:T(8,128)S(1)} %get-tuple-element.116), channel_id=1, source_target_pairs={{2,4},{4,2},{6,0},{0,6},{3,5},{5,3},{7,1},{1,7},{10,12},{12,10},{1... | collective-permute-start | bytes 49160 | tf_op jit(solution)/shard_map/ppermute | solution.py:601
  85.8 7.0 %collective-permute-start.23 = (f32[8,1024]{1,0:T(8,128)S(1)}, f32[8,1024]{1,0:T(8,128)S(1)}, u32[]{:S(2)}, u32[]{:S(2)}) collective-permute-start(f32[8,1024]{1,0:T(8,128)S(1)} %get-tuple-element.124), channel_id=1, source_target_pairs={{0,1},{1,0},{2,3},{3,2},{4,5},{5,4},{6,7},{7,6},{8,9},{9,8},{10,11... | collective-permute-start | bytes 98312 | tf_op jit(solution)/shard_map/ppermute | solution.py:605
  87.2 3.7 %collective-permute-start.19 = (f32[32,128]{1,0:T(8,128)S(1)}, f32[32,128]{1,0:T(8,128)S(1)}, u32[]{:S(2)}, u32[]{:S(2)}) collective-permute-start(f32[32,128]{1,0:T(8,128)S(1)} %get-tuple-element.120), channel_id=1, source_target_pairs={{0,8},{8,0},{16,24},{24,16},{1,9},{9,1},{17,25},{25,17},{2,10},{10... | collective-permute-start | bytes 49160 | tf_op jit(solution)/shard_map/ppermute | solution.py:600
  87.2 5.5 %collective-permute-start.20 = (f32[32,128]{1,0:T(8,128)S(1)}, f32[32,128]{1,0:T(8,128)S(1)}, u32[]{:S(2)}, u32[]{:S(2)}) collective-permute-start(f32[32,128]{1,0:T(8,128)S(1)} %get-tuple-element.121), channel_id=1, source_target_pairs={{8,16},{16,8},{24,0},{0,24},{9,17},{17,9},{25,1},{1,25},{10,18},{1... | collective-permute-start | bytes 49160 | tf_op jit(solution)/shard_map/ppermute | solution.py:601
  89.3 3.4 %collective-permute-start.21 = (f32[32,128]{1,0:T(8,128)S(1)}, f32[32,128]{1,0:T(8,128)S(1)}, u32[]{:S(2)}, u32[]{:S(2)}) collective-permute-start(f32[32,128]{1,0:T(8,128)S(1)} %get-tuple-element.122), channel_id=1, source_target_pairs={{0,2},{2,0},{4,6},{6,4},{1,3},{3,1},{5,7},{7,5},{8,10},{10,8},{12,... | collective-permute-start | bytes 49160 | tf_op jit(solution)/shard_map/ppermute | solution.py:600
  89.3 3.4 %collective-permute-start.22 = (f32[32,128]{1,0:T(8,128)S(1)}, f32[32,128]{1,0:T(8,128)S(1)}, u32[]{:S(2)}, u32[]{:S(2)}) collective-permute-start(f32[32,128]{1,0:T(8,128)S(1)} %get-tuple-element.123), channel_id=1, source_target_pairs={{2,4},{4,2},{6,0},{0,6},{3,5},{5,3},{7,1},{1,7},{10,12},{12,10},{1... | collective-permute-start | bytes 49160 | tf_op jit(solution)/shard_map/ppermute | solution.py:601
where the time goes:
time: 96.4 us; the launch traced here: 96.1 us
  Pallas kernels  35.5 us (37%)
  starting transfers between devices  24.3 us (25%)
  waiting for transfers between devices  20.8 us (22%)
  blocking collectives  9.67 us (10%)
  local copies, waits for them, and re-layouts  4.9 us (5%)
    pallas_call x11, Pallas kernels, call(): pl.pallas_call(kernel, out_shape=[jax.ShapeDtypeStruct(s, F32) for s in o...  35.5 us
    ppermute x10, starting transfers between devices, swap(): lax.ppermute(b, axis, plan.perm(axis, 1))  14.2 us
    ppermute x10, waiting for transfers between devices, swap(): lax.ppermute(b, axis, plan.perm(axis, 1))  13.2 us
    all_to_all x1, blocking collectives, per_device(): sums = lax.all_to_all(sums, AXES, 0, 0, tiled=True)  9.67 us
    ppermute x10, starting transfers between devices, swap(): lax.ppermute(a, axis, plan.perm(axis, 0))  5.12 us
    ppermute x4, starting transfers between devices, swap_z(): lax.ppermute(v, 'gz', plan.perm('gz', q))  5.01 us
    unnamed x38, local copies, waits for them, and re-layouts  4.9 us
    ppermute x10, waiting for transfers between devices, swap(): lax.ppermute(a, axis, plan.perm(axis, 0))  4.84 us
  transfers between devices with their start and end apart: 24, of which 9 were waited for; matrix products, arithmetic and copies ran while one was open for 0% of the time, Pallas kernels for 7%

commit v1 on v0

v1 whole, which is shorter than its diff:
```python
import functools
import math

import jax
import jax.numpy as jnp
import numpy as np
from jax import lax
from jax.experimental import pallas as pl
from jax.experimental.pallas import tpu as pltpu
from jax.sharding import PartitionSpec as P

INTERSECTION = 8
NEWTON = 3

WELL_INDEX = 4.0
INJECT_RATE = 2.0
TIME_STEP = 0.05

AXES = ("gx", "gy", "gz")
F32 = jnp.float32
HIGH = lax.Precision.HIGHEST
MSG_ROWS = 16
CHUNKS = 4


def sine_basis(length):
    points = np.arange(length) + 1
    angles = np.outer(points, points) % (2 * (length + 1)) * (math.pi / (length + 1))
    table = math.sqrt(2.0 / (length + 1)) * np.sin(angles)
    eigen = 2.0 - 2.0 * np.cos(points * (math.pi / (length + 1)))
    return table, eigen


def sweep_factors(count, eigen_y, eigen_z):
    shift = 2.0 + eigen_y[:, None] + eigen_z[None, :]
    factors = []
    last = np.zeros_like(shift)
    for _ in range(count):
        last = 1.0 / (shift - last)
        factors.append(last)
    return np.stack(factors), 1.0 / (1.0 - last * last)


def pairs(count, periodic, parity):
    if periodic and count % 2:
        step = 1 if parity == 0 else -1
        return [(i, (i + step) % count) for i in range(count)]
    out = []
    for i in range(parity, count, 2):
        j = i + 1
        if periodic:
            j = j % count
        if j < count:
            out += [(i, j), (j, i)]
    return out


def harmonic(one, two):
    return 2.0 * one * two / (one + two)


def dot(one, two, dims=((1,), (0,))):
    return lax.dot_general(
        one, two, (dims, ((), ())), precision=HIGH, preferred_element_type=F32
    )


def rows_of(shape):
    return lax.broadcasted_iota(jnp.int32, shape, 0)


def lanes_of(shape):
    return lax.broadcasted_iota(jnp.int32, shape, 1)


def back(value, axis):
    return pltpu.roll(value, value.shape[axis] - 1, axis)


def ahead(value, axis):
    return pltpu.roll(value, 1, axis)


class Plan:
    def __init__(self, nx, ny, nz, counts):
        self.nx, self.ny, self.nz = nx, ny, nz
        self.counts = counts
        self.z_msgs = [q for q in (0, 1) if pairs(counts["gz"], False, q)]

    def perm(self, axis, which):
        return pairs(self.counts[axis], axis != "gz", which)

    def high(self, axis, which):
        if axis != "gz" and self.counts[axis] % 2:
            return (which == 0, which == 1)
        up = (lax.axis_index(axis) % 2) == which
        return (up, up)


def call(kernel, outs, args, scratch=(), aliases=None, hbm=(), hbm_out=(), limit=28):
    def spec(k, remote):
        return pl.BlockSpec(memory_space=pltpu.HBM if k in remote else pltpu.VMEM)

    args = [
        pltpu.with_memory_space_constraint(v, pltpu.HBM) if k in hbm else v
        for k, v in enumerate(args)
    ]
    return pl.pallas_call(
        kernel,
        out_shape=[jax.ShapeDtypeStruct(s, F32) for s in outs],
        in_specs=[spec(k, hbm) for k in range(len(args))],
        out_specs=[spec(k, hbm_out) for k in range(len(outs))],
        scratch_shapes=[pltpu.VMEM(v, F32) if isinstance(v, tuple) else v for v in scratch],
        input_output_aliases=aliases or {},
        compiler_params=pltpu.CompilerParams(vmem_limit_bytes=limit << 20),
    )(*args)


def halves(value):
    top = value.astype(jnp.bfloat16)
    return top, (value - top.astype(F32)).astype(jnp.bfloat16)


def mxu(one, two, dims=((1,), (0,))):
    return lax.dot_general(one, two, (dims, ((), ())), preferred_element_type=F32)


def side(plan, axis, ref_a, ref_b, high):
    a_high = plan.high(axis, 0)[1]
    if high:
        return jnp.where(a_high, ref_a, ref_b)
    return jnp.where(a_high, ref_b, ref_a)


def pack_x(plan, ref, out_a, out_b):
    last = plan.nx - 1
    for which, out in ((0, out_a), (1, out_b)):
        out[...] = ref[jnp.where(plan.high("gx", which)[0], last, 0)]


def pack_y(plan, ref, out_a, out_b):
    low, top = ref[:, 0, :], ref[:, plan.ny - 1, :]
    for which, out in ((0, out_a), (1, out_b)):
        out[...] = jnp.where(plan.high("gy", which)[0], top, low)


def tile_put(plan, tile, i, q, value):
    group = 128 // plan.ny
    r = i // group
    rows = pl.ds((i % group) * plan.ny, plan.ny)
    moved = pltpu.roll(value, r + plan.high("gz", q)[0].astype(jnp.int32), 1)
    tile[q, rows, :] = jnp.where(lanes_of(value.shape) == r, moved, tile[q, rows, :])


def tile_out(plan, tile, outs):
    for q, out in zip(plan.z_msgs, outs):
        out[...] = jnp.transpose(tile[q])[: out.shape[0], :]


def spread(plan, gots, outs):
    vals = [got[...] for got in gots]
    if len(vals) > 1:
        vals = list(z_sides(plan, vals))
    for val, out in zip(vals, outs):
        turned = jnp.transpose(val)
        for r in range(val.shape[0]):
            out[r * 128 : (r + 1) * 128, :] = jnp.broadcast_to(turned[:, r : r + 1], (128, 128))


def stack_rows(parts):
    cells = parts[0].shape[1]
    row = rows_of((8, cells))
    out = jnp.zeros((8, cells), F32)
    for k, part in enumerate(parts):
        out = jnp.where(row == k, jnp.broadcast_to(part, (8, cells)), out)
    return out


def z_sides(plan, vals):
    low, top = jnp.zeros_like(vals[0]), jnp.zeros_like(vals[0])
    for q, val in zip(plan.z_msgs, vals):
        up = plan.high("gz", q)[1]
        low = low + jnp.where(up, 0.0, val)
        top = top + jnp.where(up, val, 0.0)
    return low, top


def mobility_kernel(
    plan, press_in, sat_in, perm_in, rock_in, oil_in,
    press, sat, mob, coef, frac, xa, xb, ya, yb, total, perm, rock, oil, sem, oil_sem,
):
    kinds = oil.shape[0]
    oil_move = pltpu.make_async_copy(oil_in, oil, oil_sem)
    oil_move.start()
    size = plan.nx // CHUNKS
    moves = []
    for c in range(CHUNKS):
        cut = pl.ds(c * size, size)
        for k, (src, dst) in enumerate(
            ((sat_in, sat), (rock_in, rock), (perm_in, perm), (press_in, press))
        ):
            move = pltpu.make_async_copy(src.at[cut], dst.at[cut], sem.at[c, k])
            move.start()
            moves.append(move)

    def layer(i, acc):
        s, kind = sat[i], rock[i]
        c = jnp.full(s.shape, oil[0], F32)
        for k in range(1, kinds):
            c = jnp.where(kind == k, oil[k], c)
        water, rest = s * s, 1.0 - s
        den = water + c * rest * rest
        m = perm[i] * den
        coef[i] = c
        mob[i] = m
        frac[i] = water / den
        return acc + m

    acc = jnp.zeros((plan.ny, plan.nz), F32)
    oil_move.wait()
    for c in range(CHUNKS):
        for move in moves[4 * c : 4 * c + 3]:
            move.wait()
        acc = lax.fori_loop(c * size, (c + 1) * size, layer, acc, unroll=4)
    total[...] = acc
    for c in range(CHUNKS):
        moves[4 * c + 3].wait()
    for k, ref in enumerate((press, mob, frac)):
        pack_x(plan, ref, xa.at[k], xb.at[k])
        pack_y(plan, ref, ya.at[k], yb.at[k])


def inner_kernel(plan, press, mob, source, compress, well, res, tx, ty, tz, diag):
    shape = (plan.ny, plan.nz)
    row, lane = rows_of(shape), lanes_of(shape)

    def layer(i, carry):
        p_last, m_last, r_last = carry
        p, m = press[i], mob[i]
        t = harmonic(m_last, m)
        tx[i] = t
        flux_x = t * (p_last - p)
        t = harmonic(jnp.where(row == 0, 0.0, ahead(m, 0)), m)
        ty[i] = t
        flux_y = t * (ahead(p, 0) - p)
        t = harmonic(jnp.where(lane == 0, 0.0, ahead(m, 1)), m)
        tz[i] = t
        flux_z = t * (ahead(p, 1) - p)
        d = compress[i] + WELL_INDEX * well[i].astype(F32) * m
        diag[i] = d
        r = source[i] - d * p + flux_x + (flux_y - back(flux_y, 0)) + (flux_z - back(flux_z, 1))
        res[jnp.maximum(i - 1, 0)] = r_last - flux_x
        return p, m, r

    zero = jnp.zeros(shape, F32)
    res[plan.nx - 1] = lax.fori_loop(0, plan.nx, layer, (zero, zero, zero), unroll=2)[2]


def rim_kernel(plan, res_in, press, mob, frac, xa, xb, ya, yb, res, *rest):
    z_outs, comp = rest[:-1], rest[-1]
    nx, ny, nz = plan.nx, plan.ny, plan.nz
    last = nx - 1
    for high, k in ((False, 0), (True, last)):
        p, m = (side(plan, "gx", xa[f], xb[f], high) for f in (0, 1))
        res[k] = res[k] + harmonic(mob[k], m) * (p - press[k])
    for high, k in ((False, 0), (True, ny - 1)):
        p, m = (side(plan, "gy", ya[f], yb[f], high) for f in (0, 1))
        res[:, k, :] = res[:, k, :] + harmonic(mob[:, k, :], m) * (p - press[:, k, :])
    lane = lanes_of((ny, nz))
    wide = INTERSECTION
    for q, out in zip(plan.z_msgs, z_outs):
        up = plan.high("gz", q)[0].astype(jnp.int32)

        def layer(i, carry):
            acc = pltpu.roll(res[i], up * wide, 1)
            for k, ref in enumerate((press, mob, frac)):
                acc = jnp.where(lane < wide + k, acc, pltpu.roll(ref[i], wide + k + up, 1))
            comp[pl.ds(i * ny, ny), :] = acc
            return carry

        lax.fori_loop(0, nx, layer, 0, unroll=4)
        for k in range(nx * ny // 128):
            cut = slice(k * 128, (k + 1) * 128)
            out[:, cut] = jnp.transpose(comp[cut, :])[:MSG_ROWS, :]


def z_flux(plan, sent, got):
    wide = INTERSECTION
    out = []
    for own, other in zip(sent, got):
        t = harmonic(own[wide + 1 : wide + 2, :], other[wide + 1 : wide + 2, :])
        q = t * (other[wide : wide + 1, :] - own[wide : wide + 1, :])
        out.append((other[wide : wide + 1, :], other[wide + 2 : wide + 3, :], t, q))
    return out


def z_kernel(plan, n_msg, res, basis, rim_low, rim_top, order, *rest):
    sent, got = rest[:n_msg], rest[n_msg : 2 * n_msg]
    spec, ya, yb = rest[2 * n_msg :]
    nx, ny, nz = plan.nx, plan.ny, plan.nz
    wide = INTERSECTION
    mixes, rims = [], []
    for q, other, (_, _, _, flux) in zip(plan.z_msgs, got, z_flux(plan, sent, got)):
        up = plan.high("gz", q)[1]
        row = rows_of(other.shape)
        near = jnp.where(up, 0, wide - 1)
        flux = jnp.broadcast_to(flux, other.shape)
        mix = jnp.where(row < wide, other[...], 0.0)
        mix = jnp.where(row == near, mix - flux, mix)
        mix = jnp.where(row == wide, flux, mix)
        top, low = halves(mix)
        mixes.append(jnp.concatenate([top, low, top], axis=0))
        rims.append(jnp.where(up, rim_top[...], rim_low[...]).astype(jnp.bfloat16))
    group = 128 // ny
    for k in range(nx // group):
        value = res[k * group : (k + 1) * group].reshape(128, nz)
        top, low = halves(value)
        out = mxu(jnp.concatenate([top, low, top], axis=1), basis[...])
        for mix, rim in zip(mixes, rims):
            out = out + mxu(mix[:, k * 128 : (k + 1) * 128], rim, ((0,), (0,)))
        spec[k * group : (k + 1) * group] = out.reshape(group, ny, out.shape[1])
    tail = 2 * wide
    per = 128 // tail
    for which, ref in ((0, ya), (1, yb)):
        start = jnp.where(plan.high("gy", which)[0], ny - wide, 0)
        rows = pl.ds(pl.multiple_of(start, 8), wide)
        ref[:nx] = spec[:, rows, :nz]
        for g in range(nx // per):
            ref[nx + g] = jnp.concatenate(
                [spec[g * per + j, rows, nz:] for j in range(per)], axis=1
            )


def faces_xy_kernel(plan, mob, tx_in, ty_in, xa, xb, ya, yb, tx, ty_low, ty_top, hx, hy, ty_rim):
    nx, ny, nz = plan.nx, plan.ny, plan.nz
    for k, high in ((0, False), (1, True)):
        for f, field in ((0, 0), (1, 2)):
            hx[k, f] = side(plan, "gx", xa[field], xb[field], high)
            hy[k, f] = side(plan, "gy", ya[field], yb[field], high)
    tx[nx] = harmonic(mob[nx - 1], side(plan, "gx", xa[1], xb[1], True))
    ty_rim[0] = harmonic(mob[:, 0, :], side(plan, "gy", ya[1], yb[1], False))
    ty_rim[1] = harmonic(mob[:, ny - 1, :], side(plan, "gy", ya[1], yb[1], True))
    row = rows_of((ny, nz))

    def layer(i, carry):
        tx[i] = tx_in[i]
        ty = ty_in[i]
        ty_low[i] = jnp.where(row == 0, ty_rim[0, pl.ds(i, 1), :], ty)
        ty_top[i] = jnp.where(row == ny - 1, ty_rim[1, pl.ds(i, 1), :], back(ty, 0))
        return carry

    lax.fori_loop(0, nx, layer, 0, unroll=4)
    tx[0] = harmonic(mob[0], side(plan, "gx", xa[1], xb[1], False))


def faces_z_kernel(plan, n_msg, res, tz_in, poro, well, *rest):
    sent, got = rest[:n_msg], rest[n_msg : 2 * n_msg]
    full, tz_low, tz_top, hz, rate, inject = rest[2 * n_msg :]
    nx, ny, nz = plan.nx, plan.ny, plan.nz
    parts = z_flux(plan, sent, got)
    split = [z_sides(plan, [part[k] for part in parts]) for k in range(4)]
    rows = stack_rows([v for pair in split for v in pair])
    for k in range(nx * ny // 128):
        cut = slice(k * 128, (k + 1) * 128)
        hz[cut, :8] = jnp.transpose(rows[:, cut])
    lane = lanes_of((ny, nz))

    def layer(i, carry):
        tz = tz_in[i]
        col = hz[pl.ds(i * ny, ny), :8]
        tz_low[i] = jnp.where(lane == 0, col[:, 4:5], tz)
        tz_top[i] = jnp.where(lane == nz - 1, col[:, 5:6], back(tz, 1))
        flux = jnp.where(lane == 0, col[:, 6:7], 0.0) + jnp.where(
            lane == nz - 1, col[:, 7:8], 0.0
        )
        full[i] = res[i] + flux
        rate[i] = poro[i] / TIME_STEP
        inject[i] = INJECT_RATE * well[i].astype(F32)
        return carry

    lax.fori_loop(0, nx, layer, 0, unroll=4)


def wide_rows(plan, msg_a, msg_b, i, high):
    nx = plan.nx
    tail = 2 * INTERSECTION
    per = 128 // tail
    ends = side(plan, "gy", msg_a[nx + i // per], msg_b[nx + i // per], high)
    ends = pltpu.roll(ends, (128 - (i % per) * tail) % 128, 1)[:, :tail]
    return jnp.concatenate([side(plan, "gy", msg_a[i], msg_b[i], high), ends], axis=1)


def thrice(value):
    top, low = halves(value)
    return jnp.concatenate([top, low, top], axis=0)


def fold(value, nz):
    rows, tail = value.shape[0], value.shape[1] - nz
    ends = jnp.concatenate(
        [value[k : k + 8, nz:] for k in range(0, rows, 8)]
        + [jnp.zeros((8, nz - rows // 8 * tail), F32)],
        axis=1,
    )
    return jnp.concatenate([value[:, :nz], ends], axis=0)


def unfold(value, tail):
    rows = value.shape[0] - 8
    ends = jnp.concatenate(
        [value[rows:, k * tail : (k + 1) * tail] for k in range(rows // 8)], axis=0
    )
    return jnp.concatenate([value[:rows], ends], axis=1)


def y_kernel(plan, spec, ya, yb, basis, factors, order, modes, xa, xb):
    nx = plan.nx
    wide = INTERSECTION

    def layer(i, carry):
        low = wide_rows(plan, ya, yb, i, False)
        top = wide_rows(plan, ya, yb, i, True)
        modes[i] = mxu(basis[...], thrice(jnp.concatenate([low, spec[i], top], axis=0)))
        return carry

    lax.fori_loop(0, nx, layer, 0, unroll=4)
    low = jnp.zeros(modes.shape[1:], F32)
    top = low
    for k in range(wide):
        low = (modes[wide - 1 - k] + low) * factors[k]
        top = (modes[nx - wide + k] + top) * factors[k]
    for which, out in ((0, xa), (1, xb)):
        out[...] = fold(jnp.where(plan.high("gx", which)[0], top, low), plan.nz)


def solve_kernel(
    plan, modes, xa, xb, factors, middle, basis_y, basis_z, total, direction, *rest
):
    (dxa, dxb, dya, dyb), z_outs, (work, tile) = rest[:4], rest[4:-2], rest[-2:]
    nx, ny, nz = plan.nx, plan.ny, plan.nz
    wide = INTERSECTION
    half = nx // 2
    low = unfold(side(plan, "gx", xa[...], xb[...], False), 2 * wide)
    top = unfold(side(plan, "gx", xa[...], xb[...], True), 2 * wide)

    def inward(k, carry):
        low, top = carry
        c = factors[wide + k]
        low = (modes[k] + low) * c
        top = (modes[nx - 1 - k] + top) * c
        modes[k] = low
        modes[nx - 1 - k] = top
        return low, top

    low, top = lax.fori_loop(0, half, inward, (low, top), unroll=2)
    c, mid = factors[wide + half - 1], middle[...]
    low, top = (low + c * top) * mid, (top + c * low) * mid

    def put(i, value):
        work[pl.ds(i * ny, ny), :] = mxu(basis_y[...], thrice(value))

    put(half - 1, low)
    put(half, top)

    def outward(k, carry):
        low, top = carry
        i = half - 2 - k
        c = factors[wide + i]
        low = modes[i] + c * low
        top = modes[nx - 1 - i] + c * top
        put(i, low)
        put(nx - 1 - i, top)
        return low, top

    lax.fori_loop(0, half - 1, outward, (low, top), unroll=3)
    mean = jnp.sum(jnp.sum(total[...], axis=0, keepdims=True), axis=1, keepdims=True) / (
        nx * ny * nz
    )
    inverse = 1.0 / mean
    group = 128 // ny
    base_top, base_low = basis_z[0], basis_z[1]

    def lift(r, carry):
        high, rest_ = halves(work[pl.ds(r * 128, 128), :])
        value = mxu(high, base_top) + (mxu(rest_, base_top) + mxu(high, base_low))
        value = value * inverse
        direction[pl.ds(r * group, group)] = value.reshape(group, ny, nz)
        for q in plan.z_msgs:
            moved = pltpu.roll(value, r + plan.high("gz", q)[0].astype(jnp.int32), 1)
            tile[q] = jnp.where(lanes_of((128, nz)) == r, moved, tile[q])
        return carry

    lax.fori_loop(0, nx // group, lift, 0, unroll=2)
    pack_x(plan, direction, dxa, dxb)
    pack_y(plan, direction, dya, dyb)
    tile_out(plan, tile, z_outs)


def image_kernel(
    plan, n_dev, direction, diag, full, tx, ty_low, ty_top, tz_low, tz_top, xa, xb, ya, yb, *rest
):
    n_msg = len(plan.z_msgs)
    got = rest[:n_msg]
    image, sums = rest[n_msg : n_msg + 2]
    hz, hy = rest[n_msg + 2 : -1], rest[-1]
    nx, ny, nz = plan.nx, plan.ny, plan.nz
    spread(plan, got, hz)
    hy[0] = side(plan, "gy", ya[...], yb[...], False)
    hy[1] = side(plan, "gy", ya[...], yb[...], True)
    row, lane = rows_of((ny, nz)), lanes_of((ny, nz))

    def layer(i, carry):
        d_last, im_last, rd, da = carry
        d = direction[i]
        flux = tx[i] * (d_last - d)
        cells = pl.ds(i * ny, ny)
        y_last = jnp.where(row == 0, hy[0, pl.ds(i, 1), :], ahead(d, 0))
        y_next = jnp.where(row == ny - 1, hy[1, pl.ds(i, 1), :], back(d, 0))
        z_last = jnp.where(lane == 0, hz[0][cells, :], ahead(d, 1))
        z_next = jnp.where(lane == nz - 1, hz[-1][cells, :], back(d, 1))
        im = (
            diag[i] * d
            - flux
            + (ty_low[i] * (d - y_last) + ty_top[i] * (d - y_next))
            + (tz_low[i] * (d - z_last) + tz_top[i] * (d - z_next))
        )
        im_last = im_last + flux
        image[jnp.maximum(i - 1, 0)] = im_last
        rd = rd + full[i] * d
        da = da + jnp.where(i > 0, d_last, 0.0) * im_last
        return d, im, rd, da

    zero = jnp.zeros((ny, nz), F32)
    low = side(plan, "gx", xa[...], xb[...], False)
    top = side(plan, "gx", xa[...], xb[...], True)
    d, im, rd, da = lax.fori_loop(0, nx, layer, (low, zero, zero, zero), unroll=4)
    im = im + tx[nx] * (d - top)
    image[nx - 1] = im
    da = da + d * im
    lane = lanes_of((n_dev, 128))
    sums[...] = jnp.where(lane < 64, jnp.sum(rd), jnp.sum(da))


def sweep(plan, first, refs, x_low, x_top, hy, z_at, done):
    nx, ny, nz = plan.nx, plan.ny, plan.nz
    (start, now, frac, coef, rate, inject, gx, gy_low, gy_top, gz_low, gz_top, outflow) = refs
    row, lane = rows_of((ny, nz)), lanes_of((ny, nz))

    def upwind(g, low, high):
        return g * jnp.where(g > 0.0, low, high)

    def layer(i, carry):
        f, flow = carry
        f_next = jnp.where(i == nx - 1, x_top, frac[jnp.minimum(i + 1, nx - 1)])
        s, c = now[i], coef[i]
        flow_next = upwind(gx[i + 1], f, f_next)
        y_last = jnp.where(row == 0, hy[0, pl.ds(i, 1), :], ahead(f, 0))
        y_next = jnp.where(row == ny - 1, hy[1, pl.ds(i, 1), :], back(f, 0))
        z_low, z_top = z_at(i)
        z_last = jnp.where(lane == 0, z_low, ahead(f, 1))
        z_next = jnp.where(lane == nz - 1, z_top, back(f, 1))
        bal = (
            (flow_next - flow)
            + (upwind(gy_top[i], f, y_next) - upwind(gy_low[i], y_last, f))
            + (upwind(gz_top[i], f, z_next) - upwind(gz_low[i], z_last, f))
            - inject[i]
        )
        if not first:
            bal = bal + rate[i] * (s - start[i])
        rest = 1.0 - s
        part = c * rest
        den = s * s + part * rest
        square = den * den
        slope = 2.0 * part * s
        s = s - bal * square / (rate[i] * square + outflow[i] * jnp.abs(slope))
        done(i, s, c)
        return f_next, flow_next

    f0 = frac[0]
    lax.fori_loop(0, nx, layer, (f0, upwind(gx[0], x_low, f0)), unroll=4)


def keep(plan, new, new_frac, tile):
    def done(i, s, c):
        new[i] = s
        water, rest = s * s, 1.0 - s
        f = water / (water + c * rest * rest)
        new_frac[i] = f
        for q in plan.z_msgs:
            tile_put(plan, tile, i, q, f)

    return done


def pack_all(plan, ref, tile, outs):
    xa, xb, ya, yb = outs[:4]
    pack_x(plan, ref, xa, xb)
    pack_y(plan, ref, ya, yb)
    tile_out(plan, tile, outs[4:])


def step_of(sums):
    both = jnp.sum(sums[...], axis=0, keepdims=True)
    return both[:, 0:1] / both[:, 64:65]


def write_out(plan, i, ref, out, sem):
    size = plan.nx // CHUNKS

    @pl.when(i % size == size - 1)
    def _():
        c = i // size
        cut = pl.ds(c * size, size)
        pltpu.make_async_copy(ref.at[cut], out.at[cut], sem.at[c]).start()


def write_end(plan, ref, out, sem):
    size = plan.nx // CHUNKS
    for c in range(CHUNKS):
        cut = pl.ds(c * size, size)
        pltpu.make_async_copy(ref.at[cut], out.at[cut], sem.at[c]).wait()


def output_kernel(plan, sums, press, direction, full, image, p_out, r_out, token, p_new, r_new, p_sem, r_sem):
    step = step_of(sums)

    def layer(i, carry):
        p_new[i] = press[i] + step * direction[i]
        write_out(plan, i, p_new, p_out, p_sem)
        r_new[i] = full[i] - step * image[i]
        write_out(plan, i, r_new, r_out, r_sem)
        return carry

    lax.fori_loop(0, plan.nx, layer, 0, unroll=4)
    token[...] = jnp.zeros(token.shape, F32)
    write_end(plan, p_new, p_out, p_sem)
    write_end(plan, r_new, r_out, r_sem)


def step_kernel(plan, *refs):
    n_msg = len(plan.z_msgs)
    (sums, press, direction, tx, ty_low, ty_top, tz_low, tz_top) = refs[:8]
    (hx, hy, hz, dxa, dxb, dya, dyb) = refs[8:15]
    dhz = refs[15 : 15 + n_msg]
    (sat, frac, coef, rate, inject) = refs[15 + n_msg : 20 + n_msg]
    outs = refs[20 + n_msg :]
    (s_new, f_new, gx, gy_low, gy_top, gz_low, gz_top, outflow) = outs[:8]
    packs = outs[8 : 12 + n_msg]
    ph, fh, tile = outs[12 + n_msg :]
    nx, ny, nz = plan.nx, plan.ny, plan.nz
    step = step_of(sums)
    x_low = hx[0, 0] + step * side(plan, "gx", dxa[...], dxb[...], False)
    x_top = hx[1, 0] + step * side(plan, "gx", dxa[...], dxb[...], True)
    ph[0] = hy[0, 0] + step * side(plan, "gy", dya[...], dyb[...], False)
    ph[1] = hy[1, 0] + step * side(plan, "gy", dya[...], dyb[...], True)
    fh[0] = hy[0, 1]
    fh[1] = hy[1, 1]
    row, lane = rows_of((ny, nz)), lanes_of((ny, nz))

    def layer(i, carry):
        p, g = carry
        k = jnp.minimum(i + 1, nx - 1)
        p_next = jnp.where(i == nx - 1, x_top, press[k] + step * direction[k])
        g_next = tx[i + 1] * (p - p_next)
        gx[i + 1] = g_next
        cells = pl.ds(i * ny, ny)
        y_last = jnp.where(row == 0, ph[0, pl.ds(i, 1), :], ahead(p, 0))
        y_next = jnp.where(row == ny - 1, ph[1, pl.ds(i, 1), :], back(p, 0))
        z_low = hz[cells, 0:1] + step * dhz[0][cells, :]
        z_top = hz[cells, 1:2] + step * dhz[-1][cells, :]
        z_last = jnp.where(lane == 0, z_low, ahead(p, 1))
        z_next = jnp.where(lane == nz - 1, z_top, back(p, 1))
        parts = (
            (gy_low, ty_low[i] * (y_last - p), -1.0),
            (gy_top, ty_top[i] * (p - y_next), 1.0),
            (gz_low, tz_low[i] * (z_last - p), -1.0),
            (gz_top, tz_top[i] * (p - z_next), 1.0),
        )
        total = jnp.maximum(g_next, 0.0) - jnp.minimum(g, 0.0)
        for ref, value, sign in parts:
            ref[i] = value
            if sign > 0:
                total = total + jnp.maximum(value, 0.0)
            else:
                total = total - jnp.minimum(value, 0.0)
        outflow[i] = total
        return p_next, g_next

    p0 = press[0] + step * direction[0]
    g0 = tx[0] * (x_low - p0)
    gx[0] = g0
    lax.fori_loop(0, nx, layer, (p0, g0), unroll=4)

    def z_at(i):
        cells = pl.ds(i * ny, ny)
        return hz[cells, 2:3], hz[cells, 3:4]

    sweep(
        plan, True,
        (sat, sat, frac, coef, rate, inject, gx, gy_low, gy_top, gz_low, gz_top, outflow),
        hx[0, 1], hx[1, 1], fh, z_at, keep(plan, s_new, f_new, tile),
    )
    pack_all(plan, f_new, tile, packs)


def later_kernel(plan, last_sweep, *refs):
    n_msg = len(plan.z_msgs)
    fields = refs[:12]
    xa, xb, ya, yb = refs[12:16]
    got = refs[16 : 16 + n_msg]
    rest = refs[17 + n_msg :]
    if last_sweep:
        out, new, sem, fh, *hz = rest

        def done(i, s, c):
            new[i] = s
            write_out(plan, i, new, out, sem)
    else:
        new, new_frac = rest[:2]
        packs = rest[2 : 6 + n_msg]
        tile, fh, *hz = rest[6 + n_msg :]
        done = keep(plan, new, new_frac, tile)
    ny = plan.ny
    spread(plan, got, hz)
    fh[0] = side(plan, "gy", ya[...], yb[...], False)
    fh[1] = side(plan, "gy", ya[...], yb[...], True)

    def z_at(i):
        cells = pl.ds(i * ny, ny)
        return hz[0][cells, :], hz[-1][cells, :]

    sweep(
        plan, False, fields,
        side(plan, "gx", xa[...], xb[...], False), side(plan, "gx", xa[...], xb[...], True),
        fh, z_at, done,
    )
    if last_sweep:
        write_end(plan, new, out, sem)
    else:
        pack_all(plan, new_frac, tile, packs)


def per_device(
    counts, pressure, source, saturation, permeability, compress, porosity, rock_type, well_mask, oil_factor
):
    nx, ny, nz = pressure.shape
    wide = INTERSECTION
    plan = Plan(nx, ny, nz, counts)
    n_msg = len(plan.z_msgs)
    n_dev = counts["gx"] * counts["gy"] * counts["gz"]
    cells = nx * ny
    my, mz = ny + 2 * wide, nz + 2 * wide
    table_y, eigen_y = sine_basis(my)
    table_z, eigen_z = sine_basis(mz)
    factors, middle = sweep_factors(wide + nx // 2, eigen_y, eigen_z)
    const = lambda v: jnp.asarray(v, F32)
    factors, middle = const(factors), const(middle)
    rim = np.zeros((2, MSG_ROWS, mz))
    rim[0, :wide] = table_z[:wide]
    rim[0, wide] = table_z[wide]
    rim[1, :wide] = table_z[mz - wide :]
    rim[1, wide] = table_z[mz - wide - 1]

    def parts(v):
        v = np.asarray(v, np.float32)
        top = v.astype(jnp.bfloat16)
        return top, (v - top.astype(np.float32)).astype(jnp.bfloat16)

    def left(v):
        top, low = parts(v)
        return jnp.asarray(np.concatenate([top, top, low], axis=1))

    def right(v):
        top, low = parts(v)
        return jnp.asarray(np.concatenate([top, top, low], axis=0))

    rims = [jnp.concatenate([right(v)], axis=0).astype(F32) for v in rim]

    def swap(axis, a, b):
        return (
            lax.ppermute(a, axis, plan.perm(axis, 0)),
            lax.ppermute(b, axis, plan.perm(axis, 1)),
        )

    def swap_z(msgs):
        return [lax.ppermute(v, "gz", plan.perm("gz", q)) for q, v in zip(plan.z_msgs, msgs)]

    full_shape = (nx, ny, nz)
    x_face, y_face, z_face = (ny, nz), (nx, nz), (cells // 128, 128)
    face_shapes = [x_face, x_face, y_face, y_face] + [z_face] * n_msg
    tile = (2, 128, nz)
    spreads = [(cells, 128)] * n_msg
    dma = pltpu.SemaphoreType.DMA

    def exchange(packs):
        z = swap_z(packs[4:])
        y = swap("gy", packs[2], packs[3])
        x = swap("gx", packs[0], packs[1])
        return [*x, *y, *z]

    press, sat, mob, coef, frac, xa, xb, ya, yb, total = call(
        functools.partial(mobility_kernel, plan),
        [full_shape] * 5 + [(3,) + x_face] * 2 + [(3,) + y_face] * 2 + [x_face],
        (pressure, saturation, permeability, rock_type, oil_factor),
        hbm=(0, 1, 2, 3, 4),
        scratch=[full_shape, pltpu.VMEM(full_shape, jnp.int32),
                 pltpu.SMEM(oil_factor.shape, F32), dma((CHUNKS, 4)), dma],
    )
    ya, yb = swap("gy", ya, yb)
    xa, xb = swap("gx", xa, xb)
    res, tx, ty, tz, diag = call(
        functools.partial(inner_kernel, plan),
        [full_shape] * 5,
        (press, mob, source, compress, well_mask),
    )
    res, *sent = call(
        functools.partial(rim_kernel, plan),
        [full_shape] + [(MSG_ROWS, cells)] * n_msg,
        (res, press, mob, frac, xa, xb, ya, yb),
        scratch=[(cells, nz)],
        aliases={0: 0},
    )
    got = swap_z(sent)
    tx, ty_low, ty_top, hx, hy = call(
        functools.partial(faces_xy_kernel, plan),
        [(nx + 1, ny, nz)] + [full_shape] * 2 + [(2, 2) + x_face, (2, 2) + y_face],
        (mob, tx, ty, xa, xb, ya, yb),
        scratch=[(2,) + y_face],
    )
    spec, sa, sb = call(
        functools.partial(z_kernel, plan, n_msg),
        [(nx, ny, mz)] + [(nx + nx * 2 * wide // 128, wide, nz)] * 2,
        (res, right(table_z[wide : wide + nz]), *rims, hx, *sent, *got),
    )
    sa, sb = swap("gy", sa, sb)
    full, tz_low, tz_top, hz, rate, inject = call(
        functools.partial(faces_z_kernel, plan, n_msg),
        [full_shape] * 3 + [(cells, 128)] + [full_shape] * 2,
        (res, tz, porosity, well_mask, *sent, *got),
    )
    modes, ma, mb = call(
        functools.partial(y_kernel, plan),
        [(nx, my, mz), (my + 8, nz), (my + 8, nz)],
        (spec, sa, sb, left(table_y), factors, hz),
    )
    ma, mb = swap("gx", ma, mb)
    direction, *packs = call(
        functools.partial(solve_kernel, plan),
        [full_shape] + face_shapes,
        (modes, ma, mb, factors, middle, left(table_y[wide : wide + ny]),
         jnp.asarray(np.stack(parts(table_z[:, wide : wide + nz]))), total),
        scratch=[(cells, mz), tile],
    )
    dhalo = exchange(packs)
    image, sums, *dhz = call(
        functools.partial(image_kernel, plan, n_dev),
        [full_shape, (n_dev, 128)] + spreads,
        (direction, diag, full, tx, ty_low, ty_top, tz_low, tz_top, *dhalo),
        scratch=[(2,) + y_face],
    )
    sums = lax.all_to_all(sums, AXES, 0, 0, tiled=True)
    outs = call(
        functools.partial(step_kernel, plan),
        [full_shape] * 2 + [(nx + 1, ny, nz)] + [full_shape] * 5 + face_shapes,
        (sums, press, direction, tx, ty_low, ty_top, tz_low, tz_top,
         hx, hy, hz, *dhalo[:4], *dhz, sat, frac, coef, rate, inject),
        scratch=[(2,) + y_face] * 2 + [tile],
        limit=40,
    )
    current, frac, *flows = outs[:8]
    packs = outs[8:]
    p_new, r_new, token = call(
        functools.partial(output_kernel, plan),
        [full_shape] * 2 + [(8, 128)],
        (sums, press, direction, full, image),
        hbm_out=(0, 1),
        scratch=[full_shape] * 2 + [dma((CHUNKS,))] * 2,
    )
    for sweep_index in range(1, NEWTON):
        halo = exchange(packs)
        last_sweep = sweep_index == NEWTON - 1
        outs = call(
            functools.partial(later_kernel, plan, last_sweep),
            [full_shape] if last_sweep else [full_shape] * 2 + face_shapes,
            (sat, current, frac, coef, rate, inject, *flows, *halo, token),
            scratch=([full_shape, dma((CHUNKS,))] if last_sweep else [tile])
            + [(2,) + y_face] + spreads,
            hbm_out=(0,) if last_sweep else (),
        )
        current = outs[0]
        if not last_sweep:
            frac, packs = outs[1], outs[2:]
    return p_new, r_new, current


def solution(mesh):
    spec = P(*AXES)
    return jax.shard_map(
        functools.partial(per_device, dict(mesh.shape)),
        mesh=mesh,
        in_specs=(spec,) * 8 + (P(),),
        out_specs=(spec,) * 3,
        check_vma=False,
    )
```

time: 96.4 us -> 77.4 us (0.80)
  Pallas kernels: 35.5 us -> 23.9 us
  local copies, waits for them, and re-layouts: 4.9 us -> 0.07 us
  waiting for transfers between devices: 20.8 us -> 16.8 us
    pallas_call x11 -> x13, Pallas kernels: 35.5 us -> 23.9 us  [call(): pl.pallas_call(kernel, out_shape=[jax.ShapeDtypeStruct(s, F32) for s in o...]
    ppermute x10, waiting for transfers between devices: 13.2 us -> 5.23 us  [swap(): lax.ppermute(b, axis, plan.perm(axis, 1))]
    ppermute x4, waiting for transfers between devices: 2.75 us -> 9.49 us  [swap_z(): lax.ppermute(v, 'gz', plan.perm('gz', q))]
    unnamed x38 -> x24, local copies, waits for them, and re-layouts: 4.9 us -> 0.07 us
    ppermute x10, waiting for transfers between devices: 4.84 us -> 2.1 us  [swap(): lax.ppermute(a, axis, plan.perm(axis, 0))]
    ppermute x10, starting transfers between devices: 14.2 us -> 16.4 us  [swap(): lax.ppermute(b, axis, plan.perm(axis, 1))]
  transfers between devices with their start and end apart: 24 -> 24, of which waited for: 9 -> 7; matrix products, arithmetic and copies ran while one was open for 0% -> 0% of each run, Pallas kernels for 7% -> 7%
where the time goes in v1:
time: 77.4 us; the launch traced here: 77.2 us
  starting transfers between devices  25 us (32%)
  Pallas kernels  23.9 us (31%)
  waiting for transfers between devices  16.8 us (22%)
  blocking collectives  10.5 us (14%)
  between operations  0.89 us (1%)
    pallas_call x13, Pallas kernels, call(): pl.pallas_call(kernel, out_shape=[jax.ShapeDtypeStruct(s, F32) for s in o...  23.9 us
    ppermute x10, starting transfers between devices, swap(): lax.ppermute(b, axis, plan.perm(axis, 1))  16.4 us
    all_to_all x1, blocking collectives, per_device(): sums = lax.all_to_all(sums, AXES, 0, 0, tiled=True)  10.5 us
    ppermute x4, waiting for transfers between devices, swap_z(): lax.ppermute(v, 'gz', plan.perm('gz', q))  9.49 us
    ppermute x10, waiting for transfers between devices, swap(): lax.ppermute(b, axis, plan.perm(axis, 1))  5.23 us
    ppermute x10, starting transfers between devices, swap(): lax.ppermute(a, axis, plan.perm(axis, 0))  4.48 us
    ppermute x4, starting transfers between devices, swap_z(): lax.ppermute(v, 'gz', plan.perm('gz', q))  4.14 us
    ppermute x10, waiting for transfers between devices, swap(): lax.ppermute(a, axis, plan.perm(axis, 0))  2.1 us
  transfers between devices with their start and end apart: 24, of which 7 were waited for; matrix products, arithmetic and copies ran while one was open for 0% of the time, Pallas kernels for 7%

profile of v1, /device:TPU:0, one launch (start us, length us, event | category | flops | bytes accessed | tf_op | source)
XLA Modules:
  0.0 77.2 jit_solution(3823746558898758764)
XLA Ops:
  0.7 2.0 %shard_map.184 = (f32[32,32,128]{2,1,0:T(8,128)S(1)}, f32[32,32,128]{2,1,0:T(8,128)S(1)}, f32[32,32,128]{2,1,0:T(8,128)S(1)}, f32[32,32,128]{2,1,0:T(8,128)S(1)}...) custom-call(f32[32,32,128]{2,1,0:T(8,128)} %press_in.1, ...), custom_call_target="tpu_custom_call" | custom-call | tf_op jit(solution)/shard_map/pallas_call | solution.py:108
  2.7 3.1 %collective-permute-start = (f32[3,32,128]{2,1,0:T(8,128)S(1)}, f32[3,32,128]{2,1,0:T(8,128)S(1)}, u32[]{:S(2)}, u32[]{:S(2)}) collective-permute-start(f32[3,32,128]{2,1,0:T(8,128)S(1)} %get-tuple-element.73), channel_id=1, source_target_pairs={{0,8},{8,0},{16,24},{24,16},{1,9},{9,1},{17,25},{25,17},{2,10},{10... | collective-permute-start | bytes 147464 | tf_op jit(solution)/shard_map/ppermute | solution.py:781
  5.8 2.5 %collective-permute-start.1 = (f32[3,32,128]{2,1,0:T(8,128)S(1)}, f32[3,32,128]{2,1,0:T(8,128)S(1)}, u32[]{:S(2)}, u32[]{:S(2)}) collective-permute-start(f32[3,32,128]{2,1,0:T(8,128)S(1)} %get-tuple-element.74), channel_id=1, source_target_pairs={{8,16},{16,8},{24,0},{0,24},{9,17},{17,9},{25,1},{1,25},{10,18},{1... | collective-permute-start | bytes 147464 | tf_op jit(solution)/shard_map/ppermute | solution.py:782
  8.3 0.0 collective-permute-start.2
  8.3 1.6 %collective-permute-start.3 = (f32[3,32,128]{2,1,0:T(8,128)S(1)}, f32[3,32,128]{2,1,0:T(8,128)S(1)}, u32[]{:S(2)}, u32[]{:S(2)}) collective-permute-start(f32[3,32,128]{2,1,0:T(8,128)S(1)} %get-tuple-element.76), channel_id=1, source_target_pairs={{2,4},{4,2},{6,0},{0,6},{3,5},{5,3},{7,1},{1,7},{10,12},{12,10},{1... | collective-permute-start | bytes 147464 | tf_op jit(solution)/shard_map/ppermute | solution.py:782
  9.9 2.5 %shard_map.185 = (f32[32,32,128]{2,1,0:T(8,128)S(1)}, f32[32,32,128]{2,1,0:T(8,128)S(1)}, f32[32,32,128]{2,1,0:T(8,128)S(1)}, f32[32,32,128]{2,1,0:T(8,128)S(1)}, f32[32,32,128]{2,1,0:T(8,128)S(1)}) custom-call(f32[32,32,128]{2,1,0:T(8,128)S(1)} %get-tuple-element.69.press.refs_1_, f32[32,32,128]{2,1,0:T(8,128)S(1)} %get-tuple-element.70.mob, ...), custom_call_target="tpu_custom_call" | custom-call | tf_op jit(solution)/shard_map/pallas_call | solution.py:108
  12.4 0.0 collective-permute-done.xa
  12.4 0.0 collective-permute-done.1.xb
  12.4 0.0 collective-permute-done.2.ya
  12.5 0.0 collective-permute-done.3.yb
  12.5 0.0 copy-start.5
  12.5 0.0 copy-start.7
  12.5 0.0 copy-start.8
  12.5 1.4 %shard_map.186 = (f32[32,32,128]{2,1,0:T(8,128)S(1)}, f32[16,1024]{1,0:T(8,128)S(1)}) custom-call(f32[32,32,128]{2,1,0:T(8,128)S(1)} %get-tuple-element.71.res_in, f32[32,32,128]{2,1,0:T(8,128)S(1)} %get-tuple-element.69.press.refs_1_, f32[32,32,128]{2,1,0:T(8,128)S(1)} %get-tuple-element.70.mob, ...), custom_call_target="tpu_custom_call", output_to_operand_aliasing={{0}: (0, {})} | custom-call | tf_op jit(solution)/shard_map/pallas_call | solution.py:108
  13.9 1.6 %collective-permute-start.4 = (f32[16,1024]{1,0:T(8,128)S(1)}, f32[16,1024]{1,0:T(8,128)S(1)}, u32[]{:S(2)}, u32[]{:S(2)}) collective-permute-start(f32[16,1024]{1,0:T(8,128)S(1)} %get-tuple-element.81.rest_0_), channel_id=1, source_target_pairs={{0,1},{1,0},{2,3},{3,2},{4,5},{5,4},{6,7},{7,6},{8,9},{9,8},{10,11... | collective-permute-start | bytes 196616 | tf_op jit(solution)/shard_map/ppermute | solution.py:786
  15.5 0.2 shard_map.187
  15.7 2.5 %collective-permute-done.4.rest_1_ = f32[16,1024]{1,0:T(8,128)S(1)} collective-permute-done((f32[16,1024]{1,0:T(8,128)S(1)}, f32[16,1024]{1,0:T(8,128)S(1)}, u32[]{:S(2)}, u32[]{:S(2)}) %collective-permute-start.4) | collective-permute-done | bytes 65568 | tf_op jit(solution)/shard_map/ppermute | solution.py:786
  18.3 0.0 copy-start
  18.3 0.0 copy-start.10
  18.3 0.8 %shard_map.188 = (f32[32,32,144]{2,1,0:T(8,128)S(1)}, f32[36,8,128]{2,1,0:T(8,128)S(1)}, f32[36,8,128]{2,1,0:T(8,128)S(1)}) custom-call(f32[32,32,128]{2,1,0:T(8,128)S(1)} %get-tuple-element.77.res, bf16[384,144]{1,0:T(8,128)(2,1)S(1)} %copy-done.5, f32[48,144]{1,0:T(8,128)S(1)} %copy-done.8, f32[48,144]{1,0:T(8,128)S(1)} %copy-done.7, ...), custom_call_target="tpu_custom_call" | custom-call | tf_op jit(solution)/shard_map/pallas_call | solution.py:108
  19.1 0.1 collective-permute-start.5
  19.1 1.1 %collective-permute-start.6 = (f32[36,8,128]{2,1,0:T(8,128)S(1)}, f32[36,8,128]{2,1,0:T(8,128)S(1)}, u32[]{:S(2)}, u32[]{:S(2)}) collective-permute-start(f32[36,8,128]{2,1,0:T(8,128)S(1)} %get-tuple-element.84), channel_id=1, source_target_pairs={{2,4},{4,2},{6,0},{0,6},{3,5},{5,3},{7,1},{1,7},{10,12},{12,10},{1... | collective-permute-start | bytes 442376 | tf_op jit(solution)/shard_map/ppermute | solution.py:782
  20.3 1.7 %shard_map.189 = (f32[32,32,128]{2,1,0:T(8,128)S(1)}, f32[32,32,128]{2,1,0:T(8,128)S(1)}, f32[32,32,128]{2,1,0:T(8,128)S(1)}, f32[1024,128]{1,0:T(8,128)S(1)}, f...) custom-call(f32[32,32,128]{2,1,0:T(8,128)S(1)} %get-tuple-element.77.res, ...), custom_call_target="tpu_custom_call" | custom-call | tf_op jit(solution)/shard_map/pallas_call | solution.py:108
  22.0 0.0 copy-start.6
  22.0 0.0 copy-start.9
  22.0 0.0 copy-start.11
  22.0 0.0 collective-permute-done.5.ya
  22.0 2.7 %collective-permute-done.6.yb = f32[36,8,128]{2,1,0:T(8,128)S(1)} collective-permute-done((f32[36,8,128]{2,1,0:T(8,128)S(1)}, f32[36,8,128]{2,1,0:T(8,128)S(1)}, u32[]{:S(2)}, u32[]{:S(2)}) %collective-permute-start.6) | collective-permute-done | bytes 147488 | tf_op jit(solution)/shard_map/ppermute | solution.py:782
  24.7 2.2 %shard_map.190 = (f32[32,48,144]{2,1,0:T(8,128)S(1)}, f32[56,128]{1,0:T(8,128)S(1)}, f32[56,128]{1,0:T(8,128)S(1)}) custom-call(f32[32,32,144]{2,1,0:T(8,128)S(1)} %get-tuple-element.82.spec, f32[36,8,128]{2,1,0:T(8,128)S(1)} %collective-permute-done.5.ya, f32[36,8,128]{2,1,0:T(8,128)S(1)} %collective-permute-done.6.yb, bf16[48,144]{1,0:T(8,128)(2,1)S(1)} %copy-done.10, ...), custom_call_target="tpu_custom_call" | custom-call | tf_op jit(solution)/shard_map/pallas_call | solution.py:108
  26.9 0.7 collective-permute-start.7
  27.7 1.1 %collective-permute-start.8 = (f32[56,128]{1,0:T(8,128)S(1)}, f32[56,128]{1,0:T(8,128)S(1)}, u32[]{:S(2)}, u32[]{:S(2)}) collective-permute-start(f32[56,128]{1,0:T(8,128)S(1)} %get-tuple-element.89), channel_id=1, source_target_pairs={{8,16},{16,8},{24,0},{0,24},{9,17},{17,9},{25,1},{1,25},{10,18},{1... | collective-permute-start | bytes 86024 | tf_op jit(solution)/shard_map/ppermute | solution.py:782
  28.8 2.1 %collective-permute-done.7.xa = f32[56,128]{1,0:T(8,128)S(1)} collective-permute-done((f32[56,128]{1,0:T(8,128)S(1)}, f32[56,128]{1,0:T(8,128)S(1)}, u32[]{:S(2)}, u32[]{:S(2)}) %collective-permute-start.7) | collective-permute-done | bytes 28704 | tf_op jit(solution)/shard_map/ppermute | solution.py:781
  30.8 2.5 %collective-permute-done.8.xb = f32[56,128]{1,0:T(8,128)S(1)} collective-permute-done((f32[56,128]{1,0:T(8,128)S(1)}, f32[56,128]{1,0:T(8,128)S(1)}, u32[]{:S(2)}, u32[]{:S(2)}) %collective-permute-start.8) | collective-permute-done | bytes 28704 | tf_op jit(solution)/shard_map/ppermute | solution.py:782
  33.3 2.9 %shard_map.191 = (f32[32,32,128]{2,1,0:T(8,128)S(1)}, f32[32,128]{1,0:T(8,128)S(1)}, f32[32,128]{1,0:T(8,128)S(1)}, f32[32,128]{1,0:T(8,128)S(1)}, f32[32,128]{1,0:T(8,128)S(1)}, /*index=5*/f32[8,128]{1,0:T(8,128)S(1)}) custom-call(f32[32,48,144]{2,1,0:T(8,128)S(1)} %get-tuple-element.87.modes, f32[56,128]{1,0:T(8,128)S(1)} %collective-permute-done.7.xa, ...), custom_call_target="tpu_custom_call" | custom-call | tf_op jit(solution)/shard_map/pallas_call | solution.py:108
  36.3 0.0 collective-permute-start.9
  36.3 1.7 %collective-permute-start.10 = (f32[32,128]{1,0:T(8,128)S(1)}, f32[32,128]{1,0:T(8,128)S(1)}, u32[]{:S(2)}, u32[]{:S(2)}) collective-permute-start(f32[32,128]{1,0:T(8,128)S(1)} %get-tuple-element.100), channel_id=1, source_target_pairs={{8,16},{16,8},{24,0},{0,24},{9,17},{17,9},{25,1},{1,25},{10,18},{1... | collective-permute-start | bytes 49160 | tf_op jit(solution)/shard_map/ppermute | solution.py:782
  38.1 0.0 collective-permute-start.11
  38.1 1.6 %collective-permute-start.12 = (f32[32,128]{1,0:T(8,128)S(1)}, f32[32,128]{1,0:T(8,128)S(1)}, u32[]{:S(2)}, u32[]{:S(2)}) collective-permute-start(f32[32,128]{1,0:T(8,128)S(1)} %get-tuple-element.102), channel_id=1, source_target_pairs={{2,4},{4,2},{6,0},{0,6},{3,5},{5,3},{7,1},{1,7},{10,12},{12,10},{1... | collective-permute-start | bytes 49160 | tf_op jit(solution)/shard_map/ppermute | solution.py:782
  39.7 1.5 %collective-permute-start.13 = (f32[8,128]{1,0:T(8,128)S(1)}, f32[8,128]{1,0:T(8,128)S(1)}, u32[]{:S(2)}, u32[]{:S(2)}) collective-permute-start(f32[8,128]{1,0:T(8,128)S(1)} %get-tuple-element.103), channel_id=1, source_target_pairs={{0,1},{1,0},{2,3},{3,2},{4,5},{5,4},{6,7},{7,6},{8,9},{9,8},{10,11... | collective-permute-start | bytes 12296 | tf_op jit(solution)/shard_map/ppermute | solution.py:786
  41.2 2.1 %collective-permute-done.13.rest_0_ = f32[8,128]{1,0:T(8,128)S(1)} collective-permute-done((f32[8,128]{1,0:T(8,128)S(1)}, f32[8,128]{1,0:T(8,128)S(1)}, u32[]{:S(2)}, u32[]{:S(2)}) %collective-permute-start.13) | collective-permute-done | bytes 4128 | tf_op jit(solution)/shard_map/ppermute | solution.py:786
  43.3 0.0 collective-permute-done.9.xa.refs_11_
  43.3 0.0 collective-permute-done.10.xb.refs_12_
  43.3 0.0 collective-permute-done.11.ya.refs_13_
  43.3 1.3 %shard_map.192 = (f32[32,32,128]{2,1,0:T(8,128)S(1)}, f32[32,128]{1,0:T(8,128)S(1)}, f32[1024,128]{1,0:T(8,128)S(1)}) custom-call(f32[32,32,128]{2,1,0:T(8,128)S(1)} %get-tuple-element.91.direction.refs_2_, f32[32,32,128]{2,1,0:T(8,128)S(1)} %get-tuple-element.92.diag, f32[32,32,128]{2,1,0:T(8,128)S(1)} %get-tuple-element.93.full, ...), custom_call_target="tpu_custom_call" | custom-call | tf_op jit(solution)/shard_map/pallas_call | solution.py:108
  44.6 10.5 %all_to_all.11 = f32[32,1,128]{2,1,0:T(1,128)S(1)} all-to-all(f32[32,1,128]{2,1,0:T(1,128)S(1)} %bitcast.6), channel_id=1, replica_groups=mesh['gx'=4,'gy'=4,'gz'=2] {'gx','gy','gz'}, dimensions={0} | all-to-all | bytes 32768 | tf_op jit(solution)/shard_map/all_to_all | solution.py:861
  55.1 3.4 %shard_map.194 = (f32[32,32,128]{2,1,0:T(8,128)S(1)}, f32[32,32,128]{2,1,0:T(8,128)S(1)}, f32[33,32,128]{2,1,0:T(8,128)S(1)}, f32[32,32,128]{2,1,0:T(8,128)S(1)}...) custom-call(f32[32,128]{1,0:T(8,128)S(1)} %bitcast.4, ...), custom_call_target="tpu_custom_call" | custom-call | tf_op jit(solution)/shard_map/pallas_call | solution.py:108
  58.5 0.5 collective-permute-start.14
  59.0 1.5 %collective-permute-start.15 = (f32[32,128]{1,0:T(8,128)S(1)}, f32[32,128]{1,0:T(8,128)S(1)}, u32[]{:S(2)}, u32[]{:S(2)}) collective-permute-start(f32[32,128]{1,0:T(8,128)S(1)} %get-tuple-element.123), channel_id=1, source_target_pairs={{8,16},{16,8},{24,0},{0,24},{9,17},{17,9},{25,1},{1,25},{10,18},{1... | collective-permute-start | bytes 49160 | tf_op jit(solution)/shard_map/ppermute | solution.py:782
  60.5 0.7 collective-permute-start.17
  61.2 0.5 collective-permute-start.18
  61.8 1.3 %shard_map.193 = (f32[32,32,128]{2,1,0:T(8,128)}, f32[32,32,128]{2,1,0:T(8,128)}, f32[8,128]{1,0:T(8,128)S(1)}) custom-call(f32[32,128]{1,0:T(8,128)S(1)} %bitcast.5, f32[32,32,128]{2,1,0:T(8,128)S(1)} %get-tuple-element.69.press.refs_1_, f32[32,32,128]{2,1,0:T(8,128)S(1)} %get-tuple-element.91.direction.refs_2_, f32[32,32,128]{2,1,0:T(8,128)S(1)} %get-tuple-element.93.full, ...), custom_call_target="tpu_custom_call" | custom-call | tf_op jit(solution)/shard_map/pallas_call | solution.py:108
  63.1 1.8 %collective-permute-done.18.refs_16_ = f32[8,128]{1,0:T(8,128)S(1)} collective-permute-done((f32[8,128]{1,0:T(8,128)S(1)}, f32[8,128]{1,0:T(8,128)S(1)}, u32[]{:S(2)}, u32[]{:S(2)}) %collective-permute-start.18) | collective-permute-done | bytes 4128 | tf_op jit(solution)/shard_map/ppermute | solution.py:786
  64.8 0.0 collective-permute-done.15.refs_13_
  64.8 0.0 collective-permute-done.16.refs_14_
  64.8 0.0 collective-permute-done.17.refs_15_
  64.8 2.1 %shard_map.195 = (f32[32,32,128]{2,1,0:T(8,128)S(1)}, f32[32,32,128]{2,1,0:T(8,128)S(1)}, f32[32,128]{1,0:T(8,128)S(1)}, f32[32,128]{1,0:T(8,128)S(1)}, f32[32,1...) custom-call(f32[32,32,128]{2,1,0:T(8,128)S(1)} %get-tuple-element.108.refs_16_.refs_0_, ...), custom_call_target="tpu_custom_call" | custom-call | tf_op jit(solution)/shard_map/pallas_call | solution.py:108
  66.9 0.0 collective-permute-start.19
  67.0 2.9 %collective-permute-start.20 = (f32[32,128]{1,0:T(8,128)S(1)}, f32[32,128]{1,0:T(8,128)S(1)}, u32[]{:S(2)}, u32[]{:S(2)}) collective-permute-start(f32[32,128]{1,0:T(8,128)S(1)} %get-tuple-element.131), channel_id=1, source_target_pairs={{8,16},{16,8},{24,0},{0,24},{9,17},{17,9},{25,1},{1,25},{10,18},{1... | collective-permute-start | bytes 49160 | tf_op jit(solution)/shard_map/ppermute | solution.py:782
  69.9 1.6 %collective-permute-start.22 = (f32[32,128]{1,0:T(8,128)S(1)}, f32[32,128]{1,0:T(8,128)S(1)}, u32[]{:S(2)}, u32[]{:S(2)}) collective-permute-start(f32[32,128]{1,0:T(8,128)S(1)} %get-tuple-element.133), channel_id=1, source_target_pairs={{2,4},{4,2},{6,0},{0,6},{3,5},{5,3},{7,1},{1,7},{10,12},{12,10},{1... | collective-permute-start | bytes 49160 | tf_op jit(solution)/shard_map/ppermute | solution.py:782
  71.5 0.5 collective-permute-start.23
  72.0 3.1 %collective-permute-done.23.refs_16_ = f32[8,128]{1,0:T(8,128)S(1)} collective-permute-done((f32[8,128]{1,0:T(8,128)S(1)}, f32[8,128]{1,0:T(8,128)S(1)}, u32[]{:S(2)}, u32[]{:S(2)}) %collective-permute-start.23) | collective-permute-done | bytes 4128 | tf_op jit(solution)/shard_map/ppermute | solution.py:786
  75.1 0.0 collective-permute-done.19.refs_12_
  75.1 0.0 collective-permute-done.20.refs_13_
  75.1 2.1 %shard_map.196 = f32[32,32,128]{2,1,0:T(8,128)} custom-call(f32[32,32,128]{2,1,0:T(8,128)S(1)} %get-tuple-element.108.refs_16_.refs_0_, f32[32,32,128]{2,1,0:T(8,128)S(1)} %get-tuple-element.128.refs_1_, f32[32,32,128]{2,1,0:T(8,128)S(1)} %get-tuple-element.129.refs_2_, f32[32,32,128]{2,1,0:T(8,128)S(1)} %get-tuple-element.111.refs_18_.refs_3_, ...), custom_call_target="tpu_custom_call" | custom-call | tf_op jit(solution)/shard_map/pallas_call | solution.py:108
  (22 shorter events, 0.0 us)
Async XLA Ops:
  0.6 9.3 %copy-start.1 = (s32[32,32,128]{2,1,0:T(8,128)S(1)}, s32[32,32,128]{2,1,0:T(8,128)}, u32[]{:S(2)}) copy-start(s32[32,32,128]{2,1,0:T(8,128)} %well.3) | copy-start | bytes 1572868
  0.6 9.3 %copy-start.3 = (f32[32,32,128]{2,1,0:T(8,128)S(1)}, f32[32,32,128]{2,1,0:T(8,128)}, u32[]{:S(2)}) copy-start(f32[32,32,128]{2,1,0:T(8,128)} %compress.1) | copy-start | bytes 1572868
  0.7 9.3 %copy-start.2 = (f32[32,32,128]{2,1,0:T(8,128)S(1)}, f32[32,32,128]{2,1,0:T(8,128)}, u32[]{:S(2)}) copy-start(f32[32,32,128]{2,1,0:T(8,128)} %source.1) | copy-start | bytes 1572868
  2.7 9.7 %collective-permute-start = (f32[3,32,128]{2,1,0:T(8,128)S(1)}, f32[3,32,128]{2,1,0:T(8,128)S(1)}, u32[]{:S(2)}, u32[]{:S(2)}) collective-permute-start(f32[3,32,128]{2,1,0:T(8,128)S(1)} %get-tuple-element.73), channel_id=1, source_target_pairs={{0,8},{8,0},{16,24},{24,16},{1,9},{9,1},{17,25},{25,17},{2,10},{10... | collective-permute-start | bytes 147464 | tf_op jit(solution)/shard_map/ppermute | solution.py:781
  5.8 6.6 %collective-permute-start.1 = (f32[3,32,128]{2,1,0:T(8,128)S(1)}, f32[3,32,128]{2,1,0:T(8,128)S(1)}, u32[]{:S(2)}, u32[]{:S(2)}) collective-permute-start(f32[3,32,128]{2,1,0:T(8,128)S(1)} %get-tuple-element.74), channel_id=1, source_target_pairs={{8,16},{16,8},{24,0},{0,24},{9,17},{17,9},{25,1},{1,25},{10,18},{1... | collective-permute-start | bytes 147464 | tf_op jit(solution)/shard_map/ppermute | solution.py:782
  8.3 4.2 %collective-permute-start.2 = (f32[3,32,128]{2,1,0:T(8,128)S(1)}, f32[3,32,128]{2,1,0:T(8,128)S(1)}, u32[]{:S(2)}, u32[]{:S(2)}) collective-permute-start(f32[3,32,128]{2,1,0:T(8,128)S(1)} %get-tuple-element.75), channel_id=1, source_target_pairs={{0,2},{2,0},{4,6},{6,4},{1,3},{3,1},{5,7},{7,5},{8,10},{10,8},{12,... | collective-permute-start | bytes 147464 | tf_op jit(solution)/shard_map/ppermute | solution.py:781
  8.3 4.2 %collective-permute-start.3 = (f32[3,32,128]{2,1,0:T(8,128)S(1)}, f32[3,32,128]{2,1,0:T(8,128)S(1)}, u32[]{:S(2)}, u32[]{:S(2)}) collective-permute-start(f32[3,32,128]{2,1,0:T(8,128)S(1)} %get-tuple-element.76), channel_id=1, source_target_pairs={{2,4},{4,2},{6,0},{0,6},{3,5},{5,3},{7,1},{1,7},{10,12},{12,10},{1... | collective-permute-start | bytes 147464 | tf_op jit(solution)/shard_map/ppermute | solution.py:782
  12.5 5.8 %copy-start.5 = (bf16[384,144]{1,0:T(8,128)(2,1)S(1)}, bf16[384,144]{1,0:T(8,128)(2,1)}, u32[]{:S(2)}) copy-start(bf16[384,144]{1,0:T(8,128)(2,1)} %constant.20.clone.basis) | copy-start | bytes 331780
  12.5 5.8 %copy-start.7 = (f32[48,144]{1,0:T(8,128)S(1)}, f32[48,144]{1,0:T(8,128)}, u32[]{:S(2)}) copy-start(f32[48,144]{1,0:T(8,128)} %constant.25.rim_top) | copy-start | bytes 82948
  12.5 5.8 %copy-start.8 = (f32[48,144]{1,0:T(8,128)S(1)}, f32[48,144]{1,0:T(8,128)}, u32[]{:S(2)}) copy-start(f32[48,144]{1,0:T(8,128)} %constant.24.rim_low) | copy-start | bytes 82948
  13.9 6.4 %copy-start.4 = (f32[32,32,128]{2,1,0:T(8,128)S(1)}, f32[32,32,128]{2,1,0:T(8,128)}, u32[]{:S(2)}) copy-start(f32[32,32,128]{2,1,0:T(8,128)} %poro.1) | copy-start | bytes 1572868
  13.9 4.3 %collective-permute-start.4 = (f32[16,1024]{1,0:T(8,128)S(1)}, f32[16,1024]{1,0:T(8,128)S(1)}, u32[]{:S(2)}, u32[]{:S(2)}) collective-permute-start(f32[16,1024]{1,0:T(8,128)S(1)} %get-tuple-element.81.rest_0_), channel_id=1, source_target_pairs={{0,1},{1,0},{2,3},{3,2},{4,5},{5,4},{6,7},{7,6},{8,9},{9,8},{10,11... | collective-permute-start | bytes 196616 | tf_op jit(solution)/shard_map/ppermute | solution.py:786
  18.3 6.5 %copy-start = (f32[24,48,144]{2,1,0:T(8,128)S(1)}, f32[24,48,144]{2,1,0:T(8,128)}, u32[]{:S(2)}) copy-start(f32[24,48,144]{2,1,0:T(8,128)} %constant.16.clone.factors) | copy-start | bytes 1990660
  18.3 6.5 %copy-start.10 = (bf16[48,144]{1,0:T(8,128)(2,1)S(1)}, bf16[48,144]{1,0:T(8,128)(2,1)}, u32[]{:S(2)}) copy-start(bf16[48,144]{1,0:T(8,128)(2,1)} %constant.21.clone.basis) | copy-start | bytes 41476
  19.1 2.9 %collective-permute-start.5 = (f32[36,8,128]{2,1,0:T(8,128)S(1)}, f32[36,8,128]{2,1,0:T(8,128)S(1)}, u32[]{:S(2)}, u32[]{:S(2)}) collective-permute-start(f32[36,8,128]{2,1,0:T(8,128)S(1)} %get-tuple-element.83), channel_id=1, source_target_pairs={{0,2},{2,0},{4,6},{6,4},{1,3},{3,1},{5,7},{7,5},{8,10},{10,8},{12,... | collective-permute-start | bytes 442376 | tf_op jit(solution)/shard_map/ppermute | solution.py:781
  19.1 5.6 %collective-permute-start.6 = (f32[36,8,128]{2,1,0:T(8,128)S(1)}, f32[36,8,128]{2,1,0:T(8,128)S(1)}, u32[]{:S(2)}, u32[]{:S(2)}) collective-permute-start(f32[36,8,128]{2,1,0:T(8,128)S(1)} %get-tuple-element.84), channel_id=1, source_target_pairs={{2,4},{4,2},{6,0},{0,6},{3,5},{5,3},{7,1},{1,7},{10,12},{12,10},{1... | collective-permute-start | bytes 442376 | tf_op jit(solution)/shard_map/ppermute | solution.py:782
  22.0 11.4 %copy-start.6 = (bf16[2,144,128]{2,1,0:T(8,128)(2,1)S(1)}, bf16[2,144,128]{2,1,0:T(8,128)(2,1)}, u32[]{:S(2)}) copy-start(bf16[2,144,128]{2,1,0:T(8,128)(2,1)} %constant.23.clone.basis_z) | copy-start | bytes 221188
  22.0 11.4 %copy-start.9 = (f32[48,144]{1,0:T(8,128)S(1)}, f32[48,144]{1,0:T(8,128)}, u32[]{:S(2)}) copy-start(f32[48,144]{1,0:T(8,128)} %constant.17.clone.middle) | copy-start | bytes 82948
  22.0 11.4 %copy-start.11 = (bf16[32,144]{1,0:T(8,128)(2,1)S(1)}, bf16[32,144]{1,0:T(8,128)(2,1)}, u32[]{:S(2)}) copy-start(bf16[32,144]{1,0:T(8,128)(2,1)} %constant.22.clone.basis_y) | copy-start | bytes 27652
  26.9 3.9 %collective-permute-start.7 = (f32[56,128]{1,0:T(8,128)S(1)}, f32[56,128]{1,0:T(8,128)S(1)}, u32[]{:S(2)}, u32[]{:S(2)}) collective-permute-start(f32[56,128]{1,0:T(8,128)S(1)} %get-tuple-element.88), channel_id=1, source_target_pairs={{0,8},{8,0},{16,24},{24,16},{1,9},{9,1},{17,25},{25,17},{2,10},{10... | collective-permute-start | bytes 86024 | tf_op jit(solution)/shard_map/ppermute | solution.py:781
  27.7 5.7 %collective-permute-start.8 = (f32[56,128]{1,0:T(8,128)S(1)}, f32[56,128]{1,0:T(8,128)S(1)}, u32[]{:S(2)}, u32[]{:S(2)}) collective-permute-start(f32[56,128]{1,0:T(8,128)S(1)} %get-tuple-element.89), channel_id=1, source_target_pairs={{8,16},{16,8},{24,0},{0,24},{9,17},{17,9},{25,1},{1,25},{10,18},{1... | collective-permute-start | bytes 86024 | tf_op jit(solution)/shard_map/ppermute | solution.py:782
  36.3 7.0 %collective-permute-start.9 = (f32[32,128]{1,0:T(8,128)S(1)}, f32[32,128]{1,0:T(8,128)S(1)}, u32[]{:S(2)}, u32[]{:S(2)}) collective-permute-start(f32[32,128]{1,0:T(8,128)S(1)} %get-tuple-element.99), channel_id=1, source_target_pairs={{0,8},{8,0},{16,24},{24,16},{1,9},{9,1},{17,25},{25,17},{2,10},{10... | collective-permute-start | bytes 49160 | tf_op jit(solution)/shard_map/ppermute | solution.py:781
  36.3 7.0 %collective-permute-start.10 = (f32[32,128]{1,0:T(8,128)S(1)}, f32[32,128]{1,0:T(8,128)S(1)}, u32[]{:S(2)}, u32[]{:S(2)}) collective-permute-start(f32[32,128]{1,0:T(8,128)S(1)} %get-tuple-element.100), channel_id=1, source_target_pairs={{8,16},{16,8},{24,0},{0,24},{9,17},{17,9},{25,1},{1,25},{10,18},{1... | collective-permute-start | bytes 49160 | tf_op jit(solution)/shard_map/ppermute | solution.py:782
  38.1 5.2 %collective-permute-start.11 = (f32[32,128]{1,0:T(8,128)S(1)}, f32[32,128]{1,0:T(8,128)S(1)}, u32[]{:S(2)}, u32[]{:S(2)}) collective-permute-start(f32[32,128]{1,0:T(8,128)S(1)} %get-tuple-element.101), channel_id=1, source_target_pairs={{0,2},{2,0},{4,6},{6,4},{1,3},{3,1},{5,7},{7,5},{8,10},{10,8},{12,... | collective-permute-start | bytes 49160 | tf_op jit(solution)/shard_map/ppermute | solution.py:781
  38.1 5.2 %collective-permute-start.12 = (f32[32,128]{1,0:T(8,128)S(1)}, f32[32,128]{1,0:T(8,128)S(1)}, u32[]{:S(2)}, u32[]{:S(2)}) collective-permute-start(f32[32,128]{1,0:T(8,128)S(1)} %get-tuple-element.102), channel_id=1, source_target_pairs={{2,4},{4,2},{6,0},{0,6},{3,5},{5,3},{7,1},{1,7},{10,12},{12,10},{1... | collective-permute-start | bytes 49160 | tf_op jit(solution)/shard_map/ppermute | solution.py:782
  39.7 3.6 %collective-permute-start.13 = (f32[8,128]{1,0:T(8,128)S(1)}, f32[8,128]{1,0:T(8,128)S(1)}, u32[]{:S(2)}, u32[]{:S(2)}) collective-permute-start(f32[8,128]{1,0:T(8,128)S(1)} %get-tuple-element.103), channel_id=1, source_target_pairs={{0,1},{1,0},{2,3},{3,2},{4,5},{5,4},{6,7},{7,6},{8,9},{9,8},{10,11... | collective-permute-start | bytes 12296 | tf_op jit(solution)/shard_map/ppermute | solution.py:786
  58.5 6.3 %collective-permute-start.14 = (f32[32,128]{1,0:T(8,128)S(1)}, f32[32,128]{1,0:T(8,128)S(1)}, u32[]{:S(2)}, u32[]{:S(2)}) collective-permute-start(f32[32,128]{1,0:T(8,128)S(1)} %get-tuple-element.122), channel_id=1, source_target_pairs={{0,8},{8,0},{16,24},{24,16},{1,9},{9,1},{17,25},{25,17},{2,10},{10... | collective-permute-start | bytes 49160 | tf_op jit(solution)/shard_map/ppermute | solution.py:781
  59.0 5.8 %collective-permute-start.15 = (f32[32,128]{1,0:T(8,128)S(1)}, f32[32,128]{1,0:T(8,128)S(1)}, u32[]{:S(2)}, u32[]{:S(2)}) collective-permute-start(f32[32,128]{1,0:T(8,128)S(1)} %get-tuple-element.123), channel_id=1, source_target_pairs={{8,16},{16,8},{24,0},{0,24},{9,17},{17,9},{25,1},{1,25},{10,18},{1... | collective-permute-start | bytes 49160 | tf_op jit(solution)/shard_map/ppermute | solution.py:782
  60.5 4.4 %collective-permute-start.16 = (f32[32,128]{1,0:T(8,128)S(1)}, f32[32,128]{1,0:T(8,128)S(1)}, u32[]{:S(2)}, u32[]{:S(2)}) collective-permute-start(f32[32,128]{1,0:T(8,128)S(1)} %get-tuple-element.124), channel_id=1, source_target_pairs={{0,2},{2,0},{4,6},{6,4},{1,3},{3,1},{5,7},{7,5},{8,10},{10,8},{12,... | collective-permute-start | bytes 49160 | tf_op jit(solution)/shard_map/ppermute | solution.py:781
  60.5 4.4 %collective-permute-start.17 = (f32[32,128]{1,0:T(8,128)S(1)}, f32[32,128]{1,0:T(8,128)S(1)}, u32[]{:S(2)}, u32[]{:S(2)}) collective-permute-start(f32[32,128]{1,0:T(8,128)S(1)} %get-tuple-element.125), channel_id=1, source_target_pairs={{2,4},{4,2},{6,0},{0,6},{3,5},{5,3},{7,1},{1,7},{10,12},{12,10},{1... | collective-permute-start | bytes 49160 | tf_op jit(solution)/shard_map/ppermute | solution.py:782
  61.2 3.6 %collective-permute-start.18 = (f32[8,128]{1,0:T(8,128)S(1)}, f32[8,128]{1,0:T(8,128)S(1)}, u32[]{:S(2)}, u32[]{:S(2)}) collective-permute-start(f32[8,128]{1,0:T(8,128)S(1)} %get-tuple-element.126), channel_id=1, source_target_pairs={{0,1},{1,0},{2,3},{3,2},{4,5},{5,4},{6,7},{7,6},{8,9},{9,8},{10,11... | collective-permute-start | bytes 12296 | tf_op jit(solution)/shard_map/ppermute | solution.py:786
  66.9 8.2 %collective-permute-start.19 = (f32[32,128]{1,0:T(8,128)S(1)}, f32[32,128]{1,0:T(8,128)S(1)}, u32[]{:S(2)}, u32[]{:S(2)}) collective-permute-start(f32[32,128]{1,0:T(8,128)S(1)} %get-tuple-element.130), channel_id=1, source_target_pairs={{0,8},{8,0},{16,24},{24,16},{1,9},{9,1},{17,25},{25,17},{2,10},{10... | collective-permute-start | bytes 49160 | tf_op jit(solution)/shard_map/ppermute | solution.py:781
  67.0 8.1 %collective-permute-start.20 = (f32[32,128]{1,0:T(8,128)S(1)}, f32[32,128]{1,0:T(8,128)S(1)}, u32[]{:S(2)}, u32[]{:S(2)}) collective-permute-start(f32[32,128]{1,0:T(8,128)S(1)} %get-tuple-element.131), channel_id=1, source_target_pairs={{8,16},{16,8},{24,0},{0,24},{9,17},{17,9},{25,1},{1,25},{10,18},{1... | collective-permute-start | bytes 49160 | tf_op jit(solution)/shard_map/ppermute | solution.py:782
  69.9 5.3 %collective-permute-start.21 = (f32[32,128]{1,0:T(8,128)S(1)}, f32[32,128]{1,0:T(8,128)S(1)}, u32[]{:S(2)}, u32[]{:S(2)}) collective-permute-start(f32[32,128]{1,0:T(8,128)S(1)} %get-tuple-element.132), channel_id=1, source_target_pairs={{0,2},{2,0},{4,6},{6,4},{1,3},{3,1},{5,7},{7,5},{8,10},{10,8},{12,... | collective-permute-start | bytes 49160 | tf_op jit(solution)/shard_map/ppermute | solution.py:781
  69.9 5.3 %collective-permute-start.22 = (f32[32,128]{1,0:T(8,128)S(1)}, f32[32,128]{1,0:T(8,128)S(1)}, u32[]{:S(2)}, u32[]{:S(2)}) collective-permute-start(f32[32,128]{1,0:T(8,128)S(1)} %get-tuple-element.133), channel_id=1, source_target_pairs={{2,4},{4,2},{6,0},{0,6},{3,5},{5,3},{7,1},{1,7},{10,12},{12,10},{1... | collective-permute-start | bytes 49160 | tf_op jit(solution)/shard_map/ppermute | solution.py:782
  71.5 3.6 %collective-permute-start.23 = (f32[8,128]{1,0:T(8,128)S(1)}, f32[8,128]{1,0:T(8,128)S(1)}, u32[]{:S(2)}, u32[]{:S(2)}) collective-permute-start(f32[8,128]{1,0:T(8,128)S(1)} %get-tuple-element.134), channel_id=1, source_target_pairs={{0,1},{1,0},{2,3},{3,2},{4,5},{5,4},{6,7},{7,6},{8,9},{9,8},{10,11... | collective-permute-start | bytes 12296 | tf_op jit(solution)/shard_map/ppermute | solution.py:786

commit v2 on v1

--- a/solution.py
+++ b/solution.py
@@ -9,6 +9,7 @@
 from jax.experimental.pallas import tpu as pltpu
 from jax.sharding import PartitionSpec as P
 
+
 INTERSECTION = 8
 NEWTON = 3
 
@@ -18,7 +19,6 @@
 
 AXES = ("gx", "gy", "gz")
 F32 = jnp.float32
-HIGH = lax.Precision.HIGHEST
 MSG_ROWS = 16
 CHUNKS = 4
 
@@ -31,14 +31,16 @@
     return table, eigen
 
 
-def sweep_factors(count, eigen_y, eigen_z):
+def sweep_factors(count, skip, eigen_y, eigen_z):
     shift = 2.0 + eigen_y[:, None] + eigen_z[None, :]
     factors = []
     last = np.zeros_like(shift)
     for _ in range(count):
         last = 1.0 / (shift - last)
         factors.append(last)
-    return np.stack(factors), 1.0 / (1.0 - last * last)
+    factors = np.stack(factors)
+    reach = np.cumprod(factors[skip:], axis=0)
+    return factors, reach, 1.0 / (1.0 - last * last)
 
 
 def pairs(count, periodic, parity):
@@ -57,12 +59,6 @@
 
 def harmonic(one, two):
     return 2.0 * one * two / (one + two)
-
-
-def dot(one, two, dims=((1,), (0,))):
-    return lax.dot_general(
-        one, two, (dims, ((), ())), precision=HIGH, preferred_element_type=F32
-    )
 
 
 def rows_of(shape):
@@ -253,7 +249,7 @@
         return p, m, r
 
     zero = jnp.zeros(shape, F32)
-    res[plan.nx - 1] = lax.fori_loop(0, plan.nx, layer, (zero, zero, zero), unroll=2)[2]
+    res[plan.nx - 1] = lax.fori_loop(0, plan.nx, layer, (zero, zero, zero), unroll=4)[2]
 
 
 def rim_kernel(plan, res_in, press, mob, frac, xa, xb, ya, yb, res, *rest):
@@ -284,7 +280,7 @@
             out[:, cut] = jnp.transpose(comp[cut, :])[:MSG_ROWS, :]
 
 
-def z_flux(plan, sent, got):
+def z_flux(sent, got):
     wide = INTERSECTION
     out = []
     for own, other in zip(sent, got):
@@ -300,7 +296,7 @@
     nx, ny, nz = plan.nx, plan.ny, plan.nz
     wide = INTERSECTION
     mixes, rims = [], []
-    for q, other, (_, _, _, flux) in zip(plan.z_msgs, got, z_flux(plan, sent, got)):
+    for q, other, (_, _, _, flux) in zip(plan.z_msgs, got, z_flux(sent, got)):
         up = plan.high("gz", q)[1]
         row = rows_of(other.shape)
         near = jnp.where(up, 0, wide - 1)
@@ -331,33 +327,59 @@
             )
 
 
-def faces_xy_kernel(plan, mob, tx_in, ty_in, xa, xb, ya, yb, tx, ty_low, ty_top, hx, hy, ty_rim):
+def faces_xy_kernel(
+    plan, mob, press, sat, coef, poro, well, tx_in, ty_in, xa, xb, ya, yb,
+    tx, ty_low, ty_top, gx, gy_low, gy_top, hx, hy, rate, inject, square, pull, push, ty_rim,
+):
     nx, ny, nz = plan.nx, plan.ny, plan.nz
     for k, high in ((0, False), (1, True)):
         for f, field in ((0, 0), (1, 2)):
             hx[k, f] = side(plan, "gx", xa[field], xb[field], high)
             hy[k, f] = side(plan, "gy", ya[field], yb[field], high)
-    tx[nx] = harmonic(mob[nx - 1], side(plan, "gx", xa[1], xb[1], True))
     ty_rim[0] = harmonic(mob[:, 0, :], side(plan, "gy", ya[1], yb[1], False))
     ty_rim[1] = harmonic(mob[:, ny - 1, :], side(plan, "gy", ya[1], yb[1], True))
     row = rows_of((ny, nz))
-
-    def layer(i, carry):
-        tx[i] = tx_in[i]
-        ty = ty_in[i]
-        ty_low[i] = jnp.where(row == 0, ty_rim[0, pl.ds(i, 1), :], ty)
-        ty_top[i] = jnp.where(row == ny - 1, ty_rim[1, pl.ds(i, 1), :], back(ty, 0))
-        return carry
-
-    lax.fori_loop(0, nx, layer, 0, unroll=4)
-    tx[0] = harmonic(mob[0], side(plan, "gx", xa[1], xb[1], False))
-
-
-def faces_z_kernel(plan, n_msg, res, tz_in, poro, well, *rest):
+    t_first = harmonic(mob[0], side(plan, "gx", xa[1], xb[1], False))
+
+    def layer(i, p_last):
+        p = press[i]
+        t = jnp.where(i == 0, t_first, tx_in[i])
+        tx[i] = t
+        gx[i] = t * (p_last - p)
+        t = ty_in[i]
+        low = jnp.where(row == 0, ty_rim[0, pl.ds(i, 1), :], t)
+        top = jnp.where(row == ny - 1, ty_rim[1, pl.ds(i, 1), :], back(t, 0))
+        ty_low[i] = low
+        ty_top[i] = top
+        y_last = jnp.where(row == 0, hy[0, 0, pl.ds(i, 1), :], ahead(p, 0))
+        y_next = jnp.where(row == ny - 1, hy[1, 0, pl.ds(i, 1), :], back(p, 0))
+        gy_low[i] = low * (y_last - p)
+        gy_top[i] = top * (p - y_next)
+        speed = poro[i] / TIME_STEP
+        s, c = sat[i], coef[i]
+        rest = 1.0 - s
+        part = c * rest
+        den = s * s + part * rest
+        den = den * den
+        rate[i] = speed
+        inject[i] = INJECT_RATE * well[i].astype(F32)
+        square[i] = den
+        pull[i] = speed * den
+        push[i] = jnp.abs(2.0 * part * s)
+        return p
+
+    p = lax.fori_loop(0, nx, layer, hx[0, 0], unroll=4)
+    t = harmonic(mob[nx - 1], side(plan, "gx", xa[1], xb[1], True))
+    tx[nx] = t
+    gx[nx] = t * (p - hx[1, 0])
+
+
+def faces_z_kernel(plan, n_msg, res, press, tz_in, *rest):
     sent, got = rest[:n_msg], rest[n_msg : 2 * n_msg]
-    full, tz_low, tz_top, hz, rate, inject = rest[2 * n_msg :]
+    full, tz_low, tz_top, gz_low, gz_top = rest[2 * n_msg : 2 * n_msg + 5]
+    fz, hz = rest[2 * n_msg + 5 : -1], rest[-1]
     nx, ny, nz = plan.nx, plan.ny, plan.nz
-    parts = z_flux(plan, sent, got)
+    parts = z_flux(sent, got)
     split = [z_sides(plan, [part[k] for part in parts]) for k in range(4)]
     rows = stack_rows([v for pair in split for v in pair])
     for k in range(nx * ny // 128):
@@ -366,16 +388,22 @@
     lane = lanes_of((ny, nz))
 
     def layer(i, carry):
-        tz = tz_in[i]
-        col = hz[pl.ds(i * ny, ny), :8]
-        tz_low[i] = jnp.where(lane == 0, col[:, 4:5], tz)
-        tz_top[i] = jnp.where(lane == nz - 1, col[:, 5:6], back(tz, 1))
-        flux = jnp.where(lane == 0, col[:, 6:7], 0.0) + jnp.where(
-            lane == nz - 1, col[:, 7:8], 0.0
-        )
+        t, p = tz_in[i], press[i]
+        cells = pl.ds(i * ny, ny)
+        col = hz[cells, :8]
+        in_low, in_top = col[:, 6:7], col[:, 7:8]
+        tz_low[i] = jnp.where(lane == 0, col[:, 4:5], t)
+        tz_top[i] = jnp.where(lane == nz - 1, col[:, 5:6], back(t, 1))
+        g = t * (ahead(p, 1) - p)
+        gz_low[i] = jnp.where(lane == 0, in_low, g)
+        gz_top[i] = jnp.where(lane == nz - 1, -in_top, back(g, 1))
+        flux = jnp.where(lane == 0, in_low, 0.0) + jnp.where(lane == nz - 1, in_top, 0.0)
         full[i] = res[i] + flux
-        rate[i] = poro[i] / TIME_STEP
-        inject[i] = INJECT_RATE * well[i].astype(F32)
+        if len(fz) == 1:
+            fz[0][cells, :] = jnp.broadcast_to(col[:, 2:3] + col[:, 3:4], (ny, nz))
+        else:
+            for k, out in enumerate(fz):
+                out[cells, :] = jnp.broadcast_to(col[:, 2 + k : 3 + k], (ny, nz))
         return carry
 
     lax.fori_loop(0, nx, layer, 0, unroll=4)
@@ -413,46 +441,74 @@
     return jnp.concatenate([value[:rows], ends], axis=1)
 
 
-def y_kernel(plan, spec, ya, yb, basis, factors, order, modes, xa, xb):
+def y_modes(plan, spec, ya, yb, basis, i):
+    low = wide_rows(plan, ya, yb, i, False)
+    top = wide_rows(plan, ya, yb, i, True)
+    return mxu(basis[...], thrice(jnp.concatenate([low, spec[i], top], axis=0)))
+
+
+def y_edge_kernel(plan, spec, ya, yb, basis, factors, order, edge, xa, xb):
     nx = plan.nx
     wide = INTERSECTION
 
     def layer(i, carry):
-        low = wide_rows(plan, ya, yb, i, False)
-        top = wide_rows(plan, ya, yb, i, True)
-        modes[i] = mxu(basis[...], thrice(jnp.concatenate([low, spec[i], top], axis=0)))
+        edge[i] = y_modes(plan, spec, ya, yb, basis, jnp.where(i < wide, i, nx - 2 * wide + i))
         return carry
 
-    lax.fori_loop(0, nx, layer, 0, unroll=4)
-    low = jnp.zeros(modes.shape[1:], F32)
+    lax.fori_loop(0, 2 * wide, layer, 0, unroll=4)
+    low = jnp.zeros(edge.shape[1:], F32)
     top = low
     for k in range(wide):
-        low = (modes[wide - 1 - k] + low) * factors[k]
-        top = (modes[nx - wide + k] + top) * factors[k]
+        low = (edge[wide - 1 - k] + low) * factors[k]
+        top = (edge[wide + k] + top) * factors[k]
     for which, out in ((0, xa), (1, xb)):
         out[...] = fold(jnp.where(plan.high("gx", which)[0], top, low), plan.nz)
 
 
+def y_mid_kernel(plan, spec, ya, yb, basis, factors, edge, zed):
+    nx = plan.nx
+    wide = INTERSECTION
+
+    def layer(i, carry):
+        zed[i] = y_modes(plan, spec, ya, yb, basis, i)
+        return carry
+
+    lax.fori_loop(wide, nx - wide, layer, 0, unroll=4)
+
+    def outer(k, carry):
+        low, top = carry
+        c = factors[wide + k]
+        low = (edge[k] + low) * c
+        top = (edge[2 * wide - 1 - k] + top) * c
+        zed[k] = low
+        zed[nx - 1 - k] = top
+        return low, top
+
+    def inner(k, carry):
+        low, top = carry
+        c = factors[wide + k]
+        low = (zed[k] + low) * c
+        top = (zed[nx - 1 - k] + top) * c
+        zed[k] = low
+        zed[nx - 1 - k] = top
+        return low, top
+
+    zero = jnp.zeros(edge.shape[1:], F32)
+    carry = lax.fori_loop(0, wide, outer, (zero, zero), unroll=2)
+    lax.fori_loop(wide, nx // 2, inner, carry, unroll=2)
+
+
 def solve_kernel(
-    plan, modes, xa, xb, factors, middle, basis_y, basis_z, total, direction, *rest
+    plan, zed, xa, xb, factors, reach, middle, basis_y, basis_z, total, direction, *rest
 ):
     (dxa, dxb, dya, dyb), z_outs, (work, tile) = rest[:4], rest[4:-2], rest[-2:]
     nx, ny, nz = plan.nx, plan.ny, plan.nz
     wide = INTERSECTION
     half = nx // 2
-    low = unfold(side(plan, "gx", xa[...], xb[...], False), 2 * wide)
-    top = unfold(side(plan, "gx", xa[...], xb[...], True), 2 * wide)
-
-    def inward(k, carry):
-        low, top = carry
-        c = factors[wide + k]
-        low = (modes[k] + low) * c
-        top = (modes[nx - 1 - k] + top) * c
-        modes[k] = low
-        modes[nx - 1 - k] = top
-        return low, top
-
-    low, top = lax.fori_loop(0, half, inward, (low, top), unroll=2)
+    low_in = unfold(side(plan, "gx", xa[...], xb[...], False), 2 * wide)
+    top_in = unfold(side(plan, "gx", xa[...], xb[...], True), 2 * wide)
+    low = zed[half - 1] + reach[half - 1] * low_in
+    top = zed[half] + reach[half - 1] * top_in
     c, mid = factors[wide + half - 1], middle[...]
     low, top = (low + c * top) * mid, (top + c * low) * mid
 
@@ -466,8 +522,9 @@
         low, top = carry
         i = half - 2 - k
         c = factors[wide + i]
-        low = modes[i] + c * low
-        top = modes[nx - 1 - i] + c * top
+        far = reach[i]
+        low = (zed[i] + far * low_in) + c * low
+        top = (zed[nx - 1 - i] + far * top_in) + c * top
         put(i, low)
         put(nx - 1 - i, top)
         return low, top
@@ -501,8 +558,8 @@
 ):
     n_msg = len(plan.z_msgs)
     got = rest[:n_msg]
-    image, sums = rest[n_msg : n_msg + 2]
-    hz, hy = rest[n_msg + 2 : -1], rest[-1]
+    image, sums, gx, gy_low, gy_top, gz_low, gz_top, hy = rest[n_msg : n_msg + 8]
+    hz = rest[n_msg + 8 :]
     nx, ny, nz = plan.nx, plan.ny, plan.nz
     spread(plan, got, hz)
     hy[0] = side(plan, "gy", ya[...], yb[...], False)
@@ -513,17 +570,21 @@
         d_last, im_last, rd, da = carry
         d = direction[i]
         flux = tx[i] * (d_last - d)
+        gx[i] = flux
         cells = pl.ds(i * ny, ny)
         y_last = jnp.where(row == 0, hy[0, pl.ds(i, 1), :], ahead(d, 0))
         y_next = jnp.where(row == ny - 1, hy[1, pl.ds(i, 1), :], back(d, 0))
         z_last = jnp.where(lane == 0, hz[0][cells, :], ahead(d, 1))
         z_next = jnp.where(lane == nz - 1, hz[-1][cells, :], back(d, 1))
-        im = (
-            diag[i] * d
-            - flux
-            + (ty_low[i] * (d - y_last) + ty_top[i] * (d - y_next))
-            + (tz_low[i] * (d - z_last) + tz_top[i] * (d - z_next))
-        )
+        im = diag[i] * d - flux
+        for ref, g, sign in (
+            (gy_low, ty_low[i] * (y_last - d), -1),
+            (gy_top, ty_top[i] * (d - y_next), 1),
+            (gz_low, tz_low[i] * (z_last - d), -1),
+            (gz_top, tz_top[i] * (d - z_next), 1),
+        ):
+            ref[i] = g
+            im = im + g if sign > 0 else im - g
         im_last = im_last + flux
         image[jnp.maximum(i - 1, 0)] = im_last
         rd = rd + full[i] * d
@@ -534,20 +595,23 @@
     low = side(plan, "gx", xa[...], xb[...], False)
     top = side(plan, "gx", xa[...], xb[...], True)
     d, im, rd, da = lax.fori_loop(0, nx, layer, (low, zero, zero, zero), unroll=4)
-    im = im + tx[nx] * (d - top)
+    flux = tx[nx] * (d - top)
+    gx[nx] = flux
+    im = im + flux
     image[nx - 1] = im
     da = da + d * im
     lane = lanes_of((n_dev, 128))
     sums[...] = jnp.where(lane < 64, jnp.sum(rd), jnp.sum(da))
 
 
-def sweep(plan, first, refs, x_low, x_top, hy, z_at, done):
+def upwind(g, low, high):
+    return g * jnp.where(g > 0.0, low, high)
+
+
+def sweep(plan, refs, x_low, x_top, hy, z_at, done):
     nx, ny, nz = plan.nx, plan.ny, plan.nz
     (start, now, frac, coef, rate, inject, gx, gy_low, gy_top, gz_low, gz_top, outflow) = refs
     row, lane = rows_of((ny, nz)), lanes_of((ny, nz))
-
-    def upwind(g, low, high):
-        return g * jnp.where(g > 0.0, low, high)
 
     def layer(i, carry):
         f, flow = carry
@@ -563,10 +627,8 @@
             (flow_next - flow)
             + (upwind(gy_top[i], f, y_next) - upwind(gy_low[i], y_last, f))
             + (upwind(gz_top[i], f, z_next) - upwind(gz_low[i], z_last, f))
-            - inject[i]
+            + (rate[i] * (s - start[i]) - inject[i])
         )
-        if not first:
-            bal = bal + rate[i] * (s - start[i])
         rest = 1.0 - s
         part = c * rest
         den = s * s + part * rest
@@ -639,67 +701,55 @@
 
 def step_kernel(plan, *refs):
     n_msg = len(plan.z_msgs)
-    (sums, press, direction, tx, ty_low, ty_top, tz_low, tz_top) = refs[:8]
-    (hx, hy, hz, dxa, dxb, dya, dyb) = refs[8:15]
-    dhz = refs[15 : 15 + n_msg]
-    (sat, frac, coef, rate, inject) = refs[15 + n_msg : 20 + n_msg]
+    sums, still, move = refs[0], refs[1:6], refs[6:11]
+    (sat, frac, coef, inject, square, pull, push, hx, hy) = refs[11:20]
+    fz = refs[20 : 20 + n_msg]
     outs = refs[20 + n_msg :]
     (s_new, f_new, gx, gy_low, gy_top, gz_low, gz_top, outflow) = outs[:8]
     packs = outs[8 : 12 + n_msg]
-    ph, fh, tile = outs[12 + n_msg :]
+    tile = outs[-1]
     nx, ny, nz = plan.nx, plan.ny, plan.nz
     step = step_of(sums)
-    x_low = hx[0, 0] + step * side(plan, "gx", dxa[...], dxb[...], False)
-    x_top = hx[1, 0] + step * side(plan, "gx", dxa[...], dxb[...], True)
-    ph[0] = hy[0, 0] + step * side(plan, "gy", dya[...], dyb[...], False)
-    ph[1] = hy[1, 0] + step * side(plan, "gy", dya[...], dyb[...], True)
-    fh[0] = hy[0, 1]
-    fh[1] = hy[1, 1]
     row, lane = rows_of((ny, nz)), lanes_of((ny, nz))
+    done = keep(plan, s_new, f_new, tile)
+
+    def flux(k, i):
+        return still[k][i] + step * move[k][i]
 
     def layer(i, carry):
-        p, g = carry
-        k = jnp.minimum(i + 1, nx - 1)
-        p_next = jnp.where(i == nx - 1, x_top, press[k] + step * direction[k])
-        g_next = tx[i + 1] * (p - p_next)
+        f, g, flow = carry
+        f_next = jnp.where(i == nx - 1, hx[1, 1], frac[jnp.minimum(i + 1, nx - 1)])
+        g_next = flux(0, i + 1)
         gx[i + 1] = g_next
+        flow_next = upwind(g_next, f, f_next)
+        out = jnp.maximum(g_next, 0.0) - jnp.minimum(g, 0.0)
+        bal = flow_next - flow - inject[i]
         cells = pl.ds(i * ny, ny)
-        y_last = jnp.where(row == 0, ph[0, pl.ds(i, 1), :], ahead(p, 0))
-        y_next = jnp.where(row == ny - 1, ph[1, pl.ds(i, 1), :], back(p, 0))
-        z_low = hz[cells, 0:1] + step * dhz[0][cells, :]
-        z_top = hz[cells, 1:2] + step * dhz[-1][cells, :]
-        z_last = jnp.where(lane == 0, z_low, ahead(p, 1))
-        z_next = jnp.where(lane == nz - 1, z_top, back(p, 1))
-        parts = (
-            (gy_low, ty_low[i] * (y_last - p), -1.0),
-            (gy_top, ty_top[i] * (p - y_next), 1.0),
-            (gz_low, tz_low[i] * (z_last - p), -1.0),
-            (gz_top, tz_top[i] * (p - z_next), 1.0),
-        )
-        total = jnp.maximum(g_next, 0.0) - jnp.minimum(g, 0.0)
-        for ref, value, sign in parts:
+        y_last = jnp.where(row == 0, hy[0, 1, pl.ds(i, 1), :], ahead(f, 0))
+        y_next = jnp.where(row == ny - 1, hy[1, 1, pl.ds(i, 1), :], back(f, 0))
+        z_last = jnp.where(lane == 0, fz[0][cells, :], ahead(f, 1))
+        z_next = jnp.where(lane == nz - 1, fz[-1][cells, :], back(f, 1))
+        for k, ref, other, low in (
+            (1, gy_low, y_last, True),
+            (2, gy_top, y_next, False),
+            (3, gz_low, z_last, True),
+            (4, gz_top, z_next, False),
+        ):
+            value = flux(k, i)
             ref[i] = value
-            if sign > 0:
-                total = total + jnp.maximum(value, 0.0)
+            if low:
+                out = out - jnp.minimum(value, 0.0)
+                bal = bal - upwind(value, other, f)
             else:
-                total = total - jnp.minimum(value, 0.0)
-        outflow[i] = total
-        return p_next, g_next
-
-    p0 = press[0] + step * direction[0]
-    g0 = tx[0] * (x_low - p0)
+                out = out + jnp.maximum(value, 0.0)
+                bal = bal + upwind(value, f, other)
+        outflow[i] = out
+        done(i, sat[i] - bal * square[i] / (pull[i] + out * push[i]), coef[i])
+        return f_next, g_next, flow_next
+
+    f0, g0 = frac[0], flux(0, 0)
     gx[0] = g0
-    lax.fori_loop(0, nx, layer, (p0, g0), unroll=4)
-
-    def z_at(i):
-        cells = pl.ds(i * ny, ny)
-        return hz[cells, 2:3], hz[cells, 3:4]
-
-    sweep(
-        plan, True,
-        (sat, sat, frac, coef, rate, inject, gx, gy_low, gy_top, gz_low, gz_top, outflow),
-        hx[0, 1], hx[1, 1], fh, z_at, keep(plan, s_new, f_new, tile),
-    )
+    lax.fori_loop(0, nx, layer, (f0, g0, upwind(g0, hx[0, 1], f0)), unroll=4)
     pack_all(plan, f_new, tile, packs)
 
 
@@ -730,7 +780,7 @@
         return hz[0][cells, :], hz[-1][cells, :]
 
     sweep(
-        plan, False, fields,
+        plan, fields,
         side(plan, "gx", xa[...], xb[...], False), side(plan, "gx", xa[...], xb[...], True),
         fh, z_at, done,
     )
@@ -752,9 +802,9 @@
     my, mz = ny + 2 * wide, nz + 2 * wide
     table_y, eigen_y = sine_basis(my)
     table_z, eigen_z = sine_basis(mz)
-    factors, middle = sweep_factors(wide + nx // 2, eigen_y, eigen_z)
+    factors, reach, middle = sweep_factors(wide + nx // 2, wide, eigen_y, eigen_z)
     const = lambda v: jnp.asarray(v, F32)
-    factors, middle = const(factors), const(middle)
+    factors, reach, middle = const(factors), const(reach), const(middle)
     rim = np.zeros((2, MSG_ROWS, mz))
     rim[0, :wide] = table_z[:wide]
     rim[0, wide] = table_z[wide]
@@ -776,14 +826,14 @@
 
     rims = [jnp.concatenate([right(v)], axis=0).astype(F32) for v in rim]
 
+    def send(value, axis, which):
+        return lax.ppermute(value, axis, plan.perm(axis, which))
+
     def swap(axis, a, b):
-        return (
-            lax.ppermute(a, axis, plan.perm(axis, 0)),
-            lax.ppermute(b, axis, plan.perm(axis, 1)),
-        )
+        return send(a, axis, 0), send(b, axis, 1)
 
     def swap_z(msgs):
-        return [lax.ppermute(v, "gz", plan.perm("gz", q)) for q, v in zip(plan.z_msgs, msgs)]
+        return [send(v, "gz", q) for q, v in zip(plan.z_msgs, msgs)]
 
     full_shape = (nx, ny, nz)
     x_face, y_face, z_face = (ny, nz), (nx, nz), (cells // 128, 128)
@@ -821,10 +871,11 @@
         aliases={0: 0},
     )
     got = swap_z(sent)
-    tx, ty_low, ty_top, hx, hy = call(
+    tx, ty_low, ty_top, gx, gy_low, gy_top, hx, hy, rate, inject, square, pull, push = call(
         functools.partial(faces_xy_kernel, plan),
-        [(nx + 1, ny, nz)] + [full_shape] * 2 + [(2, 2) + x_face, (2, 2) + y_face],
-        (mob, tx, ty, xa, xb, ya, yb),
+        [(nx + 1, ny, nz)] + [full_shape] * 2 + [(nx + 1, ny, nz)] + [full_shape] * 2
+        + [(2, 2) + x_face, (2, 2) + y_face] + [full_shape] * 5,
+        (mob, press, sat, coef, porosity, well_mask, tx, ty, xa, xb, ya, yb),
         scratch=[(2,) + y_face],
     )
     spec, sa, sb = call(
@@ -833,38 +884,44 @@
         (res, right(table_z[wide : wide + nz]), *rims, hx, *sent, *got),
     )
     sa, sb = swap("gy", sa, sb)
-    full, tz_low, tz_top, hz, rate, inject = call(
+    full, tz_low, tz_top, gz_low, gz_top, *fz = call(
         functools.partial(faces_z_kernel, plan, n_msg),
-        [full_shape] * 3 + [(cells, 128)] + [full_shape] * 2,
-        (res, tz, porosity, well_mask, *sent, *got),
-    )
-    modes, ma, mb = call(
-        functools.partial(y_kernel, plan),
-        [(nx, my, mz), (my + 8, nz), (my + 8, nz)],
-        (spec, sa, sb, left(table_y), factors, hz),
+        [full_shape] * 5 + spreads,
+        (res, press, tz, *sent, *got),
+        scratch=[(cells, 128)],
+    )
+    edge, ma, mb = call(
+        functools.partial(y_edge_kernel, plan),
+        [(2 * wide, my, mz), (my + 8, nz), (my + 8, nz)],
+        (spec, sa, sb, left(table_y), factors, gz_low),
     )
     ma, mb = swap("gx", ma, mb)
+    (zed,) = call(
+        functools.partial(y_mid_kernel, plan),
+        [(nx, my, mz)],
+        (spec, sa, sb, left(table_y), factors, edge),
+    )
     direction, *packs = call(
         functools.partial(solve_kernel, plan),
         [full_shape] + face_shapes,
-        (modes, ma, mb, factors, middle, left(table_y[wide : wide + ny]),
+        (zed, ma, mb, factors, reach, middle, left(table_y[wide : wide + ny]),
          jnp.asarray(np.stack(parts(table_z[:, wide : wide + nz]))), total),
         scratch=[(cells, mz), tile],
     )
     dhalo = exchange(packs)
-    image, sums, *dhz = call(
+    image, sums, *moves = call(
         functools.partial(image_kernel, plan, n_dev),
-        [full_shape, (n_dev, 128)] + spreads,
+        [full_shape, (n_dev, 128), (nx + 1, ny, nz)] + [full_shape] * 4,
         (direction, diag, full, tx, ty_low, ty_top, tz_low, tz_top, *dhalo),
-        scratch=[(2,) + y_face],
+        scratch=[(2,) + y_face] + spreads,
     )
     sums = lax.all_to_all(sums, AXES, 0, 0, tiled=True)
     outs = call(
         functools.partial(step_kernel, plan),
         [full_shape] * 2 + [(nx + 1, ny, nz)] + [full_shape] * 5 + face_shapes,
-        (sums, press, direction, tx, ty_low, ty_top, tz_low, tz_top,
-         hx, hy, hz, *dhalo[:4], *dhz, sat, frac, coef, rate, inject),
-        scratch=[(2,) + y_face] * 2 + [tile],
+        (sums, gx, gy_low, gy_top, gz_low, gz_top, *moves,
+         sat, frac, coef, inject, square, pull, push, hx, hy, *fz),
+        scratch=[tile],
         limit=40,
     )
     current, frac, *flows = outs[:8]
@@ -895,8 +952,12 @@
 
 def solution(mesh):
     spec = P(*AXES)
+
+    def body(*args):
+        return per_device(dict(mesh.shape), *args)
+
     return jax.shard_map(
-        functools.partial(per_device, dict(mesh.shape)),
+        body,
         mesh=mesh,
         in_specs=(spec,) * 8 + (P(),),
         out_specs=(spec,) * 3,

time: 77.4 us -> 74.7 us (0.965)
  waiting for transfers between devices: 16.8 us -> 12.6 us
  starting transfers between devices: 25 us -> 26.2 us
    ppermute x24, waiting for transfers between devices: 16.8 us -> 12.6 us  [send(): return lax.ppermute(value, axis, plan.perm(axis, which))]
    ppermute x24, starting transfers between devices: 25 us -> 26.2 us  [send(): return lax.ppermute(value, axis, plan.perm(axis, which))]
    pallas_call x13 -> x14, Pallas kernels: 23.9 us -> 24.6 us  [call(): pl.pallas_call(kernel, out_shape=[jax.ShapeDtypeStruct(s, F32) for s in o...]
  transfers between devices with their start and end apart: 24 -> 24, of which waited for: 7 -> 8; matrix products, arithmetic and copies ran while one was open for 0% -> 0% of each run, Pallas kernels for 7% -> 12%
where the time goes in v2:
time: 74.7 us; the launch traced here: 74.5 us
  starting transfers between devices  26.2 us (35%)
  Pallas kernels  24.6 us (33%)
  waiting for transfers between devices  12.6 us (17%)
  blocking collectives  10.2 us (14%)
  between operations  0.88 us (1%)
    ppermute x24, starting transfers between devices, send(): return lax.ppermute(value, axis, plan.perm(axis, which))  26.2 us
    pallas_call x14, Pallas kernels, call(): pl.pallas_call(kernel, out_shape=[jax.ShapeDtypeStruct(s, F32) for s in o...  24.6 us
    ppermute x24, waiting for transfers between devices, send(): return lax.ppermute(value, axis, plan.perm(axis, which))  12.6 us
    all_to_all x1, blocking collectives, per_device(): sums = lax.all_to_all(sums, AXES, 0, 0, tiled=True)  10.2 us
  transfers between devices with their start and end apart: 24, of which 8 were waited for; matrix products, arithmetic and copies ran while one was open for 0% of the time, Pallas kernels for 12%

profile of v2, /device:TPU:0, one launch (start us, length us, event | category | flops | bytes accessed | tf_op | source)
XLA Modules:
  0.0 74.5 jit_solution(7737381583543385801)
XLA Ops:
  0.7 2.0 %shard_map.202 = (f32[32,32,128]{2,1,0:T(8,128)S(1)}, f32[32,32,128]{2,1,0:T(8,128)S(1)}, f32[32,32,128]{2,1,0:T(8,128)S(1)}, f32[32,32,128]{2,1,0:T(8,128)S(1)}...) custom-call(f32[32,32,128]{2,1,0:T(8,128)} %press_in.1, ...), custom_call_target="tpu_custom_call" | custom-call | tf_op jit(solution)/shard_map/pallas_call | solution.py:104
  2.7 3.1 %collective-permute-start = (f32[3,32,128]{2,1,0:T(8,128)S(1)}, f32[3,32,128]{2,1,0:T(8,128)S(1)}, u32[]{:S(2)}, u32[]{:S(2)}) collective-permute-start(f32[3,32,128]{2,1,0:T(8,128)S(1)} %get-tuple-element.85), channel_id=1, source_target_pairs={{0,8},{8,0},{16,24},{24,16},{1,9},{9,1},{17,25},{25,17},{2,10},{10... | collective-permute-start | bytes 147464 | tf_op jit(solution)/shard_map/ppermute | solution.py:830
  5.8 2.5 %collective-permute-start.1 = (f32[3,32,128]{2,1,0:T(8,128)S(1)}, f32[3,32,128]{2,1,0:T(8,128)S(1)}, u32[]{:S(2)}, u32[]{:S(2)}) collective-permute-start(f32[3,32,128]{2,1,0:T(8,128)S(1)} %get-tuple-element.86), channel_id=1, source_target_pairs={{8,16},{16,8},{24,0},{0,24},{9,17},{17,9},{25,1},{1,25},{10,18},{1... | collective-permute-start | bytes 147464 | tf_op jit(solution)/shard_map/ppermute | solution.py:830
  8.3 0.0 collective-permute-start.2
  8.3 1.6 %collective-permute-start.3 = (f32[3,32,128]{2,1,0:T(8,128)S(1)}, f32[3,32,128]{2,1,0:T(8,128)S(1)}, u32[]{:S(2)}, u32[]{:S(2)}) collective-permute-start(f32[3,32,128]{2,1,0:T(8,128)S(1)} %get-tuple-element.88), channel_id=1, source_target_pairs={{2,4},{4,2},{6,0},{0,6},{3,5},{5,3},{7,1},{1,7},{10,12},{12,10},{1... | collective-permute-start | bytes 147464 | tf_op jit(solution)/shard_map/ppermute | solution.py:830
  9.9 1.4 %shard_map.203 = (f32[32,32,128]{2,1,0:T(8,128)S(1)}, f32[32,32,128]{2,1,0:T(8,128)S(1)}, f32[32,32,128]{2,1,0:T(8,128)S(1)}, f32[32,32,128]{2,1,0:T(8,128)S(1)}, f32[32,32,128]{2,1,0:T(8,128)S(1)}) custom-call(f32[32,32,128]{2,1,0:T(8,128)S(1)} %get-tuple-element.81.press, f32[32,32,128]{2,1,0:T(8,128)S(1)} %get-tuple-element.82.mob, ...), custom_call_target="tpu_custom_call" | custom-call | tf_op jit(solution)/shard_map/pallas_call | solution.py:104
  11.3 0.0 copy-start.5
  11.3 0.0 collective-permute-done.xa
  11.3 0.4 collective-permute-done.1.xb
  11.7 0.0 collective-permute-done.2.ya
  11.7 0.1 collective-permute-done.3.yb
  11.8 1.4 %shard_map.204 = (f32[32,32,128]{2,1,0:T(8,128)S(1)}, f32[16,1024]{1,0:T(8,128)S(1)}) custom-call(f32[32,32,128]{2,1,0:T(8,128)S(1)} %get-tuple-element.83.res_in, f32[32,32,128]{2,1,0:T(8,128)S(1)} %get-tuple-element.81.press, f32[32,32,128]{2,1,0:T(8,128)S(1)} %get-tuple-element.82.mob, ...), custom_call_target="tpu_custom_call", output_to_operand_aliasing={{0}: (0, {})} | custom-call | tf_op jit(solution)/shard_map/pallas_call | solution.py:104
  13.2 1.6 %collective-permute-start.4 = (f32[16,1024]{1,0:T(8,128)S(1)}, f32[16,1024]{1,0:T(8,128)S(1)}, u32[]{:S(2)}, u32[]{:S(2)}) collective-permute-start(f32[16,1024]{1,0:T(8,128)S(1)} %get-tuple-element.95.rest_0_), channel_id=1, source_target_pairs={{0,1},{1,0},{2,3},{3,2},{4,5},{5,4},{6,7},{7,6},{8,9},{9,8},{10,11... | collective-permute-start | bytes 196616 | tf_op jit(solution)/shard_map/ppermute | solution.py:830
  14.8 0.6 shard_map.205
  15.4 0.0 copy-start
  15.5 0.0 copy-start.7
  15.5 2.3 %collective-permute-done.4.rest_1_ = f32[16,1024]{1,0:T(8,128)S(1)} collective-permute-done((f32[16,1024]{1,0:T(8,128)S(1)}, f32[16,1024]{1,0:T(8,128)S(1)}, u32[]{:S(2)}, u32[]{:S(2)}) %collective-permute-start.4) | collective-permute-done | bytes 65568 | tf_op jit(solution)/shard_map/ppermute | solution.py:830
  17.8 0.8 %shard_map.206 = (f32[32,32,144]{2,1,0:T(8,128)S(1)}, f32[36,8,128]{2,1,0:T(8,128)S(1)}, f32[36,8,128]{2,1,0:T(8,128)S(1)}) custom-call(f32[32,32,128]{2,1,0:T(8,128)S(1)} %get-tuple-element.89.res, bf16[384,144]{1,0:T(8,128)(2,1)S(1)} %copy-done.6, f32[48,144]{1,0:T(8,128)S(1)} %copy-done.10, f32[48,144]{1,0:T(8,128)S(1)} %copy-done.11, ...), custom_call_target="tpu_custom_call" | custom-call | tf_op jit(solution)/shard_map/pallas_call | solution.py:104
  18.6 0.1 collective-permute-start.5
  18.6 1.6 %collective-permute-start.6 = (f32[36,8,128]{2,1,0:T(8,128)S(1)}, f32[36,8,128]{2,1,0:T(8,128)S(1)}, u32[]{:S(2)}, u32[]{:S(2)}) collective-permute-start(f32[36,8,128]{2,1,0:T(8,128)S(1)} %get-tuple-element.98), channel_id=1, source_target_pairs={{2,4},{4,2},{6,0},{0,6},{3,5},{5,3},{7,1},{1,7},{10,12},{12,10},{1... | collective-permute-start | bytes 442376 | tf_op jit(solution)/shard_map/ppermute | solution.py:830
  20.2 4.1 %shard_map.207 = (f32[32,32,128]{2,1,0:T(8,128)S(1)}, f32[32,32,128]{2,1,0:T(8,128)S(1)}, f32[32,32,128]{2,1,0:T(8,128)S(1)}, f32[32,32,128]{2,1,0:T(8,128)S(1)}...) custom-call(f32[32,32,128]{2,1,0:T(8,128)S(1)} %get-tuple-element.89.res, ...), custom_call_target="tpu_custom_call" | custom-call | tf_op jit(solution)/shard_map/pallas_call | solution.py:104
  24.3 0.0 collective-permute-done.5.ya
  24.3 0.0 collective-permute-done.6.yb
  24.3 1.2 %shard_map.208 = (f32[16,48,144]{2,1,0:T(8,128)S(1)}, f32[56,128]{1,0:T(8,128)S(1)}, f32[56,128]{1,0:T(8,128)S(1)}) custom-call(f32[32,32,144]{2,1,0:T(8,128)S(1)} %get-tuple-element.96.spec, f32[36,8,128]{2,1,0:T(8,128)S(1)} %collective-permute-done.5.ya, f32[36,8,128]{2,1,0:T(8,128)S(1)} %collective-permute-done.6.yb, bf16[48,144]{1,0:T(8,128)(2,1)S(1)} %copy-done.7, ...), custom_call_target="tpu_custom_call" | custom-call | tf_op jit(solution)/shard_map/pallas_call | solution.py:104
  25.5 0.7 collective-permute-start.7
  26.2 1.5 %collective-permute-start.8 = (f32[56,128]{1,0:T(8,128)S(1)}, f32[56,128]{1,0:T(8,128)S(1)}, u32[]{:S(2)}, u32[]{:S(2)}) collective-permute-start(f32[56,128]{1,0:T(8,128)S(1)} %get-tuple-element.103), channel_id=1, source_target_pairs={{8,16},{16,8},{24,0},{0,24},{9,17},{17,9},{25,1},{1,25},{10,18},{1... | collective-permute-start | bytes 86024 | tf_op jit(solution)/shard_map/ppermute | solution.py:830
  27.8 1.3 %shard_map.209.zed = f32[32,48,144]{2,1,0:T(8,128)S(1)} custom-call(f32[32,32,144]{2,1,0:T(8,128)S(1)} %get-tuple-element.96.spec, f32[36,8,128]{2,1,0:T(8,128)S(1)} %collective-permute-done.5.ya, f32[36,8,128]{2,1,0:T(8,128)S(1)} %collective-permute-done.6.yb, bf16[48,144]{1,0:T(8,128)(2,1)S(1)} %copy-done.7, f32[24,48,144]{2,1,0:T(8,128)S(1)} %copy-done, ...), custom_call_target="tpu_custom_call" | custom-call | tf_op jit(solution)/shard_map/pallas_call | solution.py:104
  29.1 0.4 collective-permute-done.7.xa
  29.4 2.5 %collective-permute-done.8.xb = f32[56,128]{1,0:T(8,128)S(1)} collective-permute-done((f32[56,128]{1,0:T(8,128)S(1)}, f32[56,128]{1,0:T(8,128)S(1)}, u32[]{:S(2)}, u32[]{:S(2)}) %collective-permute-start.8) | collective-permute-done | bytes 28704 | tf_op jit(solution)/shard_map/ppermute | solution.py:830
  31.9 2.9 %shard_map.210 = (f32[32,32,128]{2,1,0:T(8,128)S(1)}, f32[32,128]{1,0:T(8,128)S(1)}, f32[32,128]{1,0:T(8,128)S(1)}, f32[32,128]{1,0:T(8,128)S(1)}, f32[32,128]{1,0:T(8,128)S(1)}, /*index=5*/f32[8,128]{1,0:T(8,128)S(1)}) custom-call(f32[32,48,144]{2,1,0:T(8,128)S(1)} %shard_map.209.zed, f32[56,128]{1,0:T(8,128)S(1)} %collective-permute-done.7.xa, ...), custom_call_target="tpu_custom_call" | custom-call | tf_op jit(solution)/shard_map/pallas_call | solution.py:104
  34.8 0.0 collective-permute-start.9
  34.9 1.8 %collective-permute-start.10 = (f32[32,128]{1,0:T(8,128)S(1)}, f32[32,128]{1,0:T(8,128)S(1)}, u32[]{:S(2)}, u32[]{:S(2)}) collective-permute-start(f32[32,128]{1,0:T(8,128)S(1)} %get-tuple-element.114), channel_id=1, source_target_pairs={{8,16},{16,8},{24,0},{0,24},{9,17},{17,9},{25,1},{1,25},{10,18},{1... | collective-permute-start | bytes 49160 | tf_op jit(solution)/shard_map/ppermute | solution.py:830
  36.6 0.0 collective-permute-start.11
  36.6 1.9 %collective-permute-start.12 = (f32[32,128]{1,0:T(8,128)S(1)}, f32[32,128]{1,0:T(8,128)S(1)}, u32[]{:S(2)}, u32[]{:S(2)}) collective-permute-start(f32[32,128]{1,0:T(8,128)S(1)} %get-tuple-element.116), channel_id=1, source_target_pairs={{2,4},{4,2},{6,0},{0,6},{3,5},{5,3},{7,1},{1,7},{10,12},{12,10},{1... | collective-permute-start | bytes 49160 | tf_op jit(solution)/shard_map/ppermute | solution.py:830
  38.5 1.5 %collective-permute-start.13 = (f32[8,128]{1,0:T(8,128)S(1)}, f32[8,128]{1,0:T(8,128)S(1)}, u32[]{:S(2)}, u32[]{:S(2)}) collective-permute-start(f32[8,128]{1,0:T(8,128)S(1)} %get-tuple-element.117), channel_id=1, source_target_pairs={{0,1},{1,0},{2,3},{3,2},{4,5},{5,4},{6,7},{7,6},{8,9},{9,8},{10,11... | collective-permute-start | bytes 12296 | tf_op jit(solution)/shard_map/ppermute | solution.py:830
  40.0 2.1 %collective-permute-done.13.rest_0_ = f32[8,128]{1,0:T(8,128)S(1)} collective-permute-done((f32[8,128]{1,0:T(8,128)S(1)}, f32[8,128]{1,0:T(8,128)S(1)}, u32[]{:S(2)}, u32[]{:S(2)}) %collective-permute-start.13) | collective-permute-done | bytes 4128 | tf_op jit(solution)/shard_map/ppermute | solution.py:830
  42.1 0.0 collective-permute-done.9.xa
  42.1 0.0 collective-permute-done.10.xb
  42.1 0.0 collective-permute-done.11.ya
  42.1 0.0 collective-permute-done.12.yb
  42.2 1.3 %shard_map.211 = (f32[32,32,128]{2,1,0:T(8,128)S(1)}, f32[32,128]{1,0:T(8,128)S(1)}, f32[33,32,128]{2,1,0:T(8,128)S(1)}, f32[32,32,128]{2,1,0:T(8,128)S(1)}, f32...) custom-call(f32[32,32,128]{2,1,0:T(8,128)S(1)} %get-tuple-element.105.direction, ...), custom_call_target="tpu_custom_call" | custom-call | tf_op jit(solution)/shard_map/pallas_call | solution.py:104
  43.5 10.2 %all_to_all.11 = f32[32,1,128]{2,1,0:T(1,128)S(1)} all-to-all(f32[32,1,128]{2,1,0:T(1,128)S(1)} %bitcast.6), channel_id=1, replica_groups=mesh['gx'=4,'gy'=4,'gz'=2] {'gx','gy','gz'}, dimensions={0} | all-to-all | bytes 32768 | tf_op jit(solution)/shard_map/all_to_all | solution.py:918
  53.7 2.1 %shard_map.213 = (f32[32,32,128]{2,1,0:T(8,128)S(1)}, f32[32,32,128]{2,1,0:T(8,128)S(1)}, f32[33,32,128]{2,1,0:T(8,128)S(1)}, f32[32,32,128]{2,1,0:T(8,128)S(1)}...) custom-call(f32[32,128]{1,0:T(8,128)S(1)} %bitcast.4, ...), custom_call_target="tpu_custom_call" | custom-call | tf_op jit(solution)/shard_map/pallas_call | solution.py:104
  55.8 0.5 collective-permute-start.14
  56.3 1.5 %collective-permute-start.15 = (f32[32,128]{1,0:T(8,128)S(1)}, f32[32,128]{1,0:T(8,128)S(1)}, u32[]{:S(2)}, u32[]{:S(2)}) collective-permute-start(f32[32,128]{1,0:T(8,128)S(1)} %get-tuple-element.147), channel_id=1, source_target_pairs={{8,16},{16,8},{24,0},{0,24},{9,17},{17,9},{25,1},{1,25},{10,18},{1... | collective-permute-start | bytes 49160 | tf_op jit(solution)/shard_map/ppermute | solution.py:830
  57.7 0.0 collective-permute-start.16
  57.7 0.7 collective-permute-start.17
  58.5 0.5 collective-permute-start.18
  59.0 1.3 %shard_map.212 = (f32[32,32,128]{2,1,0:T(8,128)}, f32[32,32,128]{2,1,0:T(8,128)}, f32[8,128]{1,0:T(8,128)S(1)}) custom-call(f32[32,128]{1,0:T(8,128)S(1)} %bitcast.5, f32[32,32,128]{2,1,0:T(8,128)S(1)} %get-tuple-element.81.press, f32[32,32,128]{2,1,0:T(8,128)S(1)} %get-tuple-element.105.direction, f32[32,32,128]{2,1,0:T(8,128)S(1)} %get-tuple-element.107.full, ...), custom_call_target="tpu_custom_call" | custom-call | tf_op jit(solution)/shard_map/pallas_call | solution.py:104
  60.3 1.8 %collective-permute-done.18.refs_16_ = f32[8,128]{1,0:T(8,128)S(1)} collective-permute-done((f32[8,128]{1,0:T(8,128)S(1)}, f32[8,128]{1,0:T(8,128)S(1)}, u32[]{:S(2)}, u32[]{:S(2)}) %collective-permute-start.18) | collective-permute-done | bytes 4128 | tf_op jit(solution)/shard_map/ppermute | solution.py:830
  62.1 0.0 collective-permute-done.14.refs_12_
  62.1 0.0 collective-permute-done.15.refs_13_
  62.1 0.0 collective-permute-done.16.refs_14_
  62.1 0.0 collective-permute-done.17.refs_15_
  62.1 2.1 %shard_map.214 = (f32[32,32,128]{2,1,0:T(8,128)S(1)}, f32[32,32,128]{2,1,0:T(8,128)S(1)}, f32[32,128]{1,0:T(8,128)S(1)}, f32[32,128]{1,0:T(8,128)S(1)}, f32[32,1...) custom-call(f32[32,32,128]{2,1,0:T(8,128)S(1)} %get-tuple-element.90.sat.refs_11_.refs_0_, ...), custom_call_target="tpu_custom_call" | custom-call | tf_op jit(solution)/shard_map/pallas_call | solution.py:104
  64.2 0.0 collective-permute-start.19
  64.3 2.9 %collective-permute-start.20 = (f32[32,128]{1,0:T(8,128)S(1)}, f32[32,128]{1,0:T(8,128)S(1)}, u32[]{:S(2)}, u32[]{:S(2)}) collective-permute-start(f32[32,128]{1,0:T(8,128)S(1)} %get-tuple-element.155), channel_id=1, source_target_pairs={{8,16},{16,8},{24,0},{0,24},{9,17},{17,9},{25,1},{1,25},{10,18},{1... | collective-permute-start | bytes 49160 | tf_op jit(solution)/shard_map/ppermute | solution.py:830
  67.1 0.0 collective-permute-start.21
  67.2 1.6 %collective-permute-start.22 = (f32[32,128]{1,0:T(8,128)S(1)}, f32[32,128]{1,0:T(8,128)S(1)}, u32[]{:S(2)}, u32[]{:S(2)}) collective-permute-start(f32[32,128]{1,0:T(8,128)S(1)} %get-tuple-element.157), channel_id=1, source_target_pairs={{2,4},{4,2},{6,0},{0,6},{3,5},{5,3},{7,1},{1,7},{10,12},{12,10},{1... | collective-permute-start | bytes 49160 | tf_op jit(solution)/shard_map/ppermute | solution.py:830
  68.8 0.5 collective-permute-start.23
  69.3 3.1 %collective-permute-done.23.refs_16_ = f32[8,128]{1,0:T(8,128)S(1)} collective-permute-done((f32[8,128]{1,0:T(8,128)S(1)}, f32[8,128]{1,0:T(8,128)S(1)}, u32[]{:S(2)}, u32[]{:S(2)}) %collective-permute-start.23) | collective-permute-done | bytes 4128 | tf_op jit(solution)/shard_map/ppermute | solution.py:830
  72.4 0.0 collective-permute-done.19.refs_12_
  72.4 0.0 collective-permute-done.20.refs_13_
  72.4 2.1 %shard_map.215 = f32[32,32,128]{2,1,0:T(8,128)} custom-call(f32[32,32,128]{2,1,0:T(8,128)S(1)} %get-tuple-element.90.sat.refs_11_.refs_0_, f32[32,32,128]{2,1,0:T(8,128)S(1)} %get-tuple-element.152.refs_1_, f32[32,32,128]{2,1,0:T(8,128)S(1)} %get-tuple-element.153.refs_2_, f32[32,32,128]{2,1,0:T(8,128)S(1)} %get-tuple-element.91.coef.refs_13_.refs_3_, ...), custom_call_target="tpu_custom_call" | custom-call | tf_op jit(solution)/shard_map/pallas_call | solution.py:104
  (25 shorter events, 0.1 us)
Async XLA Ops:
  0.6 9.3 %copy-start.3 = (f32[32,32,128]{2,1,0:T(8,128)S(1)}, f32[32,32,128]{2,1,0:T(8,128)}, u32[]{:S(2)}) copy-start(f32[32,32,128]{2,1,0:T(8,128)} %source.1) | copy-start | bytes 1572868
  0.6 9.3 %copy-start.4 = (f32[32,32,128]{2,1,0:T(8,128)S(1)}, f32[32,32,128]{2,1,0:T(8,128)}, u32[]{:S(2)}) copy-start(f32[32,32,128]{2,1,0:T(8,128)} %compress.1) | copy-start | bytes 1572868
  0.7 9.3 %copy-start.1 = (s32[32,32,128]{2,1,0:T(8,128)S(1)}, s32[32,32,128]{2,1,0:T(8,128)}, u32[]{:S(2)}) copy-start(s32[32,32,128]{2,1,0:T(8,128)} %well.3) | copy-start | bytes 1572868
  2.7 8.6 %collective-permute-start = (f32[3,32,128]{2,1,0:T(8,128)S(1)}, f32[3,32,128]{2,1,0:T(8,128)S(1)}, u32[]{:S(2)}, u32[]{:S(2)}) collective-permute-start(f32[3,32,128]{2,1,0:T(8,128)S(1)} %get-tuple-element.85), channel_id=1, source_target_pairs={{0,8},{8,0},{16,24},{24,16},{1,9},{9,1},{17,25},{25,17},{2,10},{10... | collective-permute-start | bytes 147464 | tf_op jit(solution)/shard_map/ppermute | solution.py:830
  5.8 5.9 %collective-permute-start.1 = (f32[3,32,128]{2,1,0:T(8,128)S(1)}, f32[3,32,128]{2,1,0:T(8,128)S(1)}, u32[]{:S(2)}, u32[]{:S(2)}) collective-permute-start(f32[3,32,128]{2,1,0:T(8,128)S(1)} %get-tuple-element.86), channel_id=1, source_target_pairs={{8,16},{16,8},{24,0},{0,24},{9,17},{17,9},{25,1},{1,25},{10,18},{1... | collective-permute-start | bytes 147464 | tf_op jit(solution)/shard_map/ppermute | solution.py:830
  8.3 3.4 %collective-permute-start.2 = (f32[3,32,128]{2,1,0:T(8,128)S(1)}, f32[3,32,128]{2,1,0:T(8,128)S(1)}, u32[]{:S(2)}, u32[]{:S(2)}) collective-permute-start(f32[3,32,128]{2,1,0:T(8,128)S(1)} %get-tuple-element.87), channel_id=1, source_target_pairs={{0,2},{2,0},{4,6},{6,4},{1,3},{3,1},{5,7},{7,5},{8,10},{10,8},{12,... | collective-permute-start | bytes 147464 | tf_op jit(solution)/shard_map/ppermute | solution.py:830
  8.3 3.5 %collective-permute-start.3 = (f32[3,32,128]{2,1,0:T(8,128)S(1)}, f32[3,32,128]{2,1,0:T(8,128)S(1)}, u32[]{:S(2)}, u32[]{:S(2)}) collective-permute-start(f32[3,32,128]{2,1,0:T(8,128)S(1)} %get-tuple-element.88), channel_id=1, source_target_pairs={{2,4},{4,2},{6,0},{0,6},{3,5},{5,3},{7,1},{1,7},{10,12},{12,10},{1... | collective-permute-start | bytes 147464 | tf_op jit(solution)/shard_map/ppermute | solution.py:830
  11.3 3.5 %copy-start.5 = (f32[32,32,128]{2,1,0:T(8,128)S(1)}, f32[32,32,128]{2,1,0:T(8,128)}, u32[]{:S(2)}) copy-start(f32[32,32,128]{2,1,0:T(8,128)} %poro.1) | copy-start | bytes 1572868
  13.2 4.5 %collective-permute-start.4 = (f32[16,1024]{1,0:T(8,128)S(1)}, f32[16,1024]{1,0:T(8,128)S(1)}, u32[]{:S(2)}, u32[]{:S(2)}) collective-permute-start(f32[16,1024]{1,0:T(8,128)S(1)} %get-tuple-element.95.rest_0_), channel_id=1, source_target_pairs={{0,1},{1,0},{2,3},{3,2},{4,5},{5,4},{6,7},{7,6},{8,9},{9,8},{10,11... | collective-permute-start | bytes 196616 | tf_op jit(solution)/shard_map/ppermute | solution.py:830
  14.8 3.0 %copy-start.6 = (bf16[384,144]{1,0:T(8,128)(2,1)S(1)}, bf16[384,144]{1,0:T(8,128)(2,1)}, u32[]{:S(2)}) copy-start(bf16[384,144]{1,0:T(8,128)(2,1)} %constant.23.clone.basis) | copy-start | bytes 331780
  14.8 3.0 %copy-start.10 = (f32[48,144]{1,0:T(8,128)S(1)}, f32[48,144]{1,0:T(8,128)}, u32[]{:S(2)}) copy-start(f32[48,144]{1,0:T(8,128)} %constant.27.rim_low) | copy-start | bytes 82948
  14.8 3.0 %copy-start.11 = (f32[48,144]{1,0:T(8,128)S(1)}, f32[48,144]{1,0:T(8,128)}, u32[]{:S(2)}) copy-start(f32[48,144]{1,0:T(8,128)} %constant.28.rim_top) | copy-start | bytes 82948
  15.4 8.9 %copy-start = (f32[24,48,144]{2,1,0:T(8,128)S(1)}, f32[24,48,144]{2,1,0:T(8,128)}, u32[]{:S(2)}) copy-start(f32[24,48,144]{2,1,0:T(8,128)} %constant.18.clone.factors) | copy-start | bytes 1990660
  15.5 8.9 %copy-start.7 = (bf16[48,144]{1,0:T(8,128)(2,1)S(1)}, bf16[48,144]{1,0:T(8,128)(2,1)}, u32[]{:S(2)}) copy-start(bf16[48,144]{1,0:T(8,128)(2,1)} %constant.24.clone.basis) | copy-start | bytes 41476
  18.6 5.7 %collective-permute-start.5 = (f32[36,8,128]{2,1,0:T(8,128)S(1)}, f32[36,8,128]{2,1,0:T(8,128)S(1)}, u32[]{:S(2)}, u32[]{:S(2)}) collective-permute-start(f32[36,8,128]{2,1,0:T(8,128)S(1)} %get-tuple-element.97), channel_id=1, source_target_pairs={{0,2},{2,0},{4,6},{6,4},{1,3},{3,1},{5,7},{7,5},{8,10},{10,8},{12,... | collective-permute-start | bytes 442376 | tf_op jit(solution)/shard_map/ppermute | solution.py:830
  18.6 5.7 %collective-permute-start.6 = (f32[36,8,128]{2,1,0:T(8,128)S(1)}, f32[36,8,128]{2,1,0:T(8,128)S(1)}, u32[]{:S(2)}, u32[]{:S(2)}) collective-permute-start(f32[36,8,128]{2,1,0:T(8,128)S(1)} %get-tuple-element.98), channel_id=1, source_target_pairs={{2,4},{4,2},{6,0},{0,6},{3,5},{5,3},{7,1},{1,7},{10,12},{12,10},{1... | collective-permute-start | bytes 442376 | tf_op jit(solution)/shard_map/ppermute | solution.py:830
  25.5 3.9 %collective-permute-start.7 = (f32[56,128]{1,0:T(8,128)S(1)}, f32[56,128]{1,0:T(8,128)S(1)}, u32[]{:S(2)}, u32[]{:S(2)}) collective-permute-start(f32[56,128]{1,0:T(8,128)S(1)} %get-tuple-element.102), channel_id=1, source_target_pairs={{0,8},{8,0},{16,24},{24,16},{1,9},{9,1},{17,25},{25,17},{2,10},{10... | collective-permute-start | bytes 86024 | tf_op jit(solution)/shard_map/ppermute | solution.py:830
  26.2 5.7 %collective-permute-start.8 = (f32[56,128]{1,0:T(8,128)S(1)}, f32[56,128]{1,0:T(8,128)S(1)}, u32[]{:S(2)}, u32[]{:S(2)}) collective-permute-start(f32[56,128]{1,0:T(8,128)S(1)} %get-tuple-element.103), channel_id=1, source_target_pairs={{8,16},{16,8},{24,0},{0,24},{9,17},{17,9},{25,1},{1,25},{10,18},{1... | collective-permute-start | bytes 86024 | tf_op jit(solution)/shard_map/ppermute | solution.py:830
  27.8 4.1 %copy-start.2 = (f32[16,48,144]{2,1,0:T(8,128)S(1)}, f32[16,48,144]{2,1,0:T(8,128)}, u32[]{:S(2)}) copy-start(f32[16,48,144]{2,1,0:T(8,128)} %constant.19.clone.reach) | copy-start | bytes 1327108
  27.8 4.1 %copy-start.8 = (bf16[2,144,128]{2,1,0:T(8,128)(2,1)S(1)}, bf16[2,144,128]{2,1,0:T(8,128)(2,1)}, u32[]{:S(2)}) copy-start(bf16[2,144,128]{2,1,0:T(8,128)(2,1)} %constant.26.clone.basis_z) | copy-start | bytes 221188
  27.8 4.1 %copy-start.9 = (f32[48,144]{1,0:T(8,128)S(1)}, f32[48,144]{1,0:T(8,128)}, u32[]{:S(2)}) copy-start(f32[48,144]{1,0:T(8,128)} %constant.20.clone.middle) | copy-start | bytes 82948
  27.8 4.1 %copy-start.12 = (bf16[32,144]{1,0:T(8,128)(2,1)S(1)}, bf16[32,144]{1,0:T(8,128)(2,1)}, u32[]{:S(2)}) copy-start(bf16[32,144]{1,0:T(8,128)(2,1)} %constant.25.clone.basis_y) | copy-start | bytes 27652
  34.8 7.3 %collective-permute-start.9 = (f32[32,128]{1,0:T(8,128)S(1)}, f32[32,128]{1,0:T(8,128)S(1)}, u32[]{:S(2)}, u32[]{:S(2)}) collective-permute-start(f32[32,128]{1,0:T(8,128)S(1)} %get-tuple-element.113), channel_id=1, source_target_pairs={{0,8},{8,0},{16,24},{24,16},{1,9},{9,1},{17,25},{25,17},{2,10},{10... | collective-permute-start | bytes 49160 | tf_op jit(solution)/shard_map/ppermute | solution.py:830
  34.9 7.3 %collective-permute-start.10 = (f32[32,128]{1,0:T(8,128)S(1)}, f32[32,128]{1,0:T(8,128)S(1)}, u32[]{:S(2)}, u32[]{:S(2)}) collective-permute-start(f32[32,128]{1,0:T(8,128)S(1)} %get-tuple-element.114), channel_id=1, source_target_pairs={{8,16},{16,8},{24,0},{0,24},{9,17},{17,9},{25,1},{1,25},{10,18},{1... | collective-permute-start | bytes 49160 | tf_op jit(solution)/shard_map/ppermute | solution.py:830
  36.6 5.5 %collective-permute-start.11 = (f32[32,128]{1,0:T(8,128)S(1)}, f32[32,128]{1,0:T(8,128)S(1)}, u32[]{:S(2)}, u32[]{:S(2)}) collective-permute-start(f32[32,128]{1,0:T(8,128)S(1)} %get-tuple-element.115), channel_id=1, source_target_pairs={{0,2},{2,0},{4,6},{6,4},{1,3},{3,1},{5,7},{7,5},{8,10},{10,8},{12,... | collective-permute-start | bytes 49160 | tf_op jit(solution)/shard_map/ppermute | solution.py:830
  36.6 5.5 %collective-permute-start.12 = (f32[32,128]{1,0:T(8,128)S(1)}, f32[32,128]{1,0:T(8,128)S(1)}, u32[]{:S(2)}, u32[]{:S(2)}) collective-permute-start(f32[32,128]{1,0:T(8,128)S(1)} %get-tuple-element.116), channel_id=1, source_target_pairs={{2,4},{4,2},{6,0},{0,6},{3,5},{5,3},{7,1},{1,7},{10,12},{12,10},{1... | collective-permute-start | bytes 49160 | tf_op jit(solution)/shard_map/ppermute | solution.py:830
  38.5 3.6 %collective-permute-start.13 = (f32[8,128]{1,0:T(8,128)S(1)}, f32[8,128]{1,0:T(8,128)S(1)}, u32[]{:S(2)}, u32[]{:S(2)}) collective-permute-start(f32[8,128]{1,0:T(8,128)S(1)} %get-tuple-element.117), channel_id=1, source_target_pairs={{0,1},{1,0},{2,3},{3,2},{4,5},{5,4},{6,7},{7,6},{8,9},{9,8},{10,11... | collective-permute-start | bytes 12296 | tf_op jit(solution)/shard_map/ppermute | solution.py:830
  55.8 6.3 %collective-permute-start.14 = (f32[32,128]{1,0:T(8,128)S(1)}, f32[32,128]{1,0:T(8,128)S(1)}, u32[]{:S(2)}, u32[]{:S(2)}) collective-permute-start(f32[32,128]{1,0:T(8,128)S(1)} %get-tuple-element.146), channel_id=1, source_target_pairs={{0,8},{8,0},{16,24},{24,16},{1,9},{9,1},{17,25},{25,17},{2,10},{10... | collective-permute-start | bytes 49160 | tf_op jit(solution)/shard_map/ppermute | solution.py:830
  56.3 5.8 %collective-permute-start.15 = (f32[32,128]{1,0:T(8,128)S(1)}, f32[32,128]{1,0:T(8,128)S(1)}, u32[]{:S(2)}, u32[]{:S(2)}) collective-permute-start(f32[32,128]{1,0:T(8,128)S(1)} %get-tuple-element.147), channel_id=1, source_target_pairs={{8,16},{16,8},{24,0},{0,24},{9,17},{17,9},{25,1},{1,25},{10,18},{1... | collective-permute-start | bytes 49160 | tf_op jit(solution)/shard_map/ppermute | solution.py:830
  57.7 4.4 %collective-permute-start.16 = (f32[32,128]{1,0:T(8,128)S(1)}, f32[32,128]{1,0:T(8,128)S(1)}, u32[]{:S(2)}, u32[]{:S(2)}) collective-permute-start(f32[32,128]{1,0:T(8,128)S(1)} %get-tuple-element.148), channel_id=1, source_target_pairs={{0,2},{2,0},{4,6},{6,4},{1,3},{3,1},{5,7},{7,5},{8,10},{10,8},{12,... | collective-permute-start | bytes 49160 | tf_op jit(solution)/shard_map/ppermute | solution.py:830
  57.7 4.4 %collective-permute-start.17 = (f32[32,128]{1,0:T(8,128)S(1)}, f32[32,128]{1,0:T(8,128)S(1)}, u32[]{:S(2)}, u32[]{:S(2)}) collective-permute-start(f32[32,128]{1,0:T(8,128)S(1)} %get-tuple-element.149), channel_id=1, source_target_pairs={{2,4},{4,2},{6,0},{0,6},{3,5},{5,3},{7,1},{1,7},{10,12},{12,10},{1... | collective-permute-start | bytes 49160 | tf_op jit(solution)/shard_map/ppermute | solution.py:830
  58.5 3.6 %collective-permute-start.18 = (f32[8,128]{1,0:T(8,128)S(1)}, f32[8,128]{1,0:T(8,128)S(1)}, u32[]{:S(2)}, u32[]{:S(2)}) collective-permute-start(f32[8,128]{1,0:T(8,128)S(1)} %get-tuple-element.150), channel_id=1, source_target_pairs={{0,1},{1,0},{2,3},{3,2},{4,5},{5,4},{6,7},{7,6},{8,9},{9,8},{10,11... | collective-permute-start | bytes 12296 | tf_op jit(solution)/shard_map/ppermute | solution.py:830
  64.2 8.2 %collective-permute-start.19 = (f32[32,128]{1,0:T(8,128)S(1)}, f32[32,128]{1,0:T(8,128)S(1)}, u32[]{:S(2)}, u32[]{:S(2)}) collective-permute-start(f32[32,128]{1,0:T(8,128)S(1)} %get-tuple-element.154), channel_id=1, source_target_pairs={{0,8},{8,0},{16,24},{24,16},{1,9},{9,1},{17,25},{25,17},{2,10},{10... | collective-permute-start | bytes 49160 | tf_op jit(solution)/shard_map/ppermute | solution.py:830
  64.3 8.1 %collective-permute-start.20 = (f32[32,128]{1,0:T(8,128)S(1)}, f32[32,128]{1,0:T(8,128)S(1)}, u32[]{:S(2)}, u32[]{:S(2)}) collective-permute-start(f32[32,128]{1,0:T(8,128)S(1)} %get-tuple-element.155), channel_id=1, source_target_pairs={{8,16},{16,8},{24,0},{0,24},{9,17},{17,9},{25,1},{1,25},{10,18},{1... | collective-permute-start | bytes 49160 | tf_op jit(solution)/shard_map/ppermute | solution.py:830
  67.1 5.3 %collective-permute-start.21 = (f32[32,128]{1,0:T(8,128)S(1)}, f32[32,128]{1,0:T(8,128)S(1)}, u32[]{:S(2)}, u32[]{:S(2)}) collective-permute-start(f32[32,128]{1,0:T(8,128)S(1)} %get-tuple-element.156), channel_id=1, source_target_pairs={{0,2},{2,0},{4,6},{6,4},{1,3},{3,1},{5,7},{7,5},{8,10},{10,8},{12,... | collective-permute-start | bytes 49160 | tf_op jit(solution)/shard_map/ppermute | solution.py:830
  67.2 5.3 %collective-permute-start.22 = (f32[32,128]{1,0:T(8,128)S(1)}, f32[32,128]{1,0:T(8,128)S(1)}, u32[]{:S(2)}, u32[]{:S(2)}) collective-permute-start(f32[32,128]{1,0:T(8,128)S(1)} %get-tuple-element.157), channel_id=1, source_target_pairs={{2,4},{4,2},{6,0},{0,6},{3,5},{5,3},{7,1},{1,7},{10,12},{12,10},{1... | collective-permute-start | bytes 49160 | tf_op jit(solution)/shard_map/ppermute | solution.py:830
  68.8 3.6 %collective-permute-start.23 = (f32[8,128]{1,0:T(8,128)S(1)}, f32[8,128]{1,0:T(8,128)S(1)}, u32[]{:S(2)}, u32[]{:S(2)}) collective-permute-start(f32[8,128]{1,0:T(8,128)S(1)} %get-tuple-element.158), channel_id=1, source_target_pairs={{0,1},{1,0},{2,3},{3,2},{4,5},{5,4},{6,7},{7,6},{8,9},{9,8},{10,11... | collective-permute-start | bytes 12296 | tf_op jit(solution)/shard_map/ppermute | solution.py:830

commit v3 on v2

--- a/solution.py
+++ b/solution.py
@@ -75,6 +75,28 @@
 
 def ahead(value, axis):
     return pltpu.roll(value, 1, axis)
+
+
+def from_above(value, halo):
+    first = rows_of((8, value.shape[1])) == 0
+    fill = jnp.broadcast_to(halo, (8, value.shape[1]))
+    tiles = []
+    for k in range(0, value.shape[0], 8):
+        turned = pltpu.roll(value[k : k + 8], 1, 0)
+        tiles.append(jnp.where(first, fill, turned))
+        fill = turned
+    return jnp.concatenate(tiles, axis=0)
+
+
+def from_below(value, halo):
+    last = rows_of((8, value.shape[1])) == 7
+    fill = jnp.broadcast_to(halo, (8, value.shape[1]))
+    tiles = []
+    for k in range(value.shape[0] - 8, -1, -8):
+        turned = pltpu.roll(value[k : k + 8], 7, 0)
+        tiles.append(jnp.where(last, fill, turned))
+        fill = turned
+    return jnp.concatenate(tiles[::-1], axis=0)
 
 
 class Plan:
@@ -226,7 +248,7 @@
         pack_y(plan, ref, ya.at[k], yb.at[k])
 
 
-def inner_kernel(plan, press, mob, source, compress, well, res, tx, ty, tz, diag):
+def inner_kernel(plan, press, mob, frac, source, compress, well, res, tx, ty, tz, diag, *comps):
     shape = (plan.ny, plan.nz)
     row, lane = rows_of(shape), lanes_of(shape)
 
@@ -246,14 +268,23 @@
         diag[i] = d
         r = source[i] - d * p + flux_x + (flux_y - back(flux_y, 0)) + (flux_z - back(flux_z, 1))
         res[jnp.maximum(i - 1, 0)] = r_last - flux_x
+        for q, comp in zip(plan.z_msgs, comps):
+            lead = plan.high("gz", q)[0].astype(jnp.int32) + INTERSECTION
+            mix = jnp.where(
+                lane <= INTERSECTION, pltpu.roll(p, lead, 1), pltpu.roll(m, lead + 1, 1)
+            )
+            comp[pl.ds(i * plan.ny, plan.ny), :] = jnp.where(
+                lane <= INTERSECTION + 1, mix, pltpu.roll(frac[i], lead + 2, 1)
+            )
         return p, m, r
 
     zero = jnp.zeros(shape, F32)
     res[plan.nx - 1] = lax.fori_loop(0, plan.nx, layer, (zero, zero, zero), unroll=4)[2]
 
 
-def rim_kernel(plan, res_in, press, mob, frac, xa, xb, ya, yb, res, *rest):
-    z_outs, comp = rest[:-1], rest[-1]
+def rim_kernel(plan, res_in, press, mob, xa, xb, ya, yb, *rest):
+    n_msg = len(plan.z_msgs)
+    comps, res, z_outs = rest[:n_msg], rest[n_msg], rest[n_msg + 1 :]
     nx, ny, nz = plan.nx, plan.ny, plan.nz
     last = nx - 1
     for high, k in ((False, 0), (True, last)):
@@ -262,22 +293,16 @@
     for high, k in ((False, 0), (True, ny - 1)):
         p, m = (side(plan, "gy", ya[f], yb[f], high) for f in (0, 1))
         res[:, k, :] = res[:, k, :] + harmonic(mob[:, k, :], m) * (p - press[:, k, :])
-    lane = lanes_of((ny, nz))
     wide = INTERSECTION
-    for q, out in zip(plan.z_msgs, z_outs):
+    group = 128 // ny
+    for q, out, comp in zip(plan.z_msgs, z_outs, comps):
         up = plan.high("gz", q)[0].astype(jnp.int32)
-
-        def layer(i, carry):
-            acc = pltpu.roll(res[i], up * wide, 1)
-            for k, ref in enumerate((press, mob, frac)):
-                acc = jnp.where(lane < wide + k, acc, pltpu.roll(ref[i], wide + k + up, 1))
-            comp[pl.ds(i * ny, ny), :] = acc
-            return carry
-
-        lax.fori_loop(0, nx, layer, 0, unroll=4)
-        for k in range(nx * ny // 128):
+        lane = lanes_of((128, nz))
+        for k in range(nx // group):
             cut = slice(k * 128, (k + 1) * 128)
-            out[:, cut] = jnp.transpose(comp[cut, :])[:MSG_ROWS, :]
+            value = pltpu.roll(res[k * group : (k + 1) * group].reshape(128, nz), up * wide, 1)
+            value = jnp.where(lane < wide, value, comp[cut, :])
+            out[:, cut] = jnp.transpose(value)[:MSG_ROWS, :]
 
 
 def z_flux(sent, got):
@@ -329,7 +354,7 @@
 
 def faces_xy_kernel(
     plan, mob, press, sat, coef, poro, well, tx_in, ty_in, xa, xb, ya, yb,
-    tx, ty_low, ty_top, gx, gy_low, gy_top, hx, hy, rate, inject, square, pull, push, ty_rim,
+    tx, ty_low, ty_top, gx, gy_low, gy_top, hx, hy, rate, inject, anchor, square, pull, push, ty_rim,
 ):
     nx, ny, nz = plan.nx, plan.ny, plan.nz
     for k, high in ((0, False), (1, True)):
@@ -362,7 +387,9 @@
         den = s * s + part * rest
         den = den * den
         rate[i] = speed
-        inject[i] = INJECT_RATE * well[i].astype(F32)
+        gain = INJECT_RATE * well[i].astype(F32)
+        inject[i] = gain
+        anchor[i] = speed * s + gain
         square[i] = den
         pull[i] = speed * den
         push[i] = jnp.abs(2.0 * part * s)
@@ -455,7 +482,7 @@
         edge[i] = y_modes(plan, spec, ya, yb, basis, jnp.where(i < wide, i, nx - 2 * wide + i))
         return carry
 
-    lax.fori_loop(0, 2 * wide, layer, 0, unroll=4)
+    lax.fori_loop(0, 2 * wide, layer, 0, unroll=16)
     low = jnp.zeros(edge.shape[1:], F32)
     top = low
     for k in range(wide):
@@ -473,7 +500,7 @@
         zed[i] = y_modes(plan, spec, ya, yb, basis, i)
         return carry
 
-    lax.fori_loop(wide, nx - wide, layer, 0, unroll=4)
+    lax.fori_loop(wide, nx - wide, layer, 0, unroll=8)
 
     def outer(k, carry):
         low, top = carry
@@ -529,7 +556,7 @@
         put(nx - 1 - i, top)
         return low, top
 
-    lax.fori_loop(0, half - 1, outward, (low, top), unroll=3)
+    lax.fori_loop(0, half - 1, outward, (low, top), unroll=15)
     mean = jnp.sum(jnp.sum(total[...], axis=0, keepdims=True), axis=1, keepdims=True) / (
         nx * ny * nz
     )
@@ -547,7 +574,7 @@
             tile[q] = jnp.where(lanes_of((128, nz)) == r, moved, tile[q])
         return carry
 
-    lax.fori_loop(0, nx // group, lift, 0, unroll=2)
+    lax.fori_loop(0, nx // group, lift, 0, unroll=8)
     pack_x(plan, direction, dxa, dxb)
     pack_y(plan, direction, dya, dyb)
     tile_out(plan, tile, z_outs)
@@ -564,16 +591,16 @@
     spread(plan, got, hz)
     hy[0] = side(plan, "gy", ya[...], yb[...], False)
     hy[1] = side(plan, "gy", ya[...], yb[...], True)
-    row, lane = rows_of((ny, nz)), lanes_of((ny, nz))
+    lane = lanes_of((ny, nz))
 
     def layer(i, carry):
         d_last, im_last, rd, da = carry
         d = direction[i]
         flux = tx[i] * (d_last - d)
         gx[i] = flux
+        y_last = from_above(d, hy[0, pl.ds(i, 1), :])
+        y_next = from_below(d, hy[1, pl.ds(i, 1), :])
         cells = pl.ds(i * ny, ny)
-        y_last = jnp.where(row == 0, hy[0, pl.ds(i, 1), :], ahead(d, 0))
-        y_next = jnp.where(row == ny - 1, hy[1, pl.ds(i, 1), :], back(d, 0))
         z_last = jnp.where(lane == 0, hz[0][cells, :], ahead(d, 1))
         z_next = jnp.where(lane == nz - 1, hz[-1][cells, :], back(d, 1))
         im = diag[i] * d - flux
@@ -594,7 +621,7 @@
     zero = jnp.zeros((ny, nz), F32)
     low = side(plan, "gx", xa[...], xb[...], False)
     top = side(plan, "gx", xa[...], xb[...], True)
-    d, im, rd, da = lax.fori_loop(0, nx, layer, (low, zero, zero, zero), unroll=4)
+    d, im, rd, da = lax.fori_loop(0, nx, layer, (low, zero, zero, zero), unroll=16)
     flux = tx[nx] * (d - top)
     gx[nx] = flux
     im = im + flux
@@ -610,16 +637,16 @@
 
 def sweep(plan, refs, x_low, x_top, hy, z_at, done):
     nx, ny, nz = plan.nx, plan.ny, plan.nz
-    (start, now, frac, coef, rate, inject, gx, gy_low, gy_top, gz_low, gz_top, outflow) = refs
-    row, lane = rows_of((ny, nz)), lanes_of((ny, nz))
+    (now, frac, coef, rate, anchor, gx, gy_low, gy_top, gz_low, gz_top, outflow) = refs
+    lane = lanes_of((ny, nz))
 
     def layer(i, carry):
         f, flow = carry
         f_next = jnp.where(i == nx - 1, x_top, frac[jnp.minimum(i + 1, nx - 1)])
         s, c = now[i], coef[i]
         flow_next = upwind(gx[i + 1], f, f_next)
-        y_last = jnp.where(row == 0, hy[0, pl.ds(i, 1), :], ahead(f, 0))
-        y_next = jnp.where(row == ny - 1, hy[1, pl.ds(i, 1), :], back(f, 0))
+        y_last = from_above(f, hy[0, pl.ds(i, 1), :])
+        y_next = from_below(f, hy[1, pl.ds(i, 1), :])
         z_low, z_top = z_at(i)
         z_last = jnp.where(lane == 0, z_low, ahead(f, 1))
         z_next = jnp.where(lane == nz - 1, z_top, back(f, 1))
@@ -627,19 +654,18 @@
             (flow_next - flow)
             + (upwind(gy_top[i], f, y_next) - upwind(gy_low[i], y_last, f))
             + (upwind(gz_top[i], f, z_next) - upwind(gz_low[i], z_last, f))
-            + (rate[i] * (s - start[i]) - inject[i])
+            + (rate[i] * s - anchor[i])
         )
         rest = 1.0 - s
         part = c * rest
         den = s * s + part * rest
         square = den * den
-        slope = 2.0 * part * s
-        s = s - bal * square / (rate[i] * square + outflow[i] * jnp.abs(slope))
+        s = s - bal * square / (rate[i] * square + outflow[i] * jnp.abs(part * s))
         done(i, s, c)
         return f_next, flow_next
 
     f0 = frac[0]
-    lax.fori_loop(0, nx, layer, (f0, upwind(gx[0], x_low, f0)), unroll=4)
+    lax.fori_loop(0, nx, layer, (f0, upwind(gx[0], x_low, f0)), unroll=16)
 
 
 def keep(plan, new, new_frac, tile):
@@ -710,7 +736,7 @@
     tile = outs[-1]
     nx, ny, nz = plan.nx, plan.ny, plan.nz
     step = step_of(sums)
-    row, lane = rows_of((ny, nz)), lanes_of((ny, nz))
+    lane = lanes_of((ny, nz))
     done = keep(plan, s_new, f_new, tile)
 
     def flux(k, i):
@@ -725,8 +751,8 @@
         out = jnp.maximum(g_next, 0.0) - jnp.minimum(g, 0.0)
         bal = flow_next - flow - inject[i]
         cells = pl.ds(i * ny, ny)
-        y_last = jnp.where(row == 0, hy[0, 1, pl.ds(i, 1), :], ahead(f, 0))
-        y_next = jnp.where(row == ny - 1, hy[1, 1, pl.ds(i, 1), :], back(f, 0))
+        y_last = from_above(f, hy[0, 1, pl.ds(i, 1), :])
+        y_next = from_below(f, hy[1, 1, pl.ds(i, 1), :])
         z_last = jnp.where(lane == 0, fz[0][cells, :], ahead(f, 1))
         z_next = jnp.where(lane == nz - 1, fz[-1][cells, :], back(f, 1))
         for k, ref, other, low in (
@@ -743,22 +769,22 @@
             else:
                 out = out + jnp.maximum(value, 0.0)
                 bal = bal + upwind(value, f, other)
-        outflow[i] = out
+        outflow[i] = out + out
         done(i, sat[i] - bal * square[i] / (pull[i] + out * push[i]), coef[i])
         return f_next, g_next, flow_next
 
     f0, g0 = frac[0], flux(0, 0)
     gx[0] = g0
-    lax.fori_loop(0, nx, layer, (f0, g0, upwind(g0, hx[0, 1], f0)), unroll=4)
+    lax.fori_loop(0, nx, layer, (f0, g0, upwind(g0, hx[0, 1], f0)), unroll=16)
     pack_all(plan, f_new, tile, packs)
 
 
 def later_kernel(plan, last_sweep, *refs):
     n_msg = len(plan.z_msgs)
-    fields = refs[:12]
-    xa, xb, ya, yb = refs[12:16]
-    got = refs[16 : 16 + n_msg]
-    rest = refs[17 + n_msg :]
+    fields = refs[:11]
+    xa, xb, ya, yb = refs[11:15]
+    got = refs[15 : 15 + n_msg]
+    rest = refs[16 + n_msg :]
     if last_sweep:
         out, new, sem, fh, *hz = rest
 
@@ -770,13 +796,12 @@
         packs = rest[2 : 6 + n_msg]
         tile, fh, *hz = rest[6 + n_msg :]
         done = keep(plan, new, new_frac, tile)
-    ny = plan.ny
     spread(plan, got, hz)
     fh[0] = side(plan, "gy", ya[...], yb[...], False)
     fh[1] = side(plan, "gy", ya[...], yb[...], True)
 
     def z_at(i):
-        cells = pl.ds(i * ny, ny)
+        cells = pl.ds(i * plan.ny, plan.ny)
         return hz[0][cells, :], hz[-1][cells, :]
 
     sweep(
@@ -858,23 +883,22 @@
     )
     ya, yb = swap("gy", ya, yb)
     xa, xb = swap("gx", xa, xb)
-    res, tx, ty, tz, diag = call(
+    res, tx, ty, tz, diag, *comps = call(
         functools.partial(inner_kernel, plan),
-        [full_shape] * 5,
-        (press, mob, source, compress, well_mask),
+        [full_shape] * 5 + [(cells, nz)] * n_msg,
+        (press, mob, frac, source, compress, well_mask),
     )
     res, *sent = call(
         functools.partial(rim_kernel, plan),
         [full_shape] + [(MSG_ROWS, cells)] * n_msg,
-        (res, press, mob, frac, xa, xb, ya, yb),
-        scratch=[(cells, nz)],
+        (res, press, mob, xa, xb, ya, yb, *comps),
         aliases={0: 0},
     )
     got = swap_z(sent)
-    tx, ty_low, ty_top, gx, gy_low, gy_top, hx, hy, rate, inject, square, pull, push = call(
+    tx, ty_low, ty_top, gx, gy_low, gy_top, hx, hy, rate, inject, anchor, square, pull, push = call(
         functools.partial(faces_xy_kernel, plan),
         [(nx + 1, ny, nz)] + [full_shape] * 2 + [(nx + 1, ny, nz)] + [full_shape] * 2
-        + [(2, 2) + x_face, (2, 2) + y_face] + [full_shape] * 5,
+        + [(2, 2) + x_face, (2, 2) + y_face] + [full_shape] * 6,
         (mob, press, sat, coef, porosity, well_mask, tx, ty, xa, xb, ya, yb),
         scratch=[(2,) + y_face],
     )
@@ -939,7 +963,7 @@
         outs = call(
             functools.partial(later_kernel, plan, last_sweep),
             [full_shape] if last_sweep else [full_shape] * 2 + face_shapes,
-            (sat, current, frac, coef, rate, inject, *flows, *halo, token),
+            (current, frac, coef, rate, anchor, *flows, *halo, token),
             scratch=([full_shape, dma((CHUNKS,))] if last_sweep else [tile])
             + [(2,) + y_face] + spreads,
             hbm_out=(0,) if last_sweep else (),

time: 74.7 us -> 69.9 us (0.936)
  Pallas kernels: 24.6 us -> 19.7 us
    pallas_call x14, Pallas kernels: 24.6 us -> 19.7 us  [call(): pl.pallas_call(kernel, out_shape=[jax.ShapeDtypeStruct(s, F32) for s in o...]
where the time goes in v3:
time: 69.9 us; the launch traced here: 69.7 us
  starting transfers between devices  26.2 us (37%)
  Pallas kernels  19.7 us (28%)
  waiting for transfers between devices  12.7 us (18%)
  blocking collectives  10.1 us (14%)
  between operations  0.88 us (1%)
    ppermute x24, starting transfers between devices, send(): return lax.ppermute(value, axis, plan.perm(axis, which))  26.2 us
    pallas_call x14, Pallas kernels, call(): pl.pallas_call(kernel, out_shape=[jax.ShapeDtypeStruct(s, F32) for s in o...  19.7 us
    ppermute x24, waiting for transfers between devices, send(): return lax.ppermute(value, axis, plan.perm(axis, which))  12.7 us
    all_to_all x1, blocking collectives, per_device(): sums = lax.all_to_all(sums, AXES, 0, 0, tiled=True)  10.1 us
  transfers between devices with their start and end apart: 24, of which 8 were waited for; matrix products, arithmetic and copies ran while one was open for 0% of the time, Pallas kernels for 12%

profile of v3, /device:TPU:0, one launch (start us, length us, event | category | flops | bytes accessed | tf_op | source)
XLA Modules:
  0.0 69.7 jit_solution(1304917760588167971)
XLA Ops:
  0.7 2.0 %shard_map.202 = (f32[32,32,128]{2,1,0:T(8,128)S(1)}, f32[32,32,128]{2,1,0:T(8,128)S(1)}, f32[32,32,128]{2,1,0:T(8,128)S(1)}, f32[32,32,128]{2,1,0:T(8,128)S(1)}...) custom-call(f32[32,32,128]{2,1,0:T(8,128)} %press_in.1, ...), custom_call_target="tpu_custom_call" | custom-call | tf_op jit(solution)/shard_map/pallas_call | solution.py:126
  2.7 3.1 %collective-permute-start = (f32[3,32,128]{2,1,0:T(8,128)S(1)}, f32[3,32,128]{2,1,0:T(8,128)S(1)}, u32[]{:S(2)}, u32[]{:S(2)}) collective-permute-start(f32[3,32,128]{2,1,0:T(8,128)S(1)} %get-tuple-element.87), channel_id=1, source_target_pairs={{0,8},{8,0},{16,24},{24,16},{1,9},{9,1},{17,25},{25,17},{2,10},{10... | collective-permute-start | bytes 147464 | tf_op jit(solution)/shard_map/ppermute | solution.py:855
  5.8 2.5 %collective-permute-start.1 = (f32[3,32,128]{2,1,0:T(8,128)S(1)}, f32[3,32,128]{2,1,0:T(8,128)S(1)}, u32[]{:S(2)}, u32[]{:S(2)}) collective-permute-start(f32[3,32,128]{2,1,0:T(8,128)S(1)} %get-tuple-element.88), channel_id=1, source_target_pairs={{8,16},{16,8},{24,0},{0,24},{9,17},{17,9},{25,1},{1,25},{10,18},{1... | collective-permute-start | bytes 147464 | tf_op jit(solution)/shard_map/ppermute | solution.py:855
  8.3 0.0 collective-permute-start.2
  8.3 1.6 %collective-permute-start.3 = (f32[3,32,128]{2,1,0:T(8,128)S(1)}, f32[3,32,128]{2,1,0:T(8,128)S(1)}, u32[]{:S(2)}, u32[]{:S(2)}) collective-permute-start(f32[3,32,128]{2,1,0:T(8,128)S(1)} %get-tuple-element.90), channel_id=1, source_target_pairs={{2,4},{4,2},{6,0},{0,6},{3,5},{5,3},{7,1},{1,7},{10,12},{12,10},{1... | collective-permute-start | bytes 147464 | tf_op jit(solution)/shard_map/ppermute | solution.py:855
  9.9 1.7 %shard_map.203 = (f32[32,32,128]{2,1,0:T(8,128)S(1)}, f32[32,32,128]{2,1,0:T(8,128)S(1)}, f32[32,32,128]{2,1,0:T(8,128)S(1)}, f32[32,32,128]{2,1,0:T(8,128)S(1)}...) custom-call(f32[32,32,128]{2,1,0:T(8,128)S(1)} %get-tuple-element.83.press, ...), custom_call_target="tpu_custom_call" | custom-call | tf_op jit(solution)/shard_map/pallas_call | solution.py:126
  11.6 0.0 copy-start.3
  11.6 0.0 collective-permute-done.xa
  11.6 0.1 collective-permute-done.1.xb
  11.7 0.0 collective-permute-done.2.ya
  11.7 0.1 collective-permute-done.3.yb
  11.8 0.4 shard_map.204
  12.2 1.6 %collective-permute-start.4 = (f32[16,1024]{1,0:T(8,128)S(1)}, f32[16,1024]{1,0:T(8,128)S(1)}, u32[]{:S(2)}, u32[]{:S(2)}) collective-permute-start(f32[16,1024]{1,0:T(8,128)S(1)} %get-tuple-element.98.rest_0_), channel_id=1, source_target_pairs={{0,1},{1,0},{2,3},{3,2},{4,5},{5,4},{6,7},{7,6},{8,9},{9,8},{10,11... | collective-permute-start | bytes 196616 | tf_op jit(solution)/shard_map/ppermute | solution.py:855
  13.8 0.7 shard_map.205
  14.4 0.0 copy-start
  14.5 0.0 copy-start.7
  14.5 2.3 %collective-permute-done.4.rest_1_ = f32[16,1024]{1,0:T(8,128)S(1)} collective-permute-done((f32[16,1024]{1,0:T(8,128)S(1)}, f32[16,1024]{1,0:T(8,128)S(1)}, u32[]{:S(2)}, u32[]{:S(2)}) %collective-permute-start.4) | collective-permute-done | bytes 65568 | tf_op jit(solution)/shard_map/ppermute | solution.py:855
  16.8 0.8 %shard_map.206 = (f32[32,32,144]{2,1,0:T(8,128)S(1)}, f32[36,8,128]{2,1,0:T(8,128)S(1)}, f32[36,8,128]{2,1,0:T(8,128)S(1)}) custom-call(f32[32,32,128]{2,1,0:T(8,128)S(1)} %get-tuple-element.92.res, bf16[384,144]{1,0:T(8,128)(2,1)S(1)} %copy-done.6, f32[48,144]{1,0:T(8,128)S(1)} %copy-done.10, f32[48,144]{1,0:T(8,128)S(1)} %copy-done.11, ...), custom_call_target="tpu_custom_call" | custom-call | tf_op jit(solution)/shard_map/pallas_call | solution.py:126
  17.5 0.1 collective-permute-start.5
  17.6 1.6 %collective-permute-start.6 = (f32[36,8,128]{2,1,0:T(8,128)S(1)}, f32[36,8,128]{2,1,0:T(8,128)S(1)}, u32[]{:S(2)}, u32[]{:S(2)}) collective-permute-start(f32[36,8,128]{2,1,0:T(8,128)S(1)} %get-tuple-element.101), channel_id=1, source_target_pairs={{2,4},{4,2},{6,0},{0,6},{3,5},{5,3},{7,1},{1,7},{10,12},{12,10},{1... | collective-permute-start | bytes 442376 | tf_op jit(solution)/shard_map/ppermute | solution.py:855
  19.2 4.1 %shard_map.207 = (f32[32,32,128]{2,1,0:T(8,128)S(1)}, f32[32,32,128]{2,1,0:T(8,128)S(1)}, f32[32,32,128]{2,1,0:T(8,128)S(1)}, f32[32,32,128]{2,1,0:T(8,128)S(1)}...) custom-call(f32[32,32,128]{2,1,0:T(8,128)S(1)} %get-tuple-element.92.res, ...), custom_call_target="tpu_custom_call" | custom-call | tf_op jit(solution)/shard_map/pallas_call | solution.py:126
  23.3 0.0 collective-permute-done.5.ya
  23.3 0.0 collective-permute-done.6.yb
  23.3 0.5 shard_map.208
  23.8 0.7 %collective-permute-start.7 = (f32[56,128]{1,0:T(8,128)S(1)}, f32[56,128]{1,0:T(8,128)S(1)}, u32[]{:S(2)}, u32[]{:S(2)}) collective-permute-start(f32[56,128]{1,0:T(8,128)S(1)} %get-tuple-element.105), channel_id=1, source_target_pairs={{0,8},{8,0},{16,24},{24,16},{1,9},{9,1},{17,25},{25,17},{2,10},{10... | collective-permute-start | bytes 86024 | tf_op jit(solution)/shard_map/ppermute | solution.py:855
  24.5 1.5 %collective-permute-start.8 = (f32[56,128]{1,0:T(8,128)S(1)}, f32[56,128]{1,0:T(8,128)S(1)}, u32[]{:S(2)}, u32[]{:S(2)}) collective-permute-start(f32[56,128]{1,0:T(8,128)S(1)} %get-tuple-element.106), channel_id=1, source_target_pairs={{8,16},{16,8},{24,0},{0,24},{9,17},{17,9},{25,1},{1,25},{10,18},{1... | collective-permute-start | bytes 86024 | tf_op jit(solution)/shard_map/ppermute | solution.py:855
  26.0 0.8 %shard_map.209.zed = f32[32,48,144]{2,1,0:T(8,128)S(1)} custom-call(f32[32,32,144]{2,1,0:T(8,128)S(1)} %get-tuple-element.99.spec, f32[36,8,128]{2,1,0:T(8,128)S(1)} %collective-permute-done.5.ya, f32[36,8,128]{2,1,0:T(8,128)S(1)} %collective-permute-done.6.yb, bf16[48,144]{1,0:T(8,128)(2,1)S(1)} %copy-done.7, f32[24,48,144]{2,1,0:T(8,128)S(1)} %copy-done, ...), custom_call_target="tpu_custom_call" | custom-call | tf_op jit(solution)/shard_map/pallas_call | solution.py:126
  26.9 0.8 %collective-permute-done.7.xa = f32[56,128]{1,0:T(8,128)S(1)} collective-permute-done((f32[56,128]{1,0:T(8,128)S(1)}, f32[56,128]{1,0:T(8,128)S(1)}, u32[]{:S(2)}, u32[]{:S(2)}) %collective-permute-start.7) | collective-permute-done | bytes 28704 | tf_op jit(solution)/shard_map/ppermute | solution.py:855
  27.7 2.5 %collective-permute-done.8.xb = f32[56,128]{1,0:T(8,128)S(1)} collective-permute-done((f32[56,128]{1,0:T(8,128)S(1)}, f32[56,128]{1,0:T(8,128)S(1)}, u32[]{:S(2)}, u32[]{:S(2)}) %collective-permute-start.8) | collective-permute-done | bytes 28704 | tf_op jit(solution)/shard_map/ppermute | solution.py:855
  30.2 1.4 %shard_map.210 = (f32[32,32,128]{2,1,0:T(8,128)S(1)}, f32[32,128]{1,0:T(8,128)S(1)}, f32[32,128]{1,0:T(8,128)S(1)}, f32[32,128]{1,0:T(8,128)S(1)}, f32[32,128]{1,0:T(8,128)S(1)}, /*index=5*/f32[8,128]{1,0:T(8,128)S(1)}) custom-call(f32[32,48,144]{2,1,0:T(8,128)S(1)} %shard_map.209.zed, f32[56,128]{1,0:T(8,128)S(1)} %collective-permute-done.7.xa, ...), custom_call_target="tpu_custom_call" | custom-call | tf_op jit(solution)/shard_map/pallas_call | solution.py:126
  31.6 0.0 collective-permute-start.9
  31.7 1.8 %collective-permute-start.10 = (f32[32,128]{1,0:T(8,128)S(1)}, f32[32,128]{1,0:T(8,128)S(1)}, u32[]{:S(2)}, u32[]{:S(2)}) collective-permute-start(f32[32,128]{1,0:T(8,128)S(1)} %get-tuple-element.117), channel_id=1, source_target_pairs={{8,16},{16,8},{24,0},{0,24},{9,17},{17,9},{25,1},{1,25},{10,18},{1... | collective-permute-start | bytes 49160 | tf_op jit(solution)/shard_map/ppermute | solution.py:855
  33.4 0.0 collective-permute-start.11
  33.4 1.9 %collective-permute-start.12 = (f32[32,128]{1,0:T(8,128)S(1)}, f32[32,128]{1,0:T(8,128)S(1)}, u32[]{:S(2)}, u32[]{:S(2)}) collective-permute-start(f32[32,128]{1,0:T(8,128)S(1)} %get-tuple-element.119), channel_id=1, source_target_pairs={{2,4},{4,2},{6,0},{0,6},{3,5},{5,3},{7,1},{1,7},{10,12},{12,10},{1... | collective-permute-start | bytes 49160 | tf_op jit(solution)/shard_map/ppermute | solution.py:855
  35.3 1.5 %collective-permute-start.13 = (f32[8,128]{1,0:T(8,128)S(1)}, f32[8,128]{1,0:T(8,128)S(1)}, u32[]{:S(2)}, u32[]{:S(2)}) collective-permute-start(f32[8,128]{1,0:T(8,128)S(1)} %get-tuple-element.120), channel_id=1, source_target_pairs={{0,1},{1,0},{2,3},{3,2},{4,5},{5,4},{6,7},{7,6},{8,9},{9,8},{10,11... | collective-permute-start | bytes 12296 | tf_op jit(solution)/shard_map/ppermute | solution.py:855
  36.9 2.1 %collective-permute-done.13.rest_0_ = f32[8,128]{1,0:T(8,128)S(1)} collective-permute-done((f32[8,128]{1,0:T(8,128)S(1)}, f32[8,128]{1,0:T(8,128)S(1)}, u32[]{:S(2)}, u32[]{:S(2)}) %collective-permute-start.13) | collective-permute-done | bytes 4128 | tf_op jit(solution)/shard_map/ppermute | solution.py:855
  38.9 0.0 collective-permute-done.9.xa
  38.9 0.0 collective-permute-done.10.xb
  39.0 0.0 collective-permute-done.11.ya
  39.0 0.0 collective-permute-done.12.yb
  39.0 1.0 %shard_map.211 = (f32[32,32,128]{2,1,0:T(8,128)S(1)}, f32[32,128]{1,0:T(8,128)S(1)}, f32[33,32,128]{2,1,0:T(8,128)S(1)}, f32[32,32,128]{2,1,0:T(8,128)S(1)}, f32...) custom-call(f32[32,32,128]{2,1,0:T(8,128)S(1)} %get-tuple-element.108.direction, ...), custom_call_target="tpu_custom_call" | custom-call | tf_op jit(solution)/shard_map/pallas_call | solution.py:126
  40.0 10.1 %all_to_all.11 = f32[32,1,128]{2,1,0:T(1,128)S(1)} all-to-all(f32[32,1,128]{2,1,0:T(1,128)S(1)} %bitcast.6), channel_id=1, replica_groups=mesh['gx'=4,'gy'=4,'gz'=2] {'gx','gy','gz'}, dimensions={0} | all-to-all | bytes 32768 | tf_op jit(solution)/shard_map/all_to_all | solution.py:942
  50.1 1.6 %shard_map.213 = (f32[32,32,128]{2,1,0:T(8,128)S(1)}, f32[32,32,128]{2,1,0:T(8,128)S(1)}, f32[33,32,128]{2,1,0:T(8,128)S(1)}, f32[32,32,128]{2,1,0:T(8,128)S(1)}...) custom-call(f32[32,128]{1,0:T(8,128)S(1)} %bitcast.4, ...), custom_call_target="tpu_custom_call" | custom-call | tf_op jit(solution)/shard_map/pallas_call | solution.py:126
  51.7 0.5 collective-permute-start.14
  52.2 1.5 %collective-permute-start.15 = (f32[32,128]{1,0:T(8,128)S(1)}, f32[32,128]{1,0:T(8,128)S(1)}, u32[]{:S(2)}, u32[]{:S(2)}) collective-permute-start(f32[32,128]{1,0:T(8,128)S(1)} %get-tuple-element.151), channel_id=1, source_target_pairs={{8,16},{16,8},{24,0},{0,24},{9,17},{17,9},{25,1},{1,25},{10,18},{1... | collective-permute-start | bytes 49160 | tf_op jit(solution)/shard_map/ppermute | solution.py:855
  53.7 0.0 collective-permute-start.16
  53.7 0.7 %collective-permute-start.17 = (f32[32,128]{1,0:T(8,128)S(1)}, f32[32,128]{1,0:T(8,128)S(1)}, u32[]{:S(2)}, u32[]{:S(2)}) collective-permute-start(f32[32,128]{1,0:T(8,128)S(1)} %get-tuple-element.153), channel_id=1, source_target_pairs={{2,4},{4,2},{6,0},{0,6},{3,5},{5,3},{7,1},{1,7},{10,12},{12,10},{1... | collective-permute-start | bytes 49160 | tf_op jit(solution)/shard_map/ppermute | solution.py:855
  54.4 0.5 collective-permute-start.18
  55.0 1.3 %shard_map.212 = (f32[32,32,128]{2,1,0:T(8,128)}, f32[32,32,128]{2,1,0:T(8,128)}, f32[8,128]{1,0:T(8,128)S(1)}) custom-call(f32[32,128]{1,0:T(8,128)S(1)} %bitcast.5, f32[32,32,128]{2,1,0:T(8,128)S(1)} %get-tuple-element.83.press, f32[32,32,128]{2,1,0:T(8,128)S(1)} %get-tuple-element.108.direction, f32[32,32,128]{2,1,0:T(8,128)S(1)} %get-tuple-element.110.full, ...), custom_call_target="tpu_custom_call" | custom-call | tf_op jit(solution)/shard_map/pallas_call | solution.py:126
  56.3 1.8 %collective-permute-done.18.refs_15_ = f32[8,128]{1,0:T(8,128)S(1)} collective-permute-done((f32[8,128]{1,0:T(8,128)S(1)}, f32[8,128]{1,0:T(8,128)S(1)}, u32[]{:S(2)}, u32[]{:S(2)}) %collective-permute-start.18) | collective-permute-done | bytes 4128 | tf_op jit(solution)/shard_map/ppermute | solution.py:855
  58.0 0.0 collective-permute-done.14.refs_11_
  58.0 0.0 collective-permute-done.15.refs_12_
  58.0 0.0 collective-permute-done.16.refs_13_
  58.0 0.0 collective-permute-done.17.refs_14_
  58.0 1.5 %shard_map.214 = (f32[32,32,128]{2,1,0:T(8,128)S(1)}, f32[32,32,128]{2,1,0:T(8,128)S(1)}, f32[32,128]{1,0:T(8,128)S(1)}, f32[32,128]{1,0:T(8,128)S(1)}, f32[32,1...) custom-call(f32[32,32,128]{2,1,0:T(8,128)S(1)} %get-tuple-element.140.refs_0_, ...), custom_call_target="tpu_custom_call" | custom-call | tf_op jit(solution)/shard_map/pallas_call | solution.py:126
  59.6 0.0 collective-permute-start.19
  59.6 2.9 %collective-permute-start.20 = (f32[32,128]{1,0:T(8,128)S(1)}, f32[32,128]{1,0:T(8,128)S(1)}, u32[]{:S(2)}, u32[]{:S(2)}) collective-permute-start(f32[32,128]{1,0:T(8,128)S(1)} %get-tuple-element.159), channel_id=1, source_target_pairs={{8,16},{16,8},{24,0},{0,24},{9,17},{17,9},{25,1},{1,25},{10,18},{1... | collective-permute-start | bytes 49160 | tf_op jit(solution)/shard_map/ppermute | solution.py:855
  62.5 0.0 collective-permute-start.21
  62.5 1.6 %collective-permute-start.22 = (f32[32,128]{1,0:T(8,128)S(1)}, f32[32,128]{1,0:T(8,128)S(1)}, u32[]{:S(2)}, u32[]{:S(2)}) collective-permute-start(f32[32,128]{1,0:T(8,128)S(1)} %get-tuple-element.161), channel_id=1, source_target_pairs={{2,4},{4,2},{6,0},{0,6},{3,5},{5,3},{7,1},{1,7},{10,12},{12,10},{1... | collective-permute-start | bytes 49160 | tf_op jit(solution)/shard_map/ppermute | solution.py:855
  64.2 0.5 collective-permute-start.23
  64.7 3.1 %collective-permute-done.23.refs_15_ = f32[8,128]{1,0:T(8,128)S(1)} collective-permute-done((f32[8,128]{1,0:T(8,128)S(1)}, f32[8,128]{1,0:T(8,128)S(1)}, u32[]{:S(2)}, u32[]{:S(2)}) %collective-permute-start.23) | collective-permute-done | bytes 4128 | tf_op jit(solution)/shard_map/ppermute | solution.py:855
  67.8 0.0 collective-permute-done.19.refs_11_
  67.8 0.0 collective-permute-done.20.refs_12_
  67.8 1.9 %shard_map.215 = f32[32,32,128]{2,1,0:T(8,128)} custom-call(f32[32,32,128]{2,1,0:T(8,128)S(1)} %get-tuple-element.156.refs_0_, f32[32,32,128]{2,1,0:T(8,128)S(1)} %get-tuple-element.157.refs_1_, f32[32,32,128]{2,1,0:T(8,128)S(1)} %get-tuple-element.94.coef.refs_13_.refs_2_, f32[32,32,128]{2,1,0:T(8,128)S(1)} %get-tuple-element.142.refs_3_, ...), custom_call_target="tpu_custom_call" | custom-call | tf_op jit(solution)/shard_map/pallas_call | solution.py:126
  (25 shorter events, 0.0 us)
Async XLA Ops:
  0.6 9.3 %copy-start.4 = (f32[32,32,128]{2,1,0:T(8,128)S(1)}, f32[32,32,128]{2,1,0:T(8,128)}, u32[]{:S(2)}) copy-start(f32[32,32,128]{2,1,0:T(8,128)} %source.1) | copy-start | bytes 1572868
  0.6 9.3 %copy-start.5 = (f32[32,32,128]{2,1,0:T(8,128)S(1)}, f32[32,32,128]{2,1,0:T(8,128)}, u32[]{:S(2)}) copy-start(f32[32,32,128]{2,1,0:T(8,128)} %compress.1) | copy-start | bytes 1572868
  0.7 9.3 %copy-start.1 = (s32[32,32,128]{2,1,0:T(8,128)S(1)}, s32[32,32,128]{2,1,0:T(8,128)}, u32[]{:S(2)}) copy-start(s32[32,32,128]{2,1,0:T(8,128)} %well.3) | copy-start | bytes 1572868
  2.7 8.9 %collective-permute-start = (f32[3,32,128]{2,1,0:T(8,128)S(1)}, f32[3,32,128]{2,1,0:T(8,128)S(1)}, u32[]{:S(2)}, u32[]{:S(2)}) collective-permute-start(f32[3,32,128]{2,1,0:T(8,128)S(1)} %get-tuple-element.87), channel_id=1, source_target_pairs={{0,8},{8,0},{16,24},{24,16},{1,9},{9,1},{17,25},{25,17},{2,10},{10... | collective-permute-start | bytes 147464 | tf_op jit(solution)/shard_map/ppermute | solution.py:855
  5.8 5.9 %collective-permute-start.1 = (f32[3,32,128]{2,1,0:T(8,128)S(1)}, f32[3,32,128]{2,1,0:T(8,128)S(1)}, u32[]{:S(2)}, u32[]{:S(2)}) collective-permute-start(f32[3,32,128]{2,1,0:T(8,128)S(1)} %get-tuple-element.88), channel_id=1, source_target_pairs={{8,16},{16,8},{24,0},{0,24},{9,17},{17,9},{25,1},{1,25},{10,18},{1... | collective-permute-start | bytes 147464 | tf_op jit(solution)/shard_map/ppermute | solution.py:855
  8.3 3.4 %collective-permute-start.2 = (f32[3,32,128]{2,1,0:T(8,128)S(1)}, f32[3,32,128]{2,1,0:T(8,128)S(1)}, u32[]{:S(2)}, u32[]{:S(2)}) collective-permute-start(f32[3,32,128]{2,1,0:T(8,128)S(1)} %get-tuple-element.89), channel_id=1, source_target_pairs={{0,2},{2,0},{4,6},{6,4},{1,3},{3,1},{5,7},{7,5},{8,10},{10,8},{12,... | collective-permute-start | bytes 147464 | tf_op jit(solution)/shard_map/ppermute | solution.py:855
  8.3 3.5 %collective-permute-start.3 = (f32[3,32,128]{2,1,0:T(8,128)S(1)}, f32[3,32,128]{2,1,0:T(8,128)S(1)}, u32[]{:S(2)}, u32[]{:S(2)}) collective-permute-start(f32[3,32,128]{2,1,0:T(8,128)S(1)} %get-tuple-element.90), channel_id=1, source_target_pairs={{2,4},{4,2},{6,0},{0,6},{3,5},{5,3},{7,1},{1,7},{10,12},{12,10},{1... | collective-permute-start | bytes 147464 | tf_op jit(solution)/shard_map/ppermute | solution.py:855
  11.6 2.2 %copy-start.3 = (f32[32,32,128]{2,1,0:T(8,128)S(1)}, f32[32,32,128]{2,1,0:T(8,128)}, u32[]{:S(2)}) copy-start(f32[32,32,128]{2,1,0:T(8,128)} %poro.1) | copy-start | bytes 1572868
  12.2 4.6 %collective-permute-start.4 = (f32[16,1024]{1,0:T(8,128)S(1)}, f32[16,1024]{1,0:T(8,128)S(1)}, u32[]{:S(2)}, u32[]{:S(2)}) collective-permute-start(f32[16,1024]{1,0:T(8,128)S(1)} %get-tuple-element.98.rest_0_), channel_id=1, source_target_pairs={{0,1},{1,0},{2,3},{3,2},{4,5},{5,4},{6,7},{7,6},{8,9},{9,8},{10,11... | collective-permute-start | bytes 196616 | tf_op jit(solution)/shard_map/ppermute | solution.py:855
  13.8 3.0 %copy-start.6 = (bf16[384,144]{1,0:T(8,128)(2,1)S(1)}, bf16[384,144]{1,0:T(8,128)(2,1)}, u32[]{:S(2)}) copy-start(bf16[384,144]{1,0:T(8,128)(2,1)} %constant.23.clone.basis) | copy-start | bytes 331780
  13.8 3.0 %copy-start.10 = (f32[48,144]{1,0:T(8,128)S(1)}, f32[48,144]{1,0:T(8,128)}, u32[]{:S(2)}) copy-start(f32[48,144]{1,0:T(8,128)} %constant.27.rim_low) | copy-start | bytes 82948
  13.8 3.0 %copy-start.11 = (f32[48,144]{1,0:T(8,128)S(1)}, f32[48,144]{1,0:T(8,128)}, u32[]{:S(2)}) copy-start(f32[48,144]{1,0:T(8,128)} %constant.28.rim_top) | copy-start | bytes 82948
  14.4 8.8 %copy-start = (f32[24,48,144]{2,1,0:T(8,128)S(1)}, f32[24,48,144]{2,1,0:T(8,128)}, u32[]{:S(2)}) copy-start(f32[24,48,144]{2,1,0:T(8,128)} %constant.18.clone.factors) | copy-start | bytes 1990660
  14.5 8.8 %copy-start.7 = (bf16[48,144]{1,0:T(8,128)(2,1)S(1)}, bf16[48,144]{1,0:T(8,128)(2,1)}, u32[]{:S(2)}) copy-start(bf16[48,144]{1,0:T(8,128)(2,1)} %constant.24.clone.basis) | copy-start | bytes 41476
  17.5 5.7 %collective-permute-start.5 = (f32[36,8,128]{2,1,0:T(8,128)S(1)}, f32[36,8,128]{2,1,0:T(8,128)S(1)}, u32[]{:S(2)}, u32[]{:S(2)}) collective-permute-start(f32[36,8,128]{2,1,0:T(8,128)S(1)} %get-tuple-element.100), channel_id=1, source_target_pairs={{0,2},{2,0},{4,6},{6,4},{1,3},{3,1},{5,7},{7,5},{8,10},{10,8},{12,... | collective-permute-start | bytes 442376 | tf_op jit(solution)/shard_map/ppermute | solution.py:855
  17.6 5.7 %collective-permute-start.6 = (f32[36,8,128]{2,1,0:T(8,128)S(1)}, f32[36,8,128]{2,1,0:T(8,128)S(1)}, u32[]{:S(2)}, u32[]{:S(2)}) collective-permute-start(f32[36,8,128]{2,1,0:T(8,128)S(1)} %get-tuple-element.101), channel_id=1, source_target_pairs={{2,4},{4,2},{6,0},{0,6},{3,5},{5,3},{7,1},{1,7},{10,12},{12,10},{1... | collective-permute-start | bytes 442376 | tf_op jit(solution)/shard_map/ppermute | solution.py:855
  23.8 3.9 %collective-permute-start.7 = (f32[56,128]{1,0:T(8,128)S(1)}, f32[56,128]{1,0:T(8,128)S(1)}, u32[]{:S(2)}, u32[]{:S(2)}) collective-permute-start(f32[56,128]{1,0:T(8,128)S(1)} %get-tuple-element.105), channel_id=1, source_target_pairs={{0,8},{8,0},{16,24},{24,16},{1,9},{9,1},{17,25},{25,17},{2,10},{10... | collective-permute-start | bytes 86024 | tf_op jit(solution)/shard_map/ppermute | solution.py:855
  24.5 5.7 %collective-permute-start.8 = (f32[56,128]{1,0:T(8,128)S(1)}, f32[56,128]{1,0:T(8,128)S(1)}, u32[]{:S(2)}, u32[]{:S(2)}) collective-permute-start(f32[56,128]{1,0:T(8,128)S(1)} %get-tuple-element.106), channel_id=1, source_target_pairs={{8,16},{16,8},{24,0},{0,24},{9,17},{17,9},{25,1},{1,25},{10,18},{1... | collective-permute-start | bytes 86024 | tf_op jit(solution)/shard_map/ppermute | solution.py:855
  26.0 4.1 %copy-start.2 = (f32[16,48,144]{2,1,0:T(8,128)S(1)}, f32[16,48,144]{2,1,0:T(8,128)}, u32[]{:S(2)}) copy-start(f32[16,48,144]{2,1,0:T(8,128)} %constant.19.clone.reach) | copy-start | bytes 1327108
  26.0 4.1 %copy-start.8 = (bf16[2,144,128]{2,1,0:T(8,128)(2,1)S(1)}, bf16[2,144,128]{2,1,0:T(8,128)(2,1)}, u32[]{:S(2)}) copy-start(bf16[2,144,128]{2,1,0:T(8,128)(2,1)} %constant.26.clone.basis_z) | copy-start | bytes 221188
  26.0 4.1 %copy-start.9 = (f32[48,144]{1,0:T(8,128)S(1)}, f32[48,144]{1,0:T(8,128)}, u32[]{:S(2)}) copy-start(f32[48,144]{1,0:T(8,128)} %constant.20.clone.middle) | copy-start | bytes 82948
  26.0 4.1 %copy-start.12 = (bf16[32,144]{1,0:T(8,128)(2,1)S(1)}, bf16[32,144]{1,0:T(8,128)(2,1)}, u32[]{:S(2)}) copy-start(bf16[32,144]{1,0:T(8,128)(2,1)} %constant.25.clone.basis_y) | copy-start | bytes 27652
  31.6 7.3 %collective-permute-start.9 = (f32[32,128]{1,0:T(8,128)S(1)}, f32[32,128]{1,0:T(8,128)S(1)}, u32[]{:S(2)}, u32[]{:S(2)}) collective-permute-start(f32[32,128]{1,0:T(8,128)S(1)} %get-tuple-element.116), channel_id=1, source_target_pairs={{0,8},{8,0},{16,24},{24,16},{1,9},{9,1},{17,25},{25,17},{2,10},{10... | collective-permute-start | bytes 49160 | tf_op jit(solution)/shard_map/ppermute | solution.py:855
  31.7 7.3 %collective-permute-start.10 = (f32[32,128]{1,0:T(8,128)S(1)}, f32[32,128]{1,0:T(8,128)S(1)}, u32[]{:S(2)}, u32[]{:S(2)}) collective-permute-start(f32[32,128]{1,0:T(8,128)S(1)} %get-tuple-element.117), channel_id=1, source_target_pairs={{8,16},{16,8},{24,0},{0,24},{9,17},{17,9},{25,1},{1,25},{10,18},{1... | collective-permute-start | bytes 49160 | tf_op jit(solution)/shard_map/ppermute | solution.py:855
  33.4 5.5 %collective-permute-start.11 = (f32[32,128]{1,0:T(8,128)S(1)}, f32[32,128]{1,0:T(8,128)S(1)}, u32[]{:S(2)}, u32[]{:S(2)}) collective-permute-start(f32[32,128]{1,0:T(8,128)S(1)} %get-tuple-element.118), channel_id=1, source_target_pairs={{0,2},{2,0},{4,6},{6,4},{1,3},{3,1},{5,7},{7,5},{8,10},{10,8},{12,... | collective-permute-start | bytes 49160 | tf_op jit(solution)/shard_map/ppermute | solution.py:855
  33.4 5.5 %collective-permute-start.12 = (f32[32,128]{1,0:T(8,128)S(1)}, f32[32,128]{1,0:T(8,128)S(1)}, u32[]{:S(2)}, u32[]{:S(2)}) collective-permute-start(f32[32,128]{1,0:T(8,128)S(1)} %get-tuple-element.119), channel_id=1, source_target_pairs={{2,4},{4,2},{6,0},{0,6},{3,5},{5,3},{7,1},{1,7},{10,12},{12,10},{1... | collective-permute-start | bytes 49160 | tf_op jit(solution)/shard_map/ppermute | solution.py:855
  35.3 3.6 %collective-permute-start.13 = (f32[8,128]{1,0:T(8,128)S(1)}, f32[8,128]{1,0:T(8,128)S(1)}, u32[]{:S(2)}, u32[]{:S(2)}) collective-permute-start(f32[8,128]{1,0:T(8,128)S(1)} %get-tuple-element.120), channel_id=1, source_target_pairs={{0,1},{1,0},{2,3},{3,2},{4,5},{5,4},{6,7},{7,6},{8,9},{9,8},{10,11... | collective-permute-start | bytes 12296 | tf_op jit(solution)/shard_map/ppermute | solution.py:855
  51.7 6.3 %collective-permute-start.14 = (f32[32,128]{1,0:T(8,128)S(1)}, f32[32,128]{1,0:T(8,128)S(1)}, u32[]{:S(2)}, u32[]{:S(2)}) collective-permute-start(f32[32,128]{1,0:T(8,128)S(1)} %get-tuple-element.150), channel_id=1, source_target_pairs={{0,8},{8,0},{16,24},{24,16},{1,9},{9,1},{17,25},{25,17},{2,10},{10... | collective-permute-start | bytes 49160 | tf_op jit(solution)/shard_map/ppermute | solution.py:855
  52.2 5.8 %collective-permute-start.15 = (f32[32,128]{1,0:T(8,128)S(1)}, f32[32,128]{1,0:T(8,128)S(1)}, u32[]{:S(2)}, u32[]{:S(2)}) collective-permute-start(f32[32,128]{1,0:T(8,128)S(1)} %get-tuple-element.151), channel_id=1, source_target_pairs={{8,16},{16,8},{24,0},{0,24},{9,17},{17,9},{25,1},{1,25},{10,18},{1... | collective-permute-start | bytes 49160 | tf_op jit(solution)/shard_map/ppermute | solution.py:855
  53.7 4.4 %collective-permute-start.16 = (f32[32,128]{1,0:T(8,128)S(1)}, f32[32,128]{1,0:T(8,128)S(1)}, u32[]{:S(2)}, u32[]{:S(2)}) collective-permute-start(f32[32,128]{1,0:T(8,128)S(1)} %get-tuple-element.152), channel_id=1, source_target_pairs={{0,2},{2,0},{4,6},{6,4},{1,3},{3,1},{5,7},{7,5},{8,10},{10,8},{12,... | collective-permute-start | bytes 49160 | tf_op jit(solution)/shard_map/ppermute | solution.py:855
  53.7 4.4 %collective-permute-start.17 = (f32[32,128]{1,0:T(8,128)S(1)}, f32[32,128]{1,0:T(8,128)S(1)}, u32[]{:S(2)}, u32[]{:S(2)}) collective-permute-start(f32[32,128]{1,0:T(8,128)S(1)} %get-tuple-element.153), channel_id=1, source_target_pairs={{2,4},{4,2},{6,0},{0,6},{3,5},{5,3},{7,1},{1,7},{10,12},{12,10},{1... | collective-permute-start | bytes 49160 | tf_op jit(solution)/shard_map/ppermute | solution.py:855
  54.4 3.6 %collective-permute-start.18 = (f32[8,128]{1,0:T(8,128)S(1)}, f32[8,128]{1,0:T(8,128)S(1)}, u32[]{:S(2)}, u32[]{:S(2)}) collective-permute-start(f32[8,128]{1,0:T(8,128)S(1)} %get-tuple-element.154), channel_id=1, source_target_pairs={{0,1},{1,0},{2,3},{3,2},{4,5},{5,4},{6,7},{7,6},{8,9},{9,8},{10,11... | collective-permute-start | bytes 12296 | tf_op jit(solution)/shard_map/ppermute | solution.py:855
  59.6 8.2 %collective-permute-start.19 = (f32[32,128]{1,0:T(8,128)S(1)}, f32[32,128]{1,0:T(8,128)S(1)}, u32[]{:S(2)}, u32[]{:S(2)}) collective-permute-start(f32[32,128]{1,0:T(8,128)S(1)} %get-tuple-element.158), channel_id=1, source_target_pairs={{0,8},{8,0},{16,24},{24,16},{1,9},{9,1},{17,25},{25,17},{2,10},{10... | collective-permute-start | bytes 49160 | tf_op jit(solution)/shard_map/ppermute | solution.py:855
  59.6 8.1 %collective-permute-start.20 = (f32[32,128]{1,0:T(8,128)S(1)}, f32[32,128]{1,0:T(8,128)S(1)}, u32[]{:S(2)}, u32[]{:S(2)}) collective-permute-start(f32[32,128]{1,0:T(8,128)S(1)} %get-tuple-element.159), channel_id=1, source_target_pairs={{8,16},{16,8},{24,0},{0,24},{9,17},{17,9},{25,1},{1,25},{10,18},{1... | collective-permute-start | bytes 49160 | tf_op jit(solution)/shard_map/ppermute | solution.py:855
  62.5 5.3 %collective-permute-start.21 = (f32[32,128]{1,0:T(8,128)S(1)}, f32[32,128]{1,0:T(8,128)S(1)}, u32[]{:S(2)}, u32[]{:S(2)}) collective-permute-start(f32[32,128]{1,0:T(8,128)S(1)} %get-tuple-element.160), channel_id=1, source_target_pairs={{0,2},{2,0},{4,6},{6,4},{1,3},{3,1},{5,7},{7,5},{8,10},{10,8},{12,... | collective-permute-start | bytes 49160 | tf_op jit(solution)/shard_map/ppermute | solution.py:855
  62.5 5.3 %collective-permute-start.22 = (f32[32,128]{1,0:T(8,128)S(1)}, f32[32,128]{1,0:T(8,128)S(1)}, u32[]{:S(2)}, u32[]{:S(2)}) collective-permute-start(f32[32,128]{1,0:T(8,128)S(1)} %get-tuple-element.161), channel_id=1, source_target_pairs={{2,4},{4,2},{6,0},{0,6},{3,5},{5,3},{7,1},{1,7},{10,12},{12,10},{1... | collective-permute-start | bytes 49160 | tf_op jit(solution)/shard_map/ppermute | solution.py:855
  64.2 3.6 %collective-permute-start.23 = (f32[8,128]{1,0:T(8,128)S(1)}, f32[8,128]{1,0:T(8,128)S(1)}, u32[]{:S(2)}, u32[]{:S(2)}) collective-permute-start(f32[8,128]{1,0:T(8,128)S(1)} %get-tuple-element.162), channel_id=1, source_target_pairs={{0,1},{1,0},{2,3},{3,2},{4,5},{5,4},{6,7},{7,6},{8,9},{9,8},{10,11... | collective-permute-start | bytes 12296 | tf_op jit(solution)/shard_map/ppermute | solution.py:855

commit v4 on v3

--- a/solution.py
+++ b/solution.py
@@ -205,7 +205,7 @@
 
 def mobility_kernel(
     plan, press_in, sat_in, perm_in, rock_in, oil_in,
-    press, sat, mob, coef, frac, xa, xb, ya, yb, total, perm, rock, oil, sem, oil_sem,
+    press, sat, mob, coef, frac, xa, xb, ya, yb, fa, fb, total, perm, rock, oil, sem, oil_sem,
 ):
     kinds = oil.shape[0]
     oil_move = pltpu.make_async_copy(oil_in, oil, oil_sem)
@@ -243,8 +243,10 @@
     total[...] = acc
     for c in range(CHUNKS):
         moves[4 * c + 3].wait()
+    for k, ref in enumerate((press, mob)):
+        pack_x(plan, ref, xa.at[k], xb.at[k])
+    pack_x(plan, frac, fa, fb)
     for k, ref in enumerate((press, mob, frac)):
-        pack_x(plan, ref, xa.at[k], xb.at[k])
         pack_y(plan, ref, ya.at[k], yb.at[k])
 
 
@@ -298,68 +300,82 @@
     for q, out, comp in zip(plan.z_msgs, z_outs, comps):
         up = plan.high("gz", q)[0].astype(jnp.int32)
         lane = lanes_of((128, nz))
-        for k in range(nx // group):
-            cut = slice(k * 128, (k + 1) * 128)
+        blocks = nx // group
+        for k in range(blocks):
             value = pltpu.roll(res[k * group : (k + 1) * group].reshape(128, nz), up * wide, 1)
-            value = jnp.where(lane < wide, value, comp[cut, :])
-            out[:, cut] = jnp.transpose(value)[:MSG_ROWS, :]
+            value = jnp.where(lane < wide, value, comp[k * 128 : (k + 1) * 128, :])
+            turned = jnp.transpose(value)
+            out[k * wide : (k + 1) * wide, :] = turned[:wide]
+            for f in range(3):
+                row = blocks * (wide + f) + k
+                out[row : row + 1, :] = turned[wide + f : wide + f + 1]
 
 
 def z_flux(sent, got):
-    wide = INTERSECTION
     out = []
     for own, other in zip(sent, got):
-        t = harmonic(own[wide + 1 : wide + 2, :], other[wide + 1 : wide + 2, :])
-        q = t * (other[wide : wide + 1, :] - own[wide : wide + 1, :])
-        out.append((other[wide : wide + 1, :], other[wide + 2 : wide + 3, :], t, q))
+        blocks = own.shape[0] // (INTERSECTION + 3)
+        first = blocks * INTERSECTION
+        (p, m), (p_far, m_far, f_far) = (
+            [ref[first + k * blocks : first + (k + 1) * blocks, :] for k in range(count)]
+            for ref, count in ((own, 2), (other, 3))
+        )
+        t = harmonic(m, m_far)
+        out.append((p_far, f_far, t, t * (p_far - p)))
     return out
+
+
+def y_parts(plan):
+    wide, nx = INTERSECTION, plan.nx
+    return (
+        list(range(wide)) + list(range(nx - wide, nx)),
+        list(range(wide, nx - wide)),
+    )
 
 
 def z_kernel(plan, n_msg, res, basis, rim_low, rim_top, order, *rest):
     sent, got = rest[:n_msg], rest[n_msg : 2 * n_msg]
-    spec, ya, yb = rest[2 * n_msg :]
+    spec, *outs = rest[2 * n_msg :]
     nx, ny, nz = plan.nx, plan.ny, plan.nz
     wide = INTERSECTION
-    mixes, rims = [], []
-    for q, other, (_, _, _, flux) in zip(plan.z_msgs, got, z_flux(sent, got)):
-        up = plan.high("gz", q)[1]
-        row = rows_of(other.shape)
-        near = jnp.where(up, 0, wide - 1)
-        flux = jnp.broadcast_to(flux, other.shape)
-        mix = jnp.where(row < wide, other[...], 0.0)
-        mix = jnp.where(row == near, mix - flux, mix)
-        mix = jnp.where(row == wide, flux, mix)
-        top, low = halves(mix)
-        mixes.append(jnp.concatenate([top, low, top], axis=0))
-        rims.append(jnp.where(up, rim_top[...], rim_low[...]).astype(jnp.bfloat16))
+    row = rows_of((wide, 128))
+    fluxes = [part[3] for part in z_flux(sent, got)]
+    ups = [plan.high("gz", q)[1] for q in plan.z_msgs]
+    rims = [jnp.where(up, rim_top[...], rim_low[...]).astype(jnp.bfloat16) for up in ups]
     group = 128 // ny
     for k in range(nx // group):
         value = res[k * group : (k + 1) * group].reshape(128, nz)
         top, low = halves(value)
         out = mxu(jnp.concatenate([top, low, top], axis=1), basis[...])
-        for mix, rim in zip(mixes, rims):
-            out = out + mxu(mix[:, k * 128 : (k + 1) * 128], rim, ((0,), (0,)))
+        for up, other, flux, rim in zip(ups, got, fluxes, rims):
+            flux = jnp.broadcast_to(flux[k : k + 1, :], (wide, 128))
+            mix = other[k * wide : (k + 1) * wide, :]
+            mix = jnp.where(row == jnp.where(up, 0, wide - 1), mix - flux, mix)
+            mix = jnp.concatenate([mix, jnp.where(row == 0, flux, 0.0)], axis=0)
+            out = out + mxu(thrice(mix), rim, ((0,), (0,)))
         spec[k * group : (k + 1) * group] = out.reshape(group, ny, out.shape[1])
     tail = 2 * wide
     per = 128 // tail
-    for which, ref in ((0, ya), (1, yb)):
+    for which in (0, 1):
         start = jnp.where(plan.high("gy", which)[0], ny - wide, 0)
         rows = pl.ds(pl.multiple_of(start, 8), wide)
-        ref[:nx] = spec[:, rows, :nz]
-        for g in range(nx // per):
-            ref[nx + g] = jnp.concatenate(
-                [spec[g * per + j, rows, nz:] for j in range(per)], axis=1
-            )
+        for layers, ref in zip(y_parts(plan), outs[which::2]):
+            count = len(layers)
+            for g in range(count // per):
+                group = layers[g * per : (g + 1) * per]
+                for j, i in enumerate(group):
+                    ref[g * per + j] = spec[i, rows, :nz]
+                ref[count + g] = jnp.concatenate([spec[i, rows, nz:] for i in group], axis=1)
 
 
 def faces_xy_kernel(
     plan, mob, press, sat, coef, poro, well, tx_in, ty_in, xa, xb, ya, yb,
-    tx, ty_low, ty_top, gx, gy_low, gy_top, hx, hy, rate, inject, anchor, square, pull, push, ty_rim,
+    tx, ty_low, ty_top, gx, gy_low, gy_top, hy, rate, inject, anchor, square, pull, push, ty_rim,
 ):
     nx, ny, nz = plan.nx, plan.ny, plan.nz
+    x_low, x_top = (side(plan, "gx", xa[0], xb[0], high) for high in (False, True))
     for k, high in ((0, False), (1, True)):
         for f, field in ((0, 0), (1, 2)):
-            hx[k, f] = side(plan, "gx", xa[field], xb[field], high)
             hy[k, f] = side(plan, "gy", ya[field], yb[field], high)
     ty_rim[0] = harmonic(mob[:, 0, :], side(plan, "gy", ya[1], yb[1], False))
     ty_rim[1] = harmonic(mob[:, ny - 1, :], side(plan, "gy", ya[1], yb[1], True))
@@ -395,54 +411,77 @@
         push[i] = jnp.abs(2.0 * part * s)
         return p
 
-    p = lax.fori_loop(0, nx, layer, hx[0, 0], unroll=4)
+    p = lax.fori_loop(0, nx, layer, x_low, unroll=4)
     t = harmonic(mob[nx - 1], side(plan, "gx", xa[1], xb[1], True))
     tx[nx] = t
-    gx[nx] = t * (p - hx[1, 0])
-
-
-def faces_z_kernel(plan, n_msg, res, press, tz_in, *rest):
+    gx[nx] = t * (p - x_top)
+
+
+def z_ends(plan, n_msg):
+    lane = lanes_of((plan.ny, plan.nz))
+    low, top = lane == 0, lane == plan.nz - 1
+    if n_msg == 1:
+        up = plan.high("gz", plan.z_msgs[0])[1]
+        low, top = low & jnp.logical_not(up), top & up
+    return low, top
+
+
+def residual_kernel(plan, n_msg, res, *rest):
     sent, got = rest[:n_msg], rest[n_msg : 2 * n_msg]
-    full, tz_low, tz_top, gz_low, gz_top = rest[2 * n_msg : 2 * n_msg + 5]
-    fz, hz = rest[2 * n_msg + 5 : -1], rest[-1]
+    full, hz, *fz = rest[2 * n_msg :]
     nx, ny, nz = plan.nx, plan.ny, plan.nz
     parts = z_flux(sent, got)
-    split = [z_sides(plan, [part[k] for part in parts]) for k in range(4)]
-    rows = stack_rows([v for pair in split for v in pair])
+    if n_msg == 1:
+        vals = list(parts[0][1:])
+    else:
+        vals = [v for k in (1, 2, 3) for v in z_sides(plan, [part[k] for part in parts])]
     for k in range(nx * ny // 128):
-        cut = slice(k * 128, (k + 1) * 128)
-        hz[cut, :8] = jnp.transpose(rows[:, cut])
-    lane = lanes_of((ny, nz))
+        rows = stack_rows([v[k : k + 1, :] for v in vals])
+        hz[k * 128 : (k + 1) * 128, :8] = jnp.transpose(rows)
+    at_low, at_top = z_ends(plan, n_msg)
+
+    def layer(i, carry):
+        cells = pl.ds(i * ny, ny)
+        col = hz[cells, :8]
+        in_low, in_top = (
+            jnp.broadcast_to(col[:, k : k + 1], (ny, nz))
+            for k in ((2, 2) if n_msg == 1 else (4, 5))
+        )
+        full[i] = res[i] + (jnp.where(at_low, in_low, 0.0) + jnp.where(at_top, in_top, 0.0))
+        for k, out in enumerate(fz):
+            out[cells, :] = jnp.broadcast_to(col[:, k : k + 1], (ny, nz))
+        return carry
+
+    lax.fori_loop(0, nx, layer, 0, unroll=8)
+
+
+def faces_z_kernel(plan, n_msg, press, tz_in, hz, order, tz_low, tz_top, gz_low, gz_top):
+    ny, nz = plan.ny, plan.nz
+    at_low, at_top = z_ends(plan, n_msg)
 
     def layer(i, carry):
         t, p = tz_in[i], press[i]
-        cells = pl.ds(i * ny, ny)
-        col = hz[cells, :8]
-        in_low, in_top = col[:, 6:7], col[:, 7:8]
-        tz_low[i] = jnp.where(lane == 0, col[:, 4:5], t)
-        tz_top[i] = jnp.where(lane == nz - 1, col[:, 5:6], back(t, 1))
+        col = hz[pl.ds(i * ny, ny), :8]
+        t_low, t_top, in_low, in_top = (
+            jnp.broadcast_to(col[:, k : k + 1], (ny, nz))
+            for k in ((1, 1, 2, 2) if n_msg == 1 else (2, 3, 4, 5))
+        )
+        tz_low[i] = jnp.where(at_low, t_low, t)
+        tz_top[i] = jnp.where(at_top, t_top, back(t, 1))
         g = t * (ahead(p, 1) - p)
-        gz_low[i] = jnp.where(lane == 0, in_low, g)
-        gz_top[i] = jnp.where(lane == nz - 1, -in_top, back(g, 1))
-        flux = jnp.where(lane == 0, in_low, 0.0) + jnp.where(lane == nz - 1, in_top, 0.0)
-        full[i] = res[i] + flux
-        if len(fz) == 1:
-            fz[0][cells, :] = jnp.broadcast_to(col[:, 2:3] + col[:, 3:4], (ny, nz))
-        else:
-            for k, out in enumerate(fz):
-                out[cells, :] = jnp.broadcast_to(col[:, 2 + k : 3 + k], (ny, nz))
+        gz_low[i] = jnp.where(at_low, in_low, g)
+        gz_top[i] = jnp.where(at_top, -in_top, back(g, 1))
         return carry
 
-    lax.fori_loop(0, nx, layer, 0, unroll=4)
-
-
-def wide_rows(plan, msg_a, msg_b, i, high):
-    nx = plan.nx
+    lax.fori_loop(0, plan.nx, layer, 0, unroll=8)
+
+
+def wide_rows(plan, msg_a, msg_b, j, count, high):
     tail = 2 * INTERSECTION
     per = 128 // tail
-    ends = side(plan, "gy", msg_a[nx + i // per], msg_b[nx + i // per], high)
-    ends = pltpu.roll(ends, (128 - (i % per) * tail) % 128, 1)[:, :tail]
-    return jnp.concatenate([side(plan, "gy", msg_a[i], msg_b[i], high), ends], axis=1)
+    ends = side(plan, "gy", msg_a[count + j // per], msg_b[count + j // per], high)
+    ends = pltpu.roll(ends, (128 - (j % per) * tail) % 128, 1)[:, :tail]
+    return jnp.concatenate([side(plan, "gy", msg_a[j], msg_b[j], high), ends], axis=1)
 
 
 def thrice(value):
@@ -468,9 +507,9 @@
     return jnp.concatenate([value[:rows], ends], axis=1)
 
 
-def y_modes(plan, spec, ya, yb, basis, i):
-    low = wide_rows(plan, ya, yb, i, False)
-    top = wide_rows(plan, ya, yb, i, True)
+def y_modes(plan, spec, ya, yb, basis, i, j, count):
+    low = wide_rows(plan, ya, yb, j, count, False)
+    top = wide_rows(plan, ya, yb, j, count, True)
     return mxu(basis[...], thrice(jnp.concatenate([low, spec[i], top], axis=0)))
 
 
@@ -479,7 +518,8 @@
     wide = INTERSECTION
 
     def layer(i, carry):
-        edge[i] = y_modes(plan, spec, ya, yb, basis, jnp.where(i < wide, i, nx - 2 * wide + i))
+        k = jnp.where(i < wide, i, nx - 2 * wide + i)
+        edge[i] = y_modes(plan, spec, ya, yb, basis, k, i, 2 * wide)
         return carry
 
     lax.fori_loop(0, 2 * wide, layer, 0, unroll=16)
@@ -497,7 +537,7 @@
     wide = INTERSECTION
 
     def layer(i, carry):
-        zed[i] = y_modes(plan, spec, ya, yb, basis, i)
+        zed[i] = y_modes(plan, spec, ya, yb, basis, i, i - wide, nx - 2 * wide)
         return carry
 
     lax.fori_loop(wide, nx - wide, layer, 0, unroll=8)
@@ -526,7 +566,7 @@
 
 
 def solve_kernel(
-    plan, zed, xa, xb, factors, reach, middle, basis_y, basis_z, total, direction, *rest
+    plan, zed, xa, xb, factors, reach, middle, basis_y, basis_z, total, fa, fb, order, direction, *rest
 ):
     (dxa, dxb, dya, dyb), z_outs, (work, tile) = rest[:4], rest[4:-2], rest[-2:]
     nx, ny, nz = plan.nx, plan.ny, plan.nz
@@ -575,7 +615,9 @@
         return carry
 
     lax.fori_loop(0, nx // group, lift, 0, unroll=8)
-    pack_x(plan, direction, dxa, dxb)
+    pack_x(plan, direction, dxa.at[0], dxb.at[0])
+    dxa[1] = fa[...]
+    dxb[1] = fb[...]
     pack_y(plan, direction, dya, dyb)
     tile_out(plan, tile, z_outs)
 
@@ -619,8 +661,8 @@
         return d, im, rd, da
 
     zero = jnp.zeros((ny, nz), F32)
-    low = side(plan, "gx", xa[...], xb[...], False)
-    top = side(plan, "gx", xa[...], xb[...], True)
+    low = side(plan, "gx", xa[0], xb[0], False)
+    top = side(plan, "gx", xa[0], xb[0], True)
     d, im, rd, da = lax.fori_loop(0, nx, layer, (low, zero, zero, zero), unroll=16)
     flux = tx[nx] * (d - top)
     gx[nx] = flux
@@ -728,9 +770,9 @@
 def step_kernel(plan, *refs):
     n_msg = len(plan.z_msgs)
     sums, still, move = refs[0], refs[1:6], refs[6:11]
-    (sat, frac, coef, inject, square, pull, push, hx, hy) = refs[11:20]
-    fz = refs[20 : 20 + n_msg]
-    outs = refs[20 + n_msg :]
+    (sat, frac, coef, inject, square, pull, push, xa, xb, hy) = refs[11:21]
+    fz = refs[21 : 21 + n_msg]
+    outs = refs[21 + n_msg :]
     (s_new, f_new, gx, gy_low, gy_top, gz_low, gz_top, outflow) = outs[:8]
     packs = outs[8 : 12 + n_msg]
     tile = outs[-1]
@@ -738,13 +780,14 @@
     step = step_of(sums)
     lane = lanes_of((ny, nz))
     done = keep(plan, s_new, f_new, tile)
+    x_low, x_top = (side(plan, "gx", xa[1], xb[1], high) for high in (False, True))
 
     def flux(k, i):
         return still[k][i] + step * move[k][i]
 
     def layer(i, carry):
         f, g, flow = carry
-        f_next = jnp.where(i == nx - 1, hx[1, 1], frac[jnp.minimum(i + 1, nx - 1)])
+        f_next = jnp.where(i == nx - 1, x_top, frac[jnp.minimum(i + 1, nx - 1)])
         g_next = flux(0, i + 1)
         gx[i + 1] = g_next
         flow_next = upwind(g_next, f, f_next)
@@ -775,7 +818,7 @@
 
     f0, g0 = frac[0], flux(0, 0)
     gx[0] = g0
-    lax.fori_loop(0, nx, layer, (f0, g0, upwind(g0, hx[0, 1], f0)), unroll=16)
+    lax.fori_loop(0, nx, layer, (f0, g0, upwind(g0, x_low, f0)), unroll=16)
     pack_all(plan, f_new, tile, packs)
 
 
@@ -873,9 +916,9 @@
         x = swap("gx", packs[0], packs[1])
         return [*x, *y, *z]
 
-    press, sat, mob, coef, frac, xa, xb, ya, yb, total = call(
+    press, sat, mob, coef, frac, xa, xb, ya, yb, fa, fb, total = call(
         functools.partial(mobility_kernel, plan),
-        [full_shape] * 5 + [(3,) + x_face] * 2 + [(3,) + y_face] * 2 + [x_face],
+        [full_shape] * 5 + [(2,) + x_face] * 2 + [(3,) + y_face] * 2 + [x_face] * 3,
         (pressure, saturation, permeability, rock_type, oil_factor),
         hbm=(0, 1, 2, 3, 4),
         scratch=[full_shape, pltpu.VMEM(full_shape, jnp.int32),
@@ -890,46 +933,54 @@
     )
     res, *sent = call(
         functools.partial(rim_kernel, plan),
-        [full_shape] + [(MSG_ROWS, cells)] * n_msg,
+        [full_shape] + [((wide + 3) * cells // 128, 128)] * n_msg,
         (res, press, mob, xa, xb, ya, yb, *comps),
         aliases={0: 0},
     )
     got = swap_z(sent)
-    tx, ty_low, ty_top, gx, gy_low, gy_top, hx, hy, rate, inject, anchor, square, pull, push = call(
+    tx, ty_low, ty_top, gx, gy_low, gy_top, hy, rate, inject, anchor, square, pull, push = call(
         functools.partial(faces_xy_kernel, plan),
         [(nx + 1, ny, nz)] + [full_shape] * 2 + [(nx + 1, ny, nz)] + [full_shape] * 2
-        + [(2, 2) + x_face, (2, 2) + y_face] + [full_shape] * 6,
+        + [(2, 2) + y_face] + [full_shape] * 6,
         (mob, press, sat, coef, porosity, well_mask, tx, ty, xa, xb, ya, yb),
         scratch=[(2,) + y_face],
     )
-    spec, sa, sb = call(
+    slabs = [
+        (len(v) + len(v) * 2 * wide // 128, wide, nz) for v in y_parts(plan) for _ in (0, 1)
+    ]
+    spec, *slab = call(
         functools.partial(z_kernel, plan, n_msg),
-        [(nx, ny, mz)] + [(nx + nx * 2 * wide // 128, wide, nz)] * 2,
-        (res, right(table_z[wide : wide + nz]), *rims, hx, *sent, *got),
-    )
-    sa, sb = swap("gy", sa, sb)
-    full, tz_low, tz_top, gz_low, gz_top, *fz = call(
-        functools.partial(faces_z_kernel, plan, n_msg),
-        [full_shape] * 5 + spreads,
-        (res, press, tz, *sent, *got),
-        scratch=[(cells, 128)],
+        [(nx, ny, mz)] + slabs,
+        (res, right(table_z[wide : wide + nz]), *rims, hy, *sent, *got),
+    )
+    edge_slab = swap("gy", *slab[:2])
+    mid_slab = swap("gy", *slab[2:])
+    full, hz, *fz = call(
+        functools.partial(residual_kernel, plan, n_msg),
+        [full_shape] + [(cells, 128)] + spreads,
+        (res, *sent, *got),
     )
     edge, ma, mb = call(
         functools.partial(y_edge_kernel, plan),
         [(2 * wide, my, mz), (my + 8, nz), (my + 8, nz)],
-        (spec, sa, sb, left(table_y), factors, gz_low),
+        (spec, *edge_slab, left(table_y), factors, full),
     )
     ma, mb = swap("gx", ma, mb)
     (zed,) = call(
         functools.partial(y_mid_kernel, plan),
         [(nx, my, mz)],
-        (spec, sa, sb, left(table_y), factors, edge),
+        (spec, *mid_slab, left(table_y), factors, edge),
+    )
+    tz_low, tz_top, gz_low, gz_top = call(
+        functools.partial(faces_z_kernel, plan, n_msg),
+        [full_shape] * 4,
+        (press, tz, hz, edge),
     )
     direction, *packs = call(
         functools.partial(solve_kernel, plan),
-        [full_shape] + face_shapes,
+        [full_shape] + [(2,) + x_face] * 2 + face_shapes[2:],
         (zed, ma, mb, factors, reach, middle, left(table_y[wide : wide + ny]),
-         jnp.asarray(np.stack(parts(table_z[:, wide : wide + nz]))), total),
+         jnp.asarray(np.stack(parts(table_z[:, wide : wide + nz]))), total, fa, fb, gz_low),
         scratch=[(cells, mz), tile],
     )
     dhalo = exchange(packs)
@@ -944,7 +995,7 @@
         functools.partial(step_kernel, plan),
         [full_shape] * 2 + [(nx + 1, ny, nz)] + [full_shape] * 5 + face_shapes,
         (sums, gx, gy_low, gy_top, gz_low, gz_top, *moves,
-         sat, frac, coef, inject, square, pull, push, hx, hy, *fz),
+         sat, frac, coef, inject, square, pull, push, *dhalo[:2], hy, *fz),
         scratch=[tile],
         limit=40,
     )

time: 69.9 us -> 69.5 us (level)
  blocking collectives: 10.1 us -> 11.3 us
  Pallas kernels: 19.7 us -> 18.5 us
  waiting for transfers between devices: 12.7 us -> 11.6 us
  starting transfers between devices: 26.2 us -> 26.9 us
    pallas_call x14 -> x15, Pallas kernels: 19.7 us -> 18.5 us  [call(): pl.pallas_call(kernel, out_shape=[jax.ShapeDtypeStruct(s, F32) for s in o...]
    ppermute x24 -> x26, waiting for transfers between devices: 12.7 us -> 11.6 us  [send(): return lax.ppermute(value, axis, plan.perm(axis, which))]
    all_to_all x1, blocking collectives: 10.1 us -> 11.3 us  [per_device(): sums = lax.all_to_all(sums, AXES, 0, 0, tiled=True)]
    ppermute x24 -> x26, starting transfers between devices: 26.2 us -> 26.9 us  [send(): return lax.ppermute(value, axis, plan.perm(axis, which))]
  transfers between devices with their start and end apart: 24 -> 26, of which waited for: 8 -> 7; matrix products, arithmetic and copies ran while one was open for 0% -> 0% of each run, Pallas kernels for 12% -> 11%
where the time goes in v4:
time: 69.5 us; the launch traced here: 69.3 us
  starting transfers between devices  26.9 us (39%)
  Pallas kernels  18.5 us (27%)
  waiting for transfers between devices  11.6 us (17%)
  blocking collectives  11.3 us (16%)
  between operations  0.91 us (1%)
    ppermute x26, starting transfers between devices, send(): return lax.ppermute(value, axis, plan.perm(axis, which))  26.9 us
    pallas_call x15, Pallas kernels, call(): pl.pallas_call(kernel, out_shape=[jax.ShapeDtypeStruct(s, F32) for s in o...  18.5 us
    ppermute x26, waiting for transfers between devices, send(): return lax.ppermute(value, axis, plan.perm(axis, which))  11.6 us
    all_to_all x1, blocking collectives, per_device(): sums = lax.all_to_all(sums, AXES, 0, 0, tiled=True)  11.3 us
  transfers between devices with their start and end apart: 26, of which 7 were waited for; matrix products, arithmetic and copies ran while one was open for 0% of the time, Pallas kernels for 11%

profile of v4, /device:TPU:0, one launch (start us, length us, event | category | flops | bytes accessed | tf_op | source)
XLA Modules:
  0.0 69.3 jit_solution(10328714852020122505)
XLA Ops:
  0.7 2.0 %shard_map.202 = (f32[32,32,128]{2,1,0:T(8,128)S(1)}, f32[32,32,128]{2,1,0:T(8,128)S(1)}, f32[32,32,128]{2,1,0:T(8,128)S(1)}, f32[32,32,128]{2,1,0:T(8,128)S(1)}...) custom-call(f32[32,32,128]{2,1,0:T(8,128)} %press_in.1, ...), custom_call_target="tpu_custom_call" | custom-call | tf_op jit(solution)/shard_map/pallas_call | solution.py:126
  2.7 0.6 collective-permute-start.2
  3.3 2.6 %collective-permute-start.3 = (f32[3,32,128]{2,1,0:T(8,128)S(1)}, f32[3,32,128]{2,1,0:T(8,128)S(1)}, u32[]{:S(2)}, u32[]{:S(2)}) collective-permute-start(f32[3,32,128]{2,1,0:T(8,128)S(1)} %get-tuple-element.94), channel_id=1, source_target_pairs={{2,4},{4,2},{6,0},{0,6},{3,5},{5,3},{7,1},{1,7},{10,12},{12,10},{1... | collective-permute-start | bytes 147464 | tf_op jit(solution)/shard_map/ppermute | solution.py:898
  5.9 1.6 %collective-permute-start = (f32[2,32,128]{2,1,0:T(8,128)S(1)}, f32[2,32,128]{2,1,0:T(8,128)S(1)}, u32[]{:S(2)}, u32[]{:S(2)}) collective-permute-start(f32[2,32,128]{2,1,0:T(8,128)S(1)} %get-tuple-element.91), channel_id=1, source_target_pairs={{0,8},{8,0},{16,24},{24,16},{1,9},{9,1},{17,25},{25,17},{2,10},{10... | collective-permute-start | bytes 98312 | tf_op jit(solution)/shard_map/ppermute | solution.py:898
  7.4 2.5 %collective-permute-start.1 = (f32[2,32,128]{2,1,0:T(8,128)S(1)}, f32[2,32,128]{2,1,0:T(8,128)S(1)}, u32[]{:S(2)}, u32[]{:S(2)}) collective-permute-start(f32[2,32,128]{2,1,0:T(8,128)S(1)} %get-tuple-element.92), channel_id=1, source_target_pairs={{8,16},{16,8},{24,0},{0,24},{9,17},{17,9},{25,1},{1,25},{10,18},{1... | collective-permute-start | bytes 98312 | tf_op jit(solution)/shard_map/ppermute | solution.py:898
  9.9 1.7 %shard_map.203 = (f32[32,32,128]{2,1,0:T(8,128)S(1)}, f32[32,32,128]{2,1,0:T(8,128)S(1)}, f32[32,32,128]{2,1,0:T(8,128)S(1)}, f32[32,32,128]{2,1,0:T(8,128)S(1)}...) custom-call(f32[32,32,128]{2,1,0:T(8,128)S(1)} %get-tuple-element.87.press, ...), custom_call_target="tpu_custom_call" | custom-call | tf_op jit(solution)/shard_map/pallas_call | solution.py:126
  11.6 0.0 copy-start.3
  11.6 0.0 collective-permute-done.xa
  11.6 1.5 %collective-permute-done.1.xb = f32[2,32,128]{2,1,0:T(8,128)S(1)} collective-permute-done((f32[2,32,128]{2,1,0:T(8,128)S(1)}, f32[2,32,128]{2,1,0:T(8,128)S(1)}, u32[]{:S(2)}, u32[]{:S(2)}) %collective-permute-start.1) | collective-permute-done | bytes 32800 | tf_op jit(solution)/shard_map/ppermute | solution.py:898
  13.1 0.0 collective-permute-done.2.ya
  13.2 0.4 shard_map.204
  13.5 1.6 %collective-permute-start.4 = (f32[88,128]{1,0:T(8,128)S(1)}, f32[88,128]{1,0:T(8,128)S(1)}, u32[]{:S(2)}, u32[]{:S(2)}) collective-permute-start(f32[88,128]{1,0:T(8,128)S(1)} %get-tuple-element.102.rest_0_), channel_id=1, source_target_pairs={{0,1},{1,0},{2,3},{3,2},{4,5},{5,4},{6,7},{7,6},{8,9},{9,8},{10,11... | collective-permute-start | bytes 135176 | tf_op jit(solution)/shard_map/ppermute | solution.py:898
  15.1 0.7 shard_map.205
  15.8 0.0 copy-start
  15.8 0.0 copy-start.7
  15.8 1.8 %collective-permute-done.4.rest_1_ = f32[88,128]{1,0:T(8,128)S(1)} collective-permute-done((f32[88,128]{1,0:T(8,128)S(1)}, f32[88,128]{1,0:T(8,128)S(1)}, u32[]{:S(2)}, u32[]{:S(2)}) %collective-permute-start.4) | collective-permute-done | bytes 45088 | tf_op jit(solution)/shard_map/ppermute | solution.py:898
  17.6 0.8 %shard_map.206 = (f32[32,32,144]{2,1,0:T(8,128)S(1)}, f32[18,8,128]{2,1,0:T(8,128)S(1)}, f32[18,8,128]{2,1,0:T(8,128)S(1)}, f32[18,8,128]{2,1,0:T(8,128)S(1)}, f32[18,8,128]{2,1,0:T(8,128)S(1)}) custom-call(f32[32,32,128]{2,1,0:T(8,128)S(1)} %get-tuple-element.96.res, bf16[384,144]{1,0:T(8,128)(2,1)S(1)} %copy-done.6, f32[48,144]{1,0:T(8,128)S(1)} %copy-done.10, ...), custom_call_target="tpu_custom_call" | custom-call | tf_op jit(solution)/shard_map/pallas_call | solution.py:126
  18.4 0.1 collective-permute-start.7
  18.5 0.6 collective-permute-start.8
  19.2 0.1 collective-permute-start.5
  19.3 1.5 %collective-permute-start.6 = (f32[18,8,128]{2,1,0:T(8,128)S(1)}, f32[18,8,128]{2,1,0:T(8,128)S(1)}, u32[]{:S(2)}, u32[]{:S(2)}) collective-permute-start(f32[18,8,128]{2,1,0:T(8,128)S(1)} %get-tuple-element.105), channel_id=1, source_target_pairs={{2,4},{4,2},{6,0},{0,6},{3,5},{5,3},{7,1},{1,7},{10,12},{12,10},{1... | collective-permute-start | bytes 221192 | tf_op jit(solution)/shard_map/ppermute | solution.py:898
  20.8 0.8 %shard_map.207 = (f32[32,32,128]{2,1,0:T(8,128)S(1)}, f32[1024,128]{1,0:T(8,128)S(1)}, f32[1024,128]{1,0:T(8,128)S(1)}) custom-call(f32[32,32,128]{2,1,0:T(8,128)S(1)} %get-tuple-element.96.res, f32[88,128]{1,0:T(8,128)S(1)} %get-tuple-element.102.rest_0_, f32[88,128]{1,0:T(8,128)S(1)} %collective-permute-done.4.rest_1_), custom_call_target="tpu_custom_call" | custom-call | tf_op jit(solution)/shard_map/pallas_call | solution.py:126
  21.6 0.9 %collective-permute-done.8.yb = f32[18,8,128]{2,1,0:T(8,128)S(1)} collective-permute-done((f32[18,8,128]{2,1,0:T(8,128)S(1)}, f32[18,8,128]{2,1,0:T(8,128)S(1)}, u32[]{:S(2)}, u32[]{:S(2)}) %collective-permute-start.8) | collective-permute-done | bytes 73760 | tf_op jit(solution)/shard_map/ppermute | solution.py:898
  22.6 0.5 shard_map.208
  23.0 0.0 collective-permute-start.9
  23.1 2.5 %collective-permute-start.10 = (f32[56,128]{1,0:T(8,128)S(1)}, f32[56,128]{1,0:T(8,128)S(1)}, u32[]{:S(2)}, u32[]{:S(2)}) collective-permute-start(f32[56,128]{1,0:T(8,128)S(1)} %get-tuple-element.111), channel_id=1, source_target_pairs={{8,16},{16,8},{24,0},{0,24},{9,17},{17,9},{25,1},{1,25},{10,18},{1... | collective-permute-start | bytes 86024 | tf_op jit(solution)/shard_map/ppermute | solution.py:898
  25.6 2.0 %shard_map.210 = (f32[32,32,128]{2,1,0:T(8,128)S(1)}, f32[32,32,128]{2,1,0:T(8,128)S(1)}, f32[32,32,128]{2,1,0:T(8,128)S(1)}, f32[32,32,128]{2,1,0:T(8,128)S(1)}) custom-call(f32[32,32,128]{2,1,0:T(8,128)S(1)} %get-tuple-element.87.press, f32[32,32,128]{2,1,0:T(8,128)S(1)} %get-tuple-element.115.tz_in, f32[1024,128]{1,0:T(8,128)S(1)} %get-tuple-element.116.hz, ...), custom_call_target="tpu_custom_call" | custom-call | tf_op jit(solution)/shard_map/pallas_call | solution.py:126
  27.6 0.0 copy-start.2
  27.6 0.0 copy-start.8
  27.6 0.0 copy-start.9
  27.7 0.0 copy-start.12
  27.7 0.0 collective-permute-done.5.ya
  27.7 0.0 collective-permute-done.6.yb
  27.7 0.9 %shard_map.209.zed = f32[32,48,144]{2,1,0:T(8,128)S(1)} custom-call(f32[32,32,144]{2,1,0:T(8,128)S(1)} %get-tuple-element.103.spec, f32[18,8,128]{2,1,0:T(8,128)S(1)} %collective-permute-done.5.ya, f32[18,8,128]{2,1,0:T(8,128)S(1)} %collective-permute-done.6.yb, bf16[48,144]{1,0:T(8,128)(2,1)S(1)} %copy-done.7, f32[24,48,144]{2,1,0:T(8,128)S(1)} %copy-done, ...), custom_call_target="tpu_custom_call" | custom-call | tf_op jit(solution)/shard_map/pallas_call | solution.py:126
  28.6 0.0 collective-permute-done.9.xa
  28.6 0.3 collective-permute-done.10.xb
  28.9 1.4 %shard_map.211 = (f32[32,32,128]{2,1,0:T(8,128)S(1)}, f32[2,32,128]{2,1,0:T(8,128)S(1)}, f32[2,32,128]{2,1,0:T(8,128)S(1)}, f32[32,128]{1,0:T(8,128)S(1)}, f32[32,128]{1,0:T(8,128)S(1)}, /*index=5*/f32[8,128]{1,0:T(8,128)S(1)}) custom-call(f32[32,48,144]{2,1,0:T(8,128)S(1)} %shard_map.209.zed, f32[56,128]{1,0:T(8,128)S(1)} %collective-permute-done.9.xa, ...), custom_call_target="tpu_custom_call" | custom-call | tf_op jit(solution)/shard_map/pallas_call | solution.py:126
  30.4 0.9 %collective-permute-start.11 = (f32[2,32,128]{2,1,0:T(8,128)S(1)}, f32[2,32,128]{2,1,0:T(8,128)S(1)}, u32[]{:S(2)}, u32[]{:S(2)}) collective-permute-start(f32[2,32,128]{2,1,0:T(8,128)S(1)} %get-tuple-element.125), channel_id=1, source_target_pairs={{0,8},{8,0},{16,24},{24,16},{1,9},{9,1},{17,25},{25,17},{2,10},{10... | collective-permute-start | bytes 98312 | tf_op jit(solution)/shard_map/ppermute | solution.py:898
  31.3 2.5 %collective-permute-start.12 = (f32[2,32,128]{2,1,0:T(8,128)S(1)}, f32[2,32,128]{2,1,0:T(8,128)S(1)}, u32[]{:S(2)}, u32[]{:S(2)}) collective-permute-start(f32[2,32,128]{2,1,0:T(8,128)S(1)} %get-tuple-element.126), channel_id=1, source_target_pairs={{8,16},{16,8},{24,0},{0,24},{9,17},{17,9},{25,1},{1,25},{10,18},{1... | collective-permute-start | bytes 98312 | tf_op jit(solution)/shard_map/ppermute | solution.py:898
  33.7 0.0 collective-permute-start.13
  33.8 0.0 collective-permute-start.14
  33.8 1.5 %collective-permute-start.15 = (f32[8,128]{1,0:T(8,128)S(1)}, f32[8,128]{1,0:T(8,128)S(1)}, u32[]{:S(2)}, u32[]{:S(2)}) collective-permute-start(f32[8,128]{1,0:T(8,128)S(1)} %get-tuple-element.129), channel_id=1, source_target_pairs={{0,1},{1,0},{2,3},{3,2},{4,5},{5,4},{6,7},{7,6},{8,9},{9,8},{10,11... | collective-permute-start | bytes 12296 | tf_op jit(solution)/shard_map/ppermute | solution.py:898
  35.3 2.1 %collective-permute-done.15.rest_0_ = f32[8,128]{1,0:T(8,128)S(1)} collective-permute-done((f32[8,128]{1,0:T(8,128)S(1)}, f32[8,128]{1,0:T(8,128)S(1)}, u32[]{:S(2)}, u32[]{:S(2)}) %collective-permute-start.15) | collective-permute-done | bytes 4128 | tf_op jit(solution)/shard_map/ppermute | solution.py:898
  37.4 0.0 collective-permute-done.13.ya
  37.4 0.0 collective-permute-done.14.yb
  37.4 1.0 %shard_map.212 = (f32[32,32,128]{2,1,0:T(8,128)S(1)}, f32[32,128]{1,0:T(8,128)S(1)}, f32[33,32,128]{2,1,0:T(8,128)S(1)}, f32[32,32,128]{2,1,0:T(8,128)S(1)}, f32...) custom-call(f32[32,32,128]{2,1,0:T(8,128)S(1)} %get-tuple-element.118.direction, ...), custom_call_target="tpu_custom_call" | custom-call | tf_op jit(solution)/shard_map/pallas_call | solution.py:126
  38.4 11.3 %all_to_all.11 = f32[32,1,128]{2,1,0:T(1,128)S(1)} all-to-all(f32[32,1,128]{2,1,0:T(1,128)S(1)} %bitcast.6), channel_id=1, replica_groups=mesh['gx'=4,'gy'=4,'gz'=2] {'gx','gy','gz'}, dimensions={0} | all-to-all | bytes 32768 | tf_op jit(solution)/shard_map/all_to_all | solution.py:993
  49.7 1.6 %shard_map.214 = (f32[32,32,128]{2,1,0:T(8,128)S(1)}, f32[32,32,128]{2,1,0:T(8,128)S(1)}, f32[33,32,128]{2,1,0:T(8,128)S(1)}, f32[32,32,128]{2,1,0:T(8,128)S(1)}...) custom-call(f32[32,128]{1,0:T(8,128)S(1)} %bitcast.4, ...), custom_call_target="tpu_custom_call" | custom-call | tf_op jit(solution)/shard_map/pallas_call | solution.py:126
  51.3 0.5 collective-permute-start.16
  51.7 1.5 %collective-permute-start.17 = (f32[32,128]{1,0:T(8,128)S(1)}, f32[32,128]{1,0:T(8,128)S(1)}, u32[]{:S(2)}, u32[]{:S(2)}) collective-permute-start(f32[32,128]{1,0:T(8,128)S(1)} %get-tuple-element.159), channel_id=1, source_target_pairs={{8,16},{16,8},{24,0},{0,24},{9,17},{17,9},{25,1},{1,25},{10,18},{1... | collective-permute-start | bytes 49160 | tf_op jit(solution)/shard_map/ppermute | solution.py:898
  53.2 0.0 collective-permute-start.18
  53.2 0.7 %collective-permute-start.19 = (f32[32,128]{1,0:T(8,128)S(1)}, f32[32,128]{1,0:T(8,128)S(1)}, u32[]{:S(2)}, u32[]{:S(2)}) collective-permute-start(f32[32,128]{1,0:T(8,128)S(1)} %get-tuple-element.161), channel_id=1, source_target_pairs={{2,4},{4,2},{6,0},{0,6},{3,5},{5,3},{7,1},{1,7},{10,12},{12,10},{1... | collective-permute-start | bytes 49160 | tf_op jit(solution)/shard_map/ppermute | solution.py:898
  54.0 0.5 collective-permute-start.20
  54.5 1.3 %shard_map.213 = (f32[32,32,128]{2,1,0:T(8,128)}, f32[32,32,128]{2,1,0:T(8,128)}, f32[8,128]{1,0:T(8,128)S(1)}) custom-call(f32[32,128]{1,0:T(8,128)S(1)} %bitcast.5, f32[32,32,128]{2,1,0:T(8,128)S(1)} %get-tuple-element.87.press, f32[32,32,128]{2,1,0:T(8,128)S(1)} %get-tuple-element.118.direction, f32[32,32,128]{2,1,0:T(8,128)S(1)} %get-tuple-element.108.order.full, ...), custom_call_target="tpu_custom_call" | custom-call | tf_op jit(solution)/shard_map/pallas_call | solution.py:126
  55.8 1.8 %collective-permute-done.20.refs_15_ = f32[8,128]{1,0:T(8,128)S(1)} collective-permute-done((f32[8,128]{1,0:T(8,128)S(1)}, f32[8,128]{1,0:T(8,128)S(1)}, u32[]{:S(2)}, u32[]{:S(2)}) %collective-permute-start.20) | collective-permute-done | bytes 4128 | tf_op jit(solution)/shard_map/ppermute | solution.py:898
  57.6 0.0 collective-permute-done.16.refs_11_
  57.6 0.0 collective-permute-done.17.refs_12_
  57.6 1.6 %shard_map.215 = (f32[32,32,128]{2,1,0:T(8,128)S(1)}, f32[32,32,128]{2,1,0:T(8,128)S(1)}, f32[32,128]{1,0:T(8,128)S(1)}, f32[32,128]{1,0:T(8,128)S(1)}, f32[32,1...) custom-call(f32[32,32,128]{2,1,0:T(8,128)S(1)} %get-tuple-element.148.refs_0_, ...), custom_call_target="tpu_custom_call" | custom-call | tf_op jit(solution)/shard_map/pallas_call | solution.py:126
  59.2 0.0 collective-permute-start.21
  59.2 2.9 %collective-permute-start.22 = (f32[32,128]{1,0:T(8,128)S(1)}, f32[32,128]{1,0:T(8,128)S(1)}, u32[]{:S(2)}, u32[]{:S(2)}) collective-permute-start(f32[32,128]{1,0:T(8,128)S(1)} %get-tuple-element.167), channel_id=1, source_target_pairs={{8,16},{16,8},{24,0},{0,24},{9,17},{17,9},{25,1},{1,25},{10,18},{1... | collective-permute-start | bytes 49160 | tf_op jit(solution)/shard_map/ppermute | solution.py:898
  62.1 1.6 %collective-permute-start.24 = (f32[32,128]{1,0:T(8,128)S(1)}, f32[32,128]{1,0:T(8,128)S(1)}, u32[]{:S(2)}, u32[]{:S(2)}) collective-permute-start(f32[32,128]{1,0:T(8,128)S(1)} %get-tuple-element.169), channel_id=1, source_target_pairs={{2,4},{4,2},{6,0},{0,6},{3,5},{5,3},{7,1},{1,7},{10,12},{12,10},{1... | collective-permute-start | bytes 49160 | tf_op jit(solution)/shard_map/ppermute | solution.py:898
  63.7 0.5 collective-permute-start.25
  64.2 3.1 %collective-permute-done.25.refs_15_ = f32[8,128]{1,0:T(8,128)S(1)} collective-permute-done((f32[8,128]{1,0:T(8,128)S(1)}, f32[8,128]{1,0:T(8,128)S(1)}, u32[]{:S(2)}, u32[]{:S(2)}) %collective-permute-start.25) | collective-permute-done | bytes 4128 | tf_op jit(solution)/shard_map/ppermute | solution.py:898
  67.4 1.9 %shard_map.216 = f32[32,32,128]{2,1,0:T(8,128)} custom-call(f32[32,32,128]{2,1,0:T(8,128)S(1)} %get-tuple-element.164.refs_0_, f32[32,32,128]{2,1,0:T(8,128)S(1)} %get-tuple-element.165.refs_1_, f32[32,32,128]{2,1,0:T(8,128)S(1)} %get-tuple-element.98.coef.refs_13_.refs_2_, f32[32,32,128]{2,1,0:T(8,128)S(1)} %get-tuple-element.150.refs_3_, ...), custom_call_target="tpu_custom_call" | custom-call | tf_op jit(solution)/shard_map/pallas_call | solution.py:126
  (30 shorter events, 0.1 us)
Async XLA Ops:
  0.6 9.3 %copy-start.4 = (f32[32,32,128]{2,1,0:T(8,128)S(1)}, f32[32,32,128]{2,1,0:T(8,128)}, u32[]{:S(2)}) copy-start(f32[32,32,128]{2,1,0:T(8,128)} %source.1) | copy-start | bytes 1572868
  0.6 9.3 %copy-start.5 = (f32[32,32,128]{2,1,0:T(8,128)S(1)}, f32[32,32,128]{2,1,0:T(8,128)}, u32[]{:S(2)}) copy-start(f32[32,32,128]{2,1,0:T(8,128)} %compress.1) | copy-start | bytes 1572868
  0.7 9.3 %copy-start.1 = (s32[32,32,128]{2,1,0:T(8,128)S(1)}, s32[32,32,128]{2,1,0:T(8,128)}, u32[]{:S(2)}) copy-start(s32[32,32,128]{2,1,0:T(8,128)} %well.3) | copy-start | bytes 1572868
  2.7 10.4 %collective-permute-start.2 = (f32[3,32,128]{2,1,0:T(8,128)S(1)}, f32[3,32,128]{2,1,0:T(8,128)S(1)}, u32[]{:S(2)}, u32[]{:S(2)}) collective-permute-start(f32[3,32,128]{2,1,0:T(8,128)S(1)} %get-tuple-element.93), channel_id=1, source_target_pairs={{0,2},{2,0},{4,6},{6,4},{1,3},{3,1},{5,7},{7,5},{8,10},{10,8},{12,... | collective-permute-start | bytes 147464 | tf_op jit(solution)/shard_map/ppermute | solution.py:898
  3.3 9.9 %collective-permute-start.3 = (f32[3,32,128]{2,1,0:T(8,128)S(1)}, f32[3,32,128]{2,1,0:T(8,128)S(1)}, u32[]{:S(2)}, u32[]{:S(2)}) collective-permute-start(f32[3,32,128]{2,1,0:T(8,128)S(1)} %get-tuple-element.94), channel_id=1, source_target_pairs={{2,4},{4,2},{6,0},{0,6},{3,5},{5,3},{7,1},{1,7},{10,12},{12,10},{1... | collective-permute-start | bytes 147464 | tf_op jit(solution)/shard_map/ppermute | solution.py:898
  5.9 5.7 %collective-permute-start = (f32[2,32,128]{2,1,0:T(8,128)S(1)}, f32[2,32,128]{2,1,0:T(8,128)S(1)}, u32[]{:S(2)}, u32[]{:S(2)}) collective-permute-start(f32[2,32,128]{2,1,0:T(8,128)S(1)} %get-tuple-element.91), channel_id=1, source_target_pairs={{0,8},{8,0},{16,24},{24,16},{1,9},{9,1},{17,25},{25,17},{2,10},{10... | collective-permute-start | bytes 98312 | tf_op jit(solution)/shard_map/ppermute | solution.py:898
  7.4 5.7 %collective-permute-start.1 = (f32[2,32,128]{2,1,0:T(8,128)S(1)}, f32[2,32,128]{2,1,0:T(8,128)S(1)}, u32[]{:S(2)}, u32[]{:S(2)}) collective-permute-start(f32[2,32,128]{2,1,0:T(8,128)S(1)} %get-tuple-element.92), channel_id=1, source_target_pairs={{8,16},{16,8},{24,0},{0,24},{9,17},{17,9},{25,1},{1,25},{10,18},{1... | collective-permute-start | bytes 98312 | tf_op jit(solution)/shard_map/ppermute | solution.py:898
  11.6 3.5 %copy-start.3 = (f32[32,32,128]{2,1,0:T(8,128)S(1)}, f32[32,32,128]{2,1,0:T(8,128)}, u32[]{:S(2)}) copy-start(f32[32,32,128]{2,1,0:T(8,128)} %poro.1) | copy-start | bytes 1572868
  13.5 4.1 %collective-permute-start.4 = (f32[88,128]{1,0:T(8,128)S(1)}, f32[88,128]{1,0:T(8,128)S(1)}, u32[]{:S(2)}, u32[]{:S(2)}) collective-permute-start(f32[88,128]{1,0:T(8,128)S(1)} %get-tuple-element.102.rest_0_), channel_id=1, source_target_pairs={{0,1},{1,0},{2,3},{3,2},{4,5},{5,4},{6,7},{7,6},{8,9},{9,8},{10,11... | collective-permute-start | bytes 135176 | tf_op jit(solution)/shard_map/ppermute | solution.py:898
  15.1 2.5 %copy-start.6 = (bf16[384,144]{1,0:T(8,128)(2,1)S(1)}, bf16[384,144]{1,0:T(8,128)(2,1)}, u32[]{:S(2)}) copy-start(bf16[384,144]{1,0:T(8,128)(2,1)} %constant.23.clone.basis) | copy-start | bytes 331780
  15.1 2.5 %copy-start.10 = (f32[48,144]{1,0:T(8,128)S(1)}, f32[48,144]{1,0:T(8,128)}, u32[]{:S(2)}) copy-start(f32[48,144]{1,0:T(8,128)} %constant.27.rim_low) | copy-start | bytes 82948
  15.1 2.5 %copy-start.11 = (f32[48,144]{1,0:T(8,128)S(1)}, f32[48,144]{1,0:T(8,128)}, u32[]{:S(2)}) copy-start(f32[48,144]{1,0:T(8,128)} %constant.28.rim_top) | copy-start | bytes 82948
  15.8 6.8 %copy-start = (f32[24,48,144]{2,1,0:T(8,128)S(1)}, f32[24,48,144]{2,1,0:T(8,128)}, u32[]{:S(2)}) copy-start(f32[24,48,144]{2,1,0:T(8,128)} %constant.18.clone.factors) | copy-start | bytes 1990660
  15.8 6.8 %copy-start.7 = (bf16[48,144]{1,0:T(8,128)(2,1)S(1)}, bf16[48,144]{1,0:T(8,128)(2,1)}, u32[]{:S(2)}) copy-start(bf16[48,144]{1,0:T(8,128)(2,1)} %constant.24.clone.basis) | copy-start | bytes 41476
  18.4 3.2 %collective-permute-start.7 = (f32[18,8,128]{2,1,0:T(8,128)S(1)}, f32[18,8,128]{2,1,0:T(8,128)S(1)}, u32[]{:S(2)}, u32[]{:S(2)}) collective-permute-start(f32[18,8,128]{2,1,0:T(8,128)S(1)} %get-tuple-element.106), channel_id=1, source_target_pairs={{0,2},{2,0},{4,6},{6,4},{1,3},{3,1},{5,7},{7,5},{8,10},{10,8},{12,... | collective-permute-start | bytes 221192 | tf_op jit(solution)/shard_map/ppermute | solution.py:898
  18.5 4.0 %collective-permute-start.8 = (f32[18,8,128]{2,1,0:T(8,128)S(1)}, f32[18,8,128]{2,1,0:T(8,128)S(1)}, u32[]{:S(2)}, u32[]{:S(2)}) collective-permute-start(f32[18,8,128]{2,1,0:T(8,128)S(1)} %get-tuple-element.107), channel_id=1, source_target_pairs={{2,4},{4,2},{6,0},{0,6},{3,5},{5,3},{7,1},{1,7},{10,12},{12,10},{1... | collective-permute-start | bytes 221192 | tf_op jit(solution)/shard_map/ppermute | solution.py:898
  19.2 8.5 %collective-permute-start.5 = (f32[18,8,128]{2,1,0:T(8,128)S(1)}, f32[18,8,128]{2,1,0:T(8,128)S(1)}, u32[]{:S(2)}, u32[]{:S(2)}) collective-permute-start(f32[18,8,128]{2,1,0:T(8,128)S(1)} %get-tuple-element.104), channel_id=1, source_target_pairs={{0,2},{2,0},{4,6},{6,4},{1,3},{3,1},{5,7},{7,5},{8,10},{10,8},{12,... | collective-permute-start | bytes 221192 | tf_op jit(solution)/shard_map/ppermute | solution.py:898
  19.3 8.4 %collective-permute-start.6 = (f32[18,8,128]{2,1,0:T(8,128)S(1)}, f32[18,8,128]{2,1,0:T(8,128)S(1)}, u32[]{:S(2)}, u32[]{:S(2)}) collective-permute-start(f32[18,8,128]{2,1,0:T(8,128)S(1)} %get-tuple-element.105), channel_id=1, source_target_pairs={{2,4},{4,2},{6,0},{0,6},{3,5},{5,3},{7,1},{1,7},{10,12},{12,10},{1... | collective-permute-start | bytes 221192 | tf_op jit(solution)/shard_map/ppermute | solution.py:898
  23.0 5.5 %collective-permute-start.9 = (f32[56,128]{1,0:T(8,128)S(1)}, f32[56,128]{1,0:T(8,128)S(1)}, u32[]{:S(2)}, u32[]{:S(2)}) collective-permute-start(f32[56,128]{1,0:T(8,128)S(1)} %get-tuple-element.110), channel_id=1, source_target_pairs={{0,8},{8,0},{16,24},{24,16},{1,9},{9,1},{17,25},{25,17},{2,10},{10... | collective-permute-start | bytes 86024 | tf_op jit(solution)/shard_map/ppermute | solution.py:898
  23.1 5.8 %collective-permute-start.10 = (f32[56,128]{1,0:T(8,128)S(1)}, f32[56,128]{1,0:T(8,128)S(1)}, u32[]{:S(2)}, u32[]{:S(2)}) collective-permute-start(f32[56,128]{1,0:T(8,128)S(1)} %get-tuple-element.111), channel_id=1, source_target_pairs={{8,16},{16,8},{24,0},{0,24},{9,17},{17,9},{25,1},{1,25},{10,18},{1... | collective-permute-start | bytes 86024 | tf_op jit(solution)/shard_map/ppermute | solution.py:898
  27.6 1.3 %copy-start.2 = (f32[16,48,144]{2,1,0:T(8,128)S(1)}, f32[16,48,144]{2,1,0:T(8,128)}, u32[]{:S(2)}) copy-start(f32[16,48,144]{2,1,0:T(8,128)} %constant.19.clone.reach) | copy-start | bytes 1327108
  27.6 1.3 %copy-start.8 = (bf16[2,144,128]{2,1,0:T(8,128)(2,1)S(1)}, bf16[2,144,128]{2,1,0:T(8,128)(2,1)}, u32[]{:S(2)}) copy-start(bf16[2,144,128]{2,1,0:T(8,128)(2,1)} %constant.26.clone.basis_z) | copy-start | bytes 221188
  27.6 1.3 %copy-start.9 = (f32[48,144]{1,0:T(8,128)S(1)}, f32[48,144]{1,0:T(8,128)}, u32[]{:S(2)}) copy-start(f32[48,144]{1,0:T(8,128)} %constant.20.clone.middle) | copy-start | bytes 82948
  27.7 1.2 %copy-start.12 = (bf16[32,144]{1,0:T(8,128)(2,1)S(1)}, bf16[32,144]{1,0:T(8,128)(2,1)}, u32[]{:S(2)}) copy-start(bf16[32,144]{1,0:T(8,128)(2,1)} %constant.25.clone.basis_y) | copy-start | bytes 27652
  30.4 7.1 %collective-permute-start.11 = (f32[2,32,128]{2,1,0:T(8,128)S(1)}, f32[2,32,128]{2,1,0:T(8,128)S(1)}, u32[]{:S(2)}, u32[]{:S(2)}) collective-permute-start(f32[2,32,128]{2,1,0:T(8,128)S(1)} %get-tuple-element.125), channel_id=1, source_target_pairs={{0,8},{8,0},{16,24},{24,16},{1,9},{9,1},{17,25},{25,17},{2,10},{10... | collective-permute-start | bytes 98312 | tf_op jit(solution)/shard_map/ppermute | solution.py:898
  31.3 6.1 %collective-permute-start.12 = (f32[2,32,128]{2,1,0:T(8,128)S(1)}, f32[2,32,128]{2,1,0:T(8,128)S(1)}, u32[]{:S(2)}, u32[]{:S(2)}) collective-permute-start(f32[2,32,128]{2,1,0:T(8,128)S(1)} %get-tuple-element.126), channel_id=1, source_target_pairs={{8,16},{16,8},{24,0},{0,24},{9,17},{17,9},{25,1},{1,25},{10,18},{1... | collective-permute-start | bytes 98312 | tf_op jit(solution)/shard_map/ppermute | solution.py:898
  33.7 3.7 %collective-permute-start.13 = (f32[32,128]{1,0:T(8,128)S(1)}, f32[32,128]{1,0:T(8,128)S(1)}, u32[]{:S(2)}, u32[]{:S(2)}) collective-permute-start(f32[32,128]{1,0:T(8,128)S(1)} %get-tuple-element.127), channel_id=1, source_target_pairs={{0,2},{2,0},{4,6},{6,4},{1,3},{3,1},{5,7},{7,5},{8,10},{10,8},{12,... | collective-permute-start | bytes 49160 | tf_op jit(solution)/shard_map/ppermute | solution.py:898
  33.8 3.7 %collective-permute-start.14 = (f32[32,128]{1,0:T(8,128)S(1)}, f32[32,128]{1,0:T(8,128)S(1)}, u32[]{:S(2)}, u32[]{:S(2)}) collective-permute-start(f32[32,128]{1,0:T(8,128)S(1)} %get-tuple-element.128), channel_id=1, source_target_pairs={{2,4},{4,2},{6,0},{0,6},{3,5},{5,3},{7,1},{1,7},{10,12},{12,10},{1... | collective-permute-start | bytes 49160 | tf_op jit(solution)/shard_map/ppermute | solution.py:898
  33.8 3.6 %collective-permute-start.15 = (f32[8,128]{1,0:T(8,128)S(1)}, f32[8,128]{1,0:T(8,128)S(1)}, u32[]{:S(2)}, u32[]{:S(2)}) collective-permute-start(f32[8,128]{1,0:T(8,128)S(1)} %get-tuple-element.129), channel_id=1, source_target_pairs={{0,1},{1,0},{2,3},{3,2},{4,5},{5,4},{6,7},{7,6},{8,9},{9,8},{10,11... | collective-permute-start | bytes 12296 | tf_op jit(solution)/shard_map/ppermute | solution.py:898
  51.3 6.3 %collective-permute-start.16 = (f32[32,128]{1,0:T(8,128)S(1)}, f32[32,128]{1,0:T(8,128)S(1)}, u32[]{:S(2)}, u32[]{:S(2)}) collective-permute-start(f32[32,128]{1,0:T(8,128)S(1)} %get-tuple-element.158), channel_id=1, source_target_pairs={{0,8},{8,0},{16,24},{24,16},{1,9},{9,1},{17,25},{25,17},{2,10},{10... | collective-permute-start | bytes 49160 | tf_op jit(solution)/shard_map/ppermute | solution.py:898
  51.7 5.8 %collective-permute-start.17 = (f32[32,128]{1,0:T(8,128)S(1)}, f32[32,128]{1,0:T(8,128)S(1)}, u32[]{:S(2)}, u32[]{:S(2)}) collective-permute-start(f32[32,128]{1,0:T(8,128)S(1)} %get-tuple-element.159), channel_id=1, source_target_pairs={{8,16},{16,8},{24,0},{0,24},{9,17},{17,9},{25,1},{1,25},{10,18},{1... | collective-permute-start | bytes 49160 | tf_op jit(solution)/shard_map/ppermute | solution.py:898
  53.2 4.4 %collective-permute-start.18 = (f32[32,128]{1,0:T(8,128)S(1)}, f32[32,128]{1,0:T(8,128)S(1)}, u32[]{:S(2)}, u32[]{:S(2)}) collective-permute-start(f32[32,128]{1,0:T(8,128)S(1)} %get-tuple-element.160), channel_id=1, source_target_pairs={{0,2},{2,0},{4,6},{6,4},{1,3},{3,1},{5,7},{7,5},{8,10},{10,8},{12,... | collective-permute-start | bytes 49160 | tf_op jit(solution)/shard_map/ppermute | solution.py:898
  53.2 4.4 %collective-permute-start.19 = (f32[32,128]{1,0:T(8,128)S(1)}, f32[32,128]{1,0:T(8,128)S(1)}, u32[]{:S(2)}, u32[]{:S(2)}) collective-permute-start(f32[32,128]{1,0:T(8,128)S(1)} %get-tuple-element.161), channel_id=1, source_target_pairs={{2,4},{4,2},{6,0},{0,6},{3,5},{5,3},{7,1},{1,7},{10,12},{12,10},{1... | collective-permute-start | bytes 49160 | tf_op jit(solution)/shard_map/ppermute | solution.py:898
  54.0 3.6 %collective-permute-start.20 = (f32[8,128]{1,0:T(8,128)S(1)}, f32[8,128]{1,0:T(8,128)S(1)}, u32[]{:S(2)}, u32[]{:S(2)}) collective-permute-start(f32[8,128]{1,0:T(8,128)S(1)} %get-tuple-element.162), channel_id=1, source_target_pairs={{0,1},{1,0},{2,3},{3,2},{4,5},{5,4},{6,7},{7,6},{8,9},{9,8},{10,11... | collective-permute-start | bytes 12296 | tf_op jit(solution)/shard_map/ppermute | solution.py:898
  59.2 8.2 %collective-permute-start.21 = (f32[32,128]{1,0:T(8,128)S(1)}, f32[32,128]{1,0:T(8,128)S(1)}, u32[]{:S(2)}, u32[]{:S(2)}) collective-permute-start(f32[32,128]{1,0:T(8,128)S(1)} %get-tuple-element.166), channel_id=1, source_target_pairs={{0,8},{8,0},{16,24},{24,16},{1,9},{9,1},{17,25},{25,17},{2,10},{10... | collective-permute-start | bytes 49160 | tf_op jit(solution)/shard_map/ppermute | solution.py:898
  59.2 8.1 %collective-permute-start.22 = (f32[32,128]{1,0:T(8,128)S(1)}, f32[32,128]{1,0:T(8,128)S(1)}, u32[]{:S(2)}, u32[]{:S(2)}) collective-permute-start(f32[32,128]{1,0:T(8,128)S(1)} %get-tuple-element.167), channel_id=1, source_target_pairs={{8,16},{16,8},{24,0},{0,24},{9,17},{17,9},{25,1},{1,25},{10,18},{1... | collective-permute-start | bytes 49160 | tf_op jit(solution)/shard_map/ppermute | solution.py:898
  62.1 5.3 %collective-permute-start.23 = (f32[32,128]{1,0:T(8,128)S(1)}, f32[32,128]{1,0:T(8,128)S(1)}, u32[]{:S(2)}, u32[]{:S(2)}) collective-permute-start(f32[32,128]{1,0:T(8,128)S(1)} %get-tuple-element.168), channel_id=1, source_target_pairs={{0,2},{2,0},{4,6},{6,4},{1,3},{3,1},{5,7},{7,5},{8,10},{10,8},{12,... | collective-permute-start | bytes 49160 | tf_op jit(solution)/shard_map/ppermute | solution.py:898
  62.1 5.3 %collective-permute-start.24 = (f32[32,128]{1,0:T(8,128)S(1)}, f32[32,128]{1,0:T(8,128)S(1)}, u32[]{:S(2)}, u32[]{:S(2)}) collective-permute-start(f32[32,128]{1,0:T(8,128)S(1)} %get-tuple-element.169), channel_id=1, source_target_pairs={{2,4},{4,2},{6,0},{0,6},{3,5},{5,3},{7,1},{1,7},{10,12},{12,10},{1... | collective-permute-start | bytes 49160 | tf_op jit(solution)/shard_map/ppermute | solution.py:898
  63.7 3.6 %collective-permute-start.25 = (f32[8,128]{1,0:T(8,128)S(1)}, f32[8,128]{1,0:T(8,128)S(1)}, u32[]{:S(2)}, u32[]{:S(2)}) collective-permute-start(f32[8,128]{1,0:T(8,128)S(1)} %get-tuple-element.170), channel_id=1, source_target_pairs={{0,1},{1,0},{2,3},{3,2},{4,5},{5,4},{6,7},{7,6},{8,9},{9,8},{10,11... | collective-permute-start | bytes 12296 | tf_op jit(solution)/shard_map/ppermute | solution.py:898

commit v5 on v4

--- a/solution.py
+++ b/solution.py
@@ -20,7 +20,7 @@
 AXES = ("gx", "gy", "gz")
 F32 = jnp.float32
 MSG_ROWS = 16
-CHUNKS = 4
+CHUNKS = 2
 
 
 def sine_basis(length):
@@ -180,9 +180,15 @@
     if len(vals) > 1:
         vals = list(z_sides(plan, vals))
     for val, out in zip(vals, outs):
-        turned = jnp.transpose(val)
-        for r in range(val.shape[0]):
-            out[r * 128 : (r + 1) * 128, :] = jnp.broadcast_to(turned[:, r : r + 1], (128, 128))
+        high = val.astype(jnp.bfloat16)
+        mid, low = halves(val - high.astype(F32))
+        split = jnp.concatenate([v.astype(F32) for v in (high, mid, low)], axis=0)
+        blocks = val.shape[0]
+        shape = (3 * blocks, blocks * 128)
+        pick = (rows_of(shape) % blocks == lanes_of(shape) // 128).astype(F32).astype(jnp.bfloat16)
+        wide = mxu(split.astype(jnp.bfloat16), pick, ((0,), (0,)))
+        for r in range(blocks):
+            out[r * 128 : (r + 1) * 128, :] = wide[:, r * 128 : (r + 1) * 128]
 
 
 def stack_rows(parts):
@@ -663,7 +669,7 @@
     zero = jnp.zeros((ny, nz), F32)
     low = side(plan, "gx", xa[0], xb[0], False)
     top = side(plan, "gx", xa[0], xb[0], True)
-    d, im, rd, da = lax.fori_loop(0, nx, layer, (low, zero, zero, zero), unroll=16)
+    d, im, rd, da = lax.fori_loop(0, nx, layer, (low, zero, zero, zero), unroll=32)
     flux = tx[nx] * (d - top)
     gx[nx] = flux
     im = im + flux
@@ -677,7 +683,7 @@
     return g * jnp.where(g > 0.0, low, high)
 
 
-def sweep(plan, refs, x_low, x_top, hy, z_at, done):
+def sweep(plan, refs, x_low, x_top, hy, z_at, done, chunk_done=None):
     nx, ny, nz = plan.nx, plan.ny, plan.nz
     (now, frac, coef, rate, anchor, gx, gy_low, gy_top, gz_low, gz_top, outflow) = refs
     lane = lanes_of((ny, nz))
@@ -707,7 +713,14 @@
         return f_next, flow_next
 
     f0 = frac[0]
-    lax.fori_loop(0, nx, layer, (f0, upwind(gx[0], x_low, f0)), unroll=16)
+    carry = (f0, upwind(gx[0], x_low, f0))
+    if chunk_done is None:
+        lax.fori_loop(0, nx, layer, carry, unroll=16)
+    else:
+        size = nx // CHUNKS
+        for c in range(CHUNKS):
+            carry = lax.fori_loop(c * size, (c + 1) * size, layer, carry, unroll=size)
+            chunk_done(c)
 
 
 def keep(plan, new, new_frac, tile):
@@ -734,21 +747,10 @@
     return both[:, 0:1] / both[:, 64:65]
 
 
-def write_out(plan, i, ref, out, sem):
+def write_part(plan, c, ref, out, sem):
     size = plan.nx // CHUNKS
-
-    @pl.when(i % size == size - 1)
-    def _():
-        c = i // size
-        cut = pl.ds(c * size, size)
-        pltpu.make_async_copy(ref.at[cut], out.at[cut], sem.at[c]).start()
-
-
-def write_end(plan, ref, out, sem):
-    size = plan.nx // CHUNKS
-    for c in range(CHUNKS):
-        cut = pl.ds(c * size, size)
-        pltpu.make_async_copy(ref.at[cut], out.at[cut], sem.at[c]).wait()
+    cut = pl.ds(c * size, size)
+    return pltpu.make_async_copy(ref.at[cut], out.at[cut], sem.at[c])
 
 
 def output_kernel(plan, sums, press, direction, full, image, p_out, r_out, token, p_new, r_new, p_sem, r_sem):
@@ -756,15 +758,19 @@
 
     def layer(i, carry):
         p_new[i] = press[i] + step * direction[i]
-        write_out(plan, i, p_new, p_out, p_sem)
         r_new[i] = full[i] - step * image[i]
-        write_out(plan, i, r_new, r_out, r_sem)
         return carry
 
-    lax.fori_loop(0, plan.nx, layer, 0, unroll=4)
+    size = plan.nx // CHUNKS
+    pairs_out = ((p_new, p_out, p_sem), (r_new, r_out, r_sem))
+    for c in range(CHUNKS):
+        lax.fori_loop(c * size, (c + 1) * size, layer, 0, unroll=size)
+        for refs in pairs_out:
+            write_part(plan, c, *refs).start()
     token[...] = jnp.zeros(token.shape, F32)
-    write_end(plan, p_new, p_out, p_sem)
-    write_end(plan, r_new, r_out, r_sem)
+    for c in range(CHUNKS):
+        for refs in pairs_out:
+            write_part(plan, c, *refs).wait()
 
 
 def step_kernel(plan, *refs):
@@ -833,12 +839,15 @@
 
         def done(i, s, c):
             new[i] = s
-            write_out(plan, i, new, out, sem)
+
+        def chunk_done(c):
+            write_part(plan, c, new, out, sem).start()
     else:
         new, new_frac = rest[:2]
         packs = rest[2 : 6 + n_msg]
         tile, fh, *hz = rest[6 + n_msg :]
         done = keep(plan, new, new_frac, tile)
+        chunk_done = None
     spread(plan, got, hz)
     fh[0] = side(plan, "gy", ya[...], yb[...], False)
     fh[1] = side(plan, "gy", ya[...], yb[...], True)
@@ -850,10 +859,11 @@
     sweep(
         plan, fields,
         side(plan, "gx", xa[...], xb[...], False), side(plan, "gx", xa[...], xb[...], True),
-        fh, z_at, done,
+        fh, z_at, done, chunk_done,
     )
     if last_sweep:
-        write_end(plan, new, out, sem)
+        for c in range(CHUNKS):
+            write_part(plan, c, new, out, sem).wait()
     else:
         pack_all(plan, new_frac, tile, packs)
 

time: 69.5 us -> 68.9 us (level)
  no operation moved by 1% of the time
where the time goes in v5:
time: 68.9 us; the launch traced here: 68.7 us
  starting transfers between devices  26.9 us (39%)
  Pallas kernels  17.9 us (26%)
  waiting for transfers between devices  11.7 us (17%)
  blocking collectives  11.3 us (16%)
  between operations  0.91 us (1%)
    ppermute x26, starting transfers between devices, send(): return lax.ppermute(value, axis, plan.perm(axis, which))  26.9 us
    pallas_call x15, Pallas kernels, call(): pl.pallas_call(kernel, out_shape=[jax.ShapeDtypeStruct(s, F32) for s in o...  17.9 us
    ppermute x26, waiting for transfers between devices, send(): return lax.ppermute(value, axis, plan.perm(axis, which))  11.7 us
    all_to_all x1, blocking collectives, per_device(): sums = lax.all_to_all(sums, AXES, 0, 0, tiled=True)  11.3 us
  transfers between devices with their start and end apart: 26, of which 7 were waited for; matrix products, arithmetic and copies ran while one was open for 0% of the time, Pallas kernels for 11%

profile of v5, /device:TPU:0, one launch (start us, length us, event | category | flops | bytes accessed | tf_op | source)
XLA Modules:
  0.0 68.7 jit_solution(12376675682921938151)
XLA Ops:
  0.7 2.0 %shard_map.202 = (f32[32,32,128]{2,1,0:T(8,128)S(1)}, f32[32,32,128]{2,1,0:T(8,128)S(1)}, f32[32,32,128]{2,1,0:T(8,128)S(1)}, f32[32,32,128]{2,1,0:T(8,128)S(1)}...) custom-call(f32[32,32,128]{2,1,0:T(8,128)} %press_in.1, ...), custom_call_target="tpu_custom_call" | custom-call | tf_op jit(solution)/shard_map/pallas_call | solution.py:126
  2.6 0.6 collective-permute-start.2
  3.2 2.6 %collective-permute-start.3 = (f32[3,32,128]{2,1,0:T(8,128)S(1)}, f32[3,32,128]{2,1,0:T(8,128)S(1)}, u32[]{:S(2)}, u32[]{:S(2)}) collective-permute-start(f32[3,32,128]{2,1,0:T(8,128)S(1)} %get-tuple-element.94), channel_id=1, source_target_pairs={{2,4},{4,2},{6,0},{0,6},{3,5},{5,3},{7,1},{1,7},{10,12},{12,10},{1... | collective-permute-start | bytes 147464 | tf_op jit(solution)/shard_map/ppermute | solution.py:908
  5.8 1.6 %collective-permute-start = (f32[2,32,128]{2,1,0:T(8,128)S(1)}, f32[2,32,128]{2,1,0:T(8,128)S(1)}, u32[]{:S(2)}, u32[]{:S(2)}) collective-permute-start(f32[2,32,128]{2,1,0:T(8,128)S(1)} %get-tuple-element.91), channel_id=1, source_target_pairs={{0,8},{8,0},{16,24},{24,16},{1,9},{9,1},{17,25},{25,17},{2,10},{10... | collective-permute-start | bytes 98312 | tf_op jit(solution)/shard_map/ppermute | solution.py:908
  7.4 2.5 %collective-permute-start.1 = (f32[2,32,128]{2,1,0:T(8,128)S(1)}, f32[2,32,128]{2,1,0:T(8,128)S(1)}, u32[]{:S(2)}, u32[]{:S(2)}) collective-permute-start(f32[2,32,128]{2,1,0:T(8,128)S(1)} %get-tuple-element.92), channel_id=1, source_target_pairs={{8,16},{16,8},{24,0},{0,24},{9,17},{17,9},{25,1},{1,25},{10,18},{1... | collective-permute-start | bytes 98312 | tf_op jit(solution)/shard_map/ppermute | solution.py:908
  9.8 1.7 %shard_map.203 = (f32[32,32,128]{2,1,0:T(8,128)S(1)}, f32[32,32,128]{2,1,0:T(8,128)S(1)}, f32[32,32,128]{2,1,0:T(8,128)S(1)}, f32[32,32,128]{2,1,0:T(8,128)S(1)}...) custom-call(f32[32,32,128]{2,1,0:T(8,128)S(1)} %get-tuple-element.87.press, ...), custom_call_target="tpu_custom_call" | custom-call | tf_op jit(solution)/shard_map/pallas_call | solution.py:126
  11.5 0.0 copy-start.3
  11.5 0.0 collective-permute-done.xa
  11.5 1.5 %collective-permute-done.1.xb = f32[2,32,128]{2,1,0:T(8,128)S(1)} collective-permute-done((f32[2,32,128]{2,1,0:T(8,128)S(1)}, f32[2,32,128]{2,1,0:T(8,128)S(1)}, u32[]{:S(2)}, u32[]{:S(2)}) %collective-permute-start.1) | collective-permute-done | bytes 32800 | tf_op jit(solution)/shard_map/ppermute | solution.py:908
  13.1 0.0 collective-permute-done.2.ya
  13.1 0.0 collective-permute-done.3.yb
  13.1 0.4 shard_map.204
  13.4 1.6 %collective-permute-start.4 = (f32[88,128]{1,0:T(8,128)S(1)}, f32[88,128]{1,0:T(8,128)S(1)}, u32[]{:S(2)}, u32[]{:S(2)}) collective-permute-start(f32[88,128]{1,0:T(8,128)S(1)} %get-tuple-element.102.rest_0_), channel_id=1, source_target_pairs={{0,1},{1,0},{2,3},{3,2},{4,5},{5,4},{6,7},{7,6},{8,9},{9,8},{10,11... | collective-permute-start | bytes 135176 | tf_op jit(solution)/shard_map/ppermute | solution.py:908
  15.0 0.7 shard_map.205
  15.7 0.0 copy-start
  15.7 0.0 copy-start.7
  15.7 1.8 %collective-permute-done.4.rest_1_ = f32[88,128]{1,0:T(8,128)S(1)} collective-permute-done((f32[88,128]{1,0:T(8,128)S(1)}, f32[88,128]{1,0:T(8,128)S(1)}, u32[]{:S(2)}, u32[]{:S(2)}) %collective-permute-start.4) | collective-permute-done | bytes 45088 | tf_op jit(solution)/shard_map/ppermute | solution.py:908
  17.6 0.8 %shard_map.206 = (f32[32,32,144]{2,1,0:T(8,128)S(1)}, f32[18,8,128]{2,1,0:T(8,128)S(1)}, f32[18,8,128]{2,1,0:T(8,128)S(1)}, f32[18,8,128]{2,1,0:T(8,128)S(1)}, f32[18,8,128]{2,1,0:T(8,128)S(1)}) custom-call(f32[32,32,128]{2,1,0:T(8,128)S(1)} %get-tuple-element.96.res, bf16[384,144]{1,0:T(8,128)(2,1)S(1)} %copy-done.6, f32[48,144]{1,0:T(8,128)S(1)} %copy-done.10, ...), custom_call_target="tpu_custom_call" | custom-call | tf_op jit(solution)/shard_map/pallas_call | solution.py:126
  18.4 0.1 collective-permute-start.7
  18.5 0.6 collective-permute-start.8
  19.1 0.1 collective-permute-start.5
  19.2 1.5 %collective-permute-start.6 = (f32[18,8,128]{2,1,0:T(8,128)S(1)}, f32[18,8,128]{2,1,0:T(8,128)S(1)}, u32[]{:S(2)}, u32[]{:S(2)}) collective-permute-start(f32[18,8,128]{2,1,0:T(8,128)S(1)} %get-tuple-element.105), channel_id=1, source_target_pairs={{2,4},{4,2},{6,0},{0,6},{3,5},{5,3},{7,1},{1,7},{10,12},{12,10},{1... | collective-permute-start | bytes 221192 | tf_op jit(solution)/shard_map/ppermute | solution.py:908
  20.7 0.8 %shard_map.207 = (f32[32,32,128]{2,1,0:T(8,128)S(1)}, f32[1024,128]{1,0:T(8,128)S(1)}, f32[1024,128]{1,0:T(8,128)S(1)}) custom-call(f32[32,32,128]{2,1,0:T(8,128)S(1)} %get-tuple-element.96.res, f32[88,128]{1,0:T(8,128)S(1)} %get-tuple-element.102.rest_0_, f32[88,128]{1,0:T(8,128)S(1)} %collective-permute-done.4.rest_1_), custom_call_target="tpu_custom_call" | custom-call | tf_op jit(solution)/shard_map/pallas_call | solution.py:126
  21.5 0.0 collective-permute-done.7.ya
  21.6 0.9 %collective-permute-done.8.yb = f32[18,8,128]{2,1,0:T(8,128)S(1)} collective-permute-done((f32[18,8,128]{2,1,0:T(8,128)S(1)}, f32[18,8,128]{2,1,0:T(8,128)S(1)}, u32[]{:S(2)}, u32[]{:S(2)}) %collective-permute-start.8) | collective-permute-done | bytes 73760 | tf_op jit(solution)/shard_map/ppermute | solution.py:908
  22.5 0.5 shard_map.208
  23.0 0.0 collective-permute-start.9
  23.0 2.5 %collective-permute-start.10 = (f32[56,128]{1,0:T(8,128)S(1)}, f32[56,128]{1,0:T(8,128)S(1)}, u32[]{:S(2)}, u32[]{:S(2)}) collective-permute-start(f32[56,128]{1,0:T(8,128)S(1)} %get-tuple-element.111), channel_id=1, source_target_pairs={{8,16},{16,8},{24,0},{0,24},{9,17},{17,9},{25,1},{1,25},{10,18},{1... | collective-permute-start | bytes 86024 | tf_op jit(solution)/shard_map/ppermute | solution.py:908
  25.5 2.0 %shard_map.210 = (f32[32,32,128]{2,1,0:T(8,128)S(1)}, f32[32,32,128]{2,1,0:T(8,128)S(1)}, f32[32,32,128]{2,1,0:T(8,128)S(1)}, f32[32,32,128]{2,1,0:T(8,128)S(1)}) custom-call(f32[32,32,128]{2,1,0:T(8,128)S(1)} %get-tuple-element.87.press, f32[32,32,128]{2,1,0:T(8,128)S(1)} %get-tuple-element.115.tz_in, f32[1024,128]{1,0:T(8,128)S(1)} %get-tuple-element.116.hz, ...), custom_call_target="tpu_custom_call" | custom-call | tf_op jit(solution)/shard_map/pallas_call | solution.py:126
  27.5 0.0 copy-start.2
  27.6 0.0 copy-start.8
  27.6 0.0 copy-start.9
  27.6 0.0 copy-start.12
  27.6 0.0 collective-permute-done.6.yb
  27.6 0.9 %shard_map.209.zed = f32[32,48,144]{2,1,0:T(8,128)S(1)} custom-call(f32[32,32,144]{2,1,0:T(8,128)S(1)} %get-tuple-element.103.spec, f32[18,8,128]{2,1,0:T(8,128)S(1)} %collective-permute-done.5.ya, f32[18,8,128]{2,1,0:T(8,128)S(1)} %collective-permute-done.6.yb, bf16[48,144]{1,0:T(8,128)(2,1)S(1)} %copy-done.7, f32[24,48,144]{2,1,0:T(8,128)S(1)} %copy-done, ...), custom_call_target="tpu_custom_call" | custom-call | tf_op jit(solution)/shard_map/pallas_call | solution.py:126
  28.5 0.0 collective-permute-done.9.xa
  28.5 0.3 collective-permute-done.10.xb
  28.8 1.4 %shard_map.211 = (f32[32,32,128]{2,1,0:T(8,128)S(1)}, f32[2,32,128]{2,1,0:T(8,128)S(1)}, f32[2,32,128]{2,1,0:T(8,128)S(1)}, f32[32,128]{1,0:T(8,128)S(1)}, f32[32,128]{1,0:T(8,128)S(1)}, /*index=5*/f32[8,128]{1,0:T(8,128)S(1)}) custom-call(f32[32,48,144]{2,1,0:T(8,128)S(1)} %shard_map.209.zed, f32[56,128]{1,0:T(8,128)S(1)} %collective-permute-done.9.xa, ...), custom_call_target="tpu_custom_call" | custom-call | tf_op jit(solution)/shard_map/pallas_call | solution.py:126
  30.3 0.9 %collective-permute-start.11 = (f32[2,32,128]{2,1,0:T(8,128)S(1)}, f32[2,32,128]{2,1,0:T(8,128)S(1)}, u32[]{:S(2)}, u32[]{:S(2)}) collective-permute-start(f32[2,32,128]{2,1,0:T(8,128)S(1)} %get-tuple-element.125), channel_id=1, source_target_pairs={{0,8},{8,0},{16,24},{24,16},{1,9},{9,1},{17,25},{25,17},{2,10},{10... | collective-permute-start | bytes 98312 | tf_op jit(solution)/shard_map/ppermute | solution.py:908
  31.2 2.5 %collective-permute-start.12 = (f32[2,32,128]{2,1,0:T(8,128)S(1)}, f32[2,32,128]{2,1,0:T(8,128)S(1)}, u32[]{:S(2)}, u32[]{:S(2)}) collective-permute-start(f32[2,32,128]{2,1,0:T(8,128)S(1)} %get-tuple-element.126), channel_id=1, source_target_pairs={{8,16},{16,8},{24,0},{0,24},{9,17},{17,9},{25,1},{1,25},{10,18},{1... | collective-permute-start | bytes 98312 | tf_op jit(solution)/shard_map/ppermute | solution.py:908
  33.7 0.1 collective-permute-start.14
  33.7 1.5 %collective-permute-start.15 = (f32[8,128]{1,0:T(8,128)S(1)}, f32[8,128]{1,0:T(8,128)S(1)}, u32[]{:S(2)}, u32[]{:S(2)}) collective-permute-start(f32[8,128]{1,0:T(8,128)S(1)} %get-tuple-element.129), channel_id=1, source_target_pairs={{0,1},{1,0},{2,3},{3,2},{4,5},{5,4},{6,7},{7,6},{8,9},{9,8},{10,11... | collective-permute-start | bytes 12296 | tf_op jit(solution)/shard_map/ppermute | solution.py:908
  35.2 2.1 %collective-permute-done.15.rest_0_ = f32[8,128]{1,0:T(8,128)S(1)} collective-permute-done((f32[8,128]{1,0:T(8,128)S(1)}, f32[8,128]{1,0:T(8,128)S(1)}, u32[]{:S(2)}, u32[]{:S(2)}) %collective-permute-start.15) | collective-permute-done | bytes 4128 | tf_op jit(solution)/shard_map/ppermute | solution.py:908
  37.3 0.0 collective-permute-done.11.xa.refs_18_
  37.3 0.0 collective-permute-done.12.xb.refs_19_
  37.3 0.8 %shard_map.212 = (f32[32,32,128]{2,1,0:T(8,128)S(1)}, f32[32,128]{1,0:T(8,128)S(1)}, f32[33,32,128]{2,1,0:T(8,128)S(1)}, f32[32,32,128]{2,1,0:T(8,128)S(1)}, f32...) custom-call(f32[32,32,128]{2,1,0:T(8,128)S(1)} %get-tuple-element.118.direction, ...), custom_call_target="tpu_custom_call" | custom-call | tf_op jit(solution)/shard_map/pallas_call | solution.py:126
  38.2 11.3 %all_to_all.11 = f32[32,1,128]{2,1,0:T(1,128)S(1)} all-to-all(f32[32,1,128]{2,1,0:T(1,128)S(1)} %bitcast.6), channel_id=1, replica_groups=mesh['gx'=4,'gy'=4,'gz'=2] {'gx','gy','gz'}, dimensions={0} | all-to-all | bytes 32768 | tf_op jit(solution)/shard_map/all_to_all | solution.py:1003
  49.4 1.6 %shard_map.214 = (f32[32,32,128]{2,1,0:T(8,128)S(1)}, f32[32,32,128]{2,1,0:T(8,128)S(1)}, f32[33,32,128]{2,1,0:T(8,128)S(1)}, f32[32,32,128]{2,1,0:T(8,128)S(1)}...) custom-call(f32[32,128]{1,0:T(8,128)S(1)} %bitcast.4, ...), custom_call_target="tpu_custom_call" | custom-call | tf_op jit(solution)/shard_map/pallas_call | solution.py:126
  51.0 0.5 collective-permute-start.16
  51.5 1.5 %collective-permute-start.17 = (f32[32,128]{1,0:T(8,128)S(1)}, f32[32,128]{1,0:T(8,128)S(1)}, u32[]{:S(2)}, u32[]{:S(2)}) collective-permute-start(f32[32,128]{1,0:T(8,128)S(1)} %get-tuple-element.159), channel_id=1, source_target_pairs={{8,16},{16,8},{24,0},{0,24},{9,17},{17,9},{25,1},{1,25},{10,18},{1... | collective-permute-start | bytes 49160 | tf_op jit(solution)/shard_map/ppermute | solution.py:908
  53.0 0.0 collective-permute-start.18
  53.0 0.7 %collective-permute-start.19 = (f32[32,128]{1,0:T(8,128)S(1)}, f32[32,128]{1,0:T(8,128)S(1)}, u32[]{:S(2)}, u32[]{:S(2)}) collective-permute-start(f32[32,128]{1,0:T(8,128)S(1)} %get-tuple-element.161), channel_id=1, source_target_pairs={{2,4},{4,2},{6,0},{0,6},{3,5},{5,3},{7,1},{1,7},{10,12},{12,10},{1... | collective-permute-start | bytes 49160 | tf_op jit(solution)/shard_map/ppermute | solution.py:908
  53.7 0.5 collective-permute-start.20
  54.2 1.2 %shard_map.213 = (f32[32,32,128]{2,1,0:T(8,128)}, f32[32,32,128]{2,1,0:T(8,128)}, f32[8,128]{1,0:T(8,128)S(1)}) custom-call(f32[32,128]{1,0:T(8,128)S(1)} %bitcast.5, f32[32,32,128]{2,1,0:T(8,128)S(1)} %get-tuple-element.87.press, f32[32,32,128]{2,1,0:T(8,128)S(1)} %get-tuple-element.118.direction, f32[32,32,128]{2,1,0:T(8,128)S(1)} %get-tuple-element.108.order.full, ...), custom_call_target="tpu_custom_call" | custom-call | tf_op jit(solution)/shard_map/pallas_call | solution.py:126
  55.4 1.9 %collective-permute-done.20.refs_15_ = f32[8,128]{1,0:T(8,128)S(1)} collective-permute-done((f32[8,128]{1,0:T(8,128)S(1)}, f32[8,128]{1,0:T(8,128)S(1)}, u32[]{:S(2)}, u32[]{:S(2)}) %collective-permute-start.20) | collective-permute-done | bytes 4128 | tf_op jit(solution)/shard_map/ppermute | solution.py:908
  57.3 0.0 collective-permute-done.16.refs_11_
  57.3 0.0 collective-permute-done.17.refs_12_
  57.3 1.5 %shard_map.215 = (f32[32,32,128]{2,1,0:T(8,128)S(1)}, f32[32,32,128]{2,1,0:T(8,128)S(1)}, f32[32,128]{1,0:T(8,128)S(1)}, f32[32,128]{1,0:T(8,128)S(1)}, f32[32,1...) custom-call(f32[32,32,128]{2,1,0:T(8,128)S(1)} %get-tuple-element.148.refs_0_, ...), custom_call_target="tpu_custom_call" | custom-call | tf_op jit(solution)/shard_map/pallas_call | solution.py:126
  58.8 0.0 collective-permute-start.21
  58.9 2.9 %collective-permute-start.22 = (f32[32,128]{1,0:T(8,128)S(1)}, f32[32,128]{1,0:T(8,128)S(1)}, u32[]{:S(2)}, u32[]{:S(2)}) collective-permute-start(f32[32,128]{1,0:T(8,128)S(1)} %get-tuple-element.167), channel_id=1, source_target_pairs={{8,16},{16,8},{24,0},{0,24},{9,17},{17,9},{25,1},{1,25},{10,18},{1... | collective-permute-start | bytes 49160 | tf_op jit(solution)/shard_map/ppermute | solution.py:908
  61.8 1.6 %collective-permute-start.24 = (f32[32,128]{1,0:T(8,128)S(1)}, f32[32,128]{1,0:T(8,128)S(1)}, u32[]{:S(2)}, u32[]{:S(2)}) collective-permute-start(f32[32,128]{1,0:T(8,128)S(1)} %get-tuple-element.169), channel_id=1, source_target_pairs={{2,4},{4,2},{6,0},{0,6},{3,5},{5,3},{7,1},{1,7},{10,12},{12,10},{1... | collective-permute-start | bytes 49160 | tf_op jit(solution)/shard_map/ppermute | solution.py:908
  63.4 0.5 collective-permute-start.25
  63.9 3.1 %collective-permute-done.25.refs_15_ = f32[8,128]{1,0:T(8,128)S(1)} collective-permute-done((f32[8,128]{1,0:T(8,128)S(1)}, f32[8,128]{1,0:T(8,128)S(1)}, u32[]{:S(2)}, u32[]{:S(2)}) %collective-permute-start.25) | collective-permute-done | bytes 4128 | tf_op jit(solution)/shard_map/ppermute | solution.py:908
  67.0 1.7 %shard_map.216 = f32[32,32,128]{2,1,0:T(8,128)} custom-call(f32[32,32,128]{2,1,0:T(8,128)S(1)} %get-tuple-element.164.refs_0_, f32[32,32,128]{2,1,0:T(8,128)S(1)} %get-tuple-element.165.refs_1_, f32[32,32,128]{2,1,0:T(8,128)S(1)} %get-tuple-element.98.coef.refs_13_.refs_2_, f32[32,32,128]{2,1,0:T(8,128)S(1)} %get-tuple-element.150.refs_3_, ...), custom_call_target="tpu_custom_call" | custom-call | tf_op jit(solution)/shard_map/pallas_call | solution.py:126
  (30 shorter events, 0.1 us)
Async XLA Ops:
  0.6 9.2 %copy-start.4 = (f32[32,32,128]{2,1,0:T(8,128)S(1)}, f32[32,32,128]{2,1,0:T(8,128)}, u32[]{:S(2)}) copy-start(f32[32,32,128]{2,1,0:T(8,128)} %source.1) | copy-start | bytes 1572868
  0.6 9.2 %copy-start.5 = (f32[32,32,128]{2,1,0:T(8,128)S(1)}, f32[32,32,128]{2,1,0:T(8,128)}, u32[]{:S(2)}) copy-start(f32[32,32,128]{2,1,0:T(8,128)} %compress.1) | copy-start | bytes 1572868
  0.7 9.2 %copy-start.1 = (s32[32,32,128]{2,1,0:T(8,128)S(1)}, s32[32,32,128]{2,1,0:T(8,128)}, u32[]{:S(2)}) copy-start(s32[32,32,128]{2,1,0:T(8,128)} %well.3) | copy-start | bytes 1572868
  2.6 10.4 %collective-permute-start.2 = (f32[3,32,128]{2,1,0:T(8,128)S(1)}, f32[3,32,128]{2,1,0:T(8,128)S(1)}, u32[]{:S(2)}, u32[]{:S(2)}) collective-permute-start(f32[3,32,128]{2,1,0:T(8,128)S(1)} %get-tuple-element.93), channel_id=1, source_target_pairs={{0,2},{2,0},{4,6},{6,4},{1,3},{3,1},{5,7},{7,5},{8,10},{10,8},{12,... | collective-permute-start | bytes 147464 | tf_op jit(solution)/shard_map/ppermute | solution.py:908
  3.2 9.9 %collective-permute-start.3 = (f32[3,32,128]{2,1,0:T(8,128)S(1)}, f32[3,32,128]{2,1,0:T(8,128)S(1)}, u32[]{:S(2)}, u32[]{:S(2)}) collective-permute-start(f32[3,32,128]{2,1,0:T(8,128)S(1)} %get-tuple-element.94), channel_id=1, source_target_pairs={{2,4},{4,2},{6,0},{0,6},{3,5},{5,3},{7,1},{1,7},{10,12},{12,10},{1... | collective-permute-start | bytes 147464 | tf_op jit(solution)/shard_map/ppermute | solution.py:908
  5.8 5.7 %collective-permute-start = (f32[2,32,128]{2,1,0:T(8,128)S(1)}, f32[2,32,128]{2,1,0:T(8,128)S(1)}, u32[]{:S(2)}, u32[]{:S(2)}) collective-permute-start(f32[2,32,128]{2,1,0:T(8,128)S(1)} %get-tuple-element.91), channel_id=1, source_target_pairs={{0,8},{8,0},{16,24},{24,16},{1,9},{9,1},{17,25},{25,17},{2,10},{10... | collective-permute-start | bytes 98312 | tf_op jit(solution)/shard_map/ppermute | solution.py:908
  7.4 5.7 %collective-permute-start.1 = (f32[2,32,128]{2,1,0:T(8,128)S(1)}, f32[2,32,128]{2,1,0:T(8,128)S(1)}, u32[]{:S(2)}, u32[]{:S(2)}) collective-permute-start(f32[2,32,128]{2,1,0:T(8,128)S(1)} %get-tuple-element.92), channel_id=1, source_target_pairs={{8,16},{16,8},{24,0},{0,24},{9,17},{17,9},{25,1},{1,25},{10,18},{1... | collective-permute-start | bytes 98312 | tf_op jit(solution)/shard_map/ppermute | solution.py:908
  11.5 3.5 %copy-start.3 = (f32[32,32,128]{2,1,0:T(8,128)S(1)}, f32[32,32,128]{2,1,0:T(8,128)}, u32[]{:S(2)}) copy-start(f32[32,32,128]{2,1,0:T(8,128)} %poro.1) | copy-start | bytes 1572868
  13.4 4.1 %collective-permute-start.4 = (f32[88,128]{1,0:T(8,128)S(1)}, f32[88,128]{1,0:T(8,128)S(1)}, u32[]{:S(2)}, u32[]{:S(2)}) collective-permute-start(f32[88,128]{1,0:T(8,128)S(1)} %get-tuple-element.102.rest_0_), channel_id=1, source_target_pairs={{0,1},{1,0},{2,3},{3,2},{4,5},{5,4},{6,7},{7,6},{8,9},{9,8},{10,11... | collective-permute-start | bytes 135176 | tf_op jit(solution)/shard_map/ppermute | solution.py:908
  15.0 2.5 %copy-start.6 = (bf16[384,144]{1,0:T(8,128)(2,1)S(1)}, bf16[384,144]{1,0:T(8,128)(2,1)}, u32[]{:S(2)}) copy-start(bf16[384,144]{1,0:T(8,128)(2,1)} %constant.23.clone.basis) | copy-start | bytes 331780
  15.0 2.5 %copy-start.10 = (f32[48,144]{1,0:T(8,128)S(1)}, f32[48,144]{1,0:T(8,128)}, u32[]{:S(2)}) copy-start(f32[48,144]{1,0:T(8,128)} %constant.27.rim_low) | copy-start | bytes 82948
  15.0 2.5 %copy-start.11 = (f32[48,144]{1,0:T(8,128)S(1)}, f32[48,144]{1,0:T(8,128)}, u32[]{:S(2)}) copy-start(f32[48,144]{1,0:T(8,128)} %constant.28.rim_top) | copy-start | bytes 82948
  15.7 6.8 %copy-start = (f32[24,48,144]{2,1,0:T(8,128)S(1)}, f32[24,48,144]{2,1,0:T(8,128)}, u32[]{:S(2)}) copy-start(f32[24,48,144]{2,1,0:T(8,128)} %constant.18.clone.factors) | copy-start | bytes 1990660
  15.7 6.8 %copy-start.7 = (bf16[48,144]{1,0:T(8,128)(2,1)S(1)}, bf16[48,144]{1,0:T(8,128)(2,1)}, u32[]{:S(2)}) copy-start(bf16[48,144]{1,0:T(8,128)(2,1)} %constant.24.clone.basis) | copy-start | bytes 41476
  18.4 3.2 %collective-permute-start.7 = (f32[18,8,128]{2,1,0:T(8,128)S(1)}, f32[18,8,128]{2,1,0:T(8,128)S(1)}, u32[]{:S(2)}, u32[]{:S(2)}) collective-permute-start(f32[18,8,128]{2,1,0:T(8,128)S(1)} %get-tuple-element.106), channel_id=1, source_target_pairs={{0,2},{2,0},{4,6},{6,4},{1,3},{3,1},{5,7},{7,5},{8,10},{10,8},{12,... | collective-permute-start | bytes 221192 | tf_op jit(solution)/shard_map/ppermute | solution.py:908
  18.5 4.0 %collective-permute-start.8 = (f32[18,8,128]{2,1,0:T(8,128)S(1)}, f32[18,8,128]{2,1,0:T(8,128)S(1)}, u32[]{:S(2)}, u32[]{:S(2)}) collective-permute-start(f32[18,8,128]{2,1,0:T(8,128)S(1)} %get-tuple-element.107), channel_id=1, source_target_pairs={{2,4},{4,2},{6,0},{0,6},{3,5},{5,3},{7,1},{1,7},{10,12},{12,10},{1... | collective-permute-start | bytes 221192 | tf_op jit(solution)/shard_map/ppermute | solution.py:908
  19.1 8.5 %collective-permute-start.5 = (f32[18,8,128]{2,1,0:T(8,128)S(1)}, f32[18,8,128]{2,1,0:T(8,128)S(1)}, u32[]{:S(2)}, u32[]{:S(2)}) collective-permute-start(f32[18,8,128]{2,1,0:T(8,128)S(1)} %get-tuple-element.104), channel_id=1, source_target_pairs={{0,2},{2,0},{4,6},{6,4},{1,3},{3,1},{5,7},{7,5},{8,10},{10,8},{12,... | collective-permute-start | bytes 221192 | tf_op jit(solution)/shard_map/ppermute | solution.py:908
  19.2 8.4 %collective-permute-start.6 = (f32[18,8,128]{2,1,0:T(8,128)S(1)}, f32[18,8,128]{2,1,0:T(8,128)S(1)}, u32[]{:S(2)}, u32[]{:S(2)}) collective-permute-start(f32[18,8,128]{2,1,0:T(8,128)S(1)} %get-tuple-element.105), channel_id=1, source_target_pairs={{2,4},{4,2},{6,0},{0,6},{3,5},{5,3},{7,1},{1,7},{10,12},{12,10},{1... | collective-permute-start | bytes 221192 | tf_op jit(solution)/shard_map/ppermute | solution.py:908
  23.0 5.5 %collective-permute-start.9 = (f32[56,128]{1,0:T(8,128)S(1)}, f32[56,128]{1,0:T(8,128)S(1)}, u32[]{:S(2)}, u32[]{:S(2)}) collective-permute-start(f32[56,128]{1,0:T(8,128)S(1)} %get-tuple-element.110), channel_id=1, source_target_pairs={{0,8},{8,0},{16,24},{24,16},{1,9},{9,1},{17,25},{25,17},{2,10},{10... | collective-permute-start | bytes 86024 | tf_op jit(solution)/shard_map/ppermute | solution.py:908
  23.0 5.8 %collective-permute-start.10 = (f32[56,128]{1,0:T(8,128)S(1)}, f32[56,128]{1,0:T(8,128)S(1)}, u32[]{:S(2)}, u32[]{:S(2)}) collective-permute-start(f32[56,128]{1,0:T(8,128)S(1)} %get-tuple-element.111), channel_id=1, source_target_pairs={{8,16},{16,8},{24,0},{0,24},{9,17},{17,9},{25,1},{1,25},{10,18},{1... | collective-permute-start | bytes 86024 | tf_op jit(solution)/shard_map/ppermute | solution.py:908
  27.5 1.3 %copy-start.2 = (f32[16,48,144]{2,1,0:T(8,128)S(1)}, f32[16,48,144]{2,1,0:T(8,128)}, u32[]{:S(2)}) copy-start(f32[16,48,144]{2,1,0:T(8,128)} %constant.19.clone.reach) | copy-start | bytes 1327108
  27.6 1.3 %copy-start.8 = (bf16[2,144,128]{2,1,0:T(8,128)(2,1)S(1)}, bf16[2,144,128]{2,1,0:T(8,128)(2,1)}, u32[]{:S(2)}) copy-start(bf16[2,144,128]{2,1,0:T(8,128)(2,1)} %constant.26.clone.basis_z) | copy-start | bytes 221188
  27.6 1.3 %copy-start.9 = (f32[48,144]{1,0:T(8,128)S(1)}, f32[48,144]{1,0:T(8,128)}, u32[]{:S(2)}) copy-start(f32[48,144]{1,0:T(8,128)} %constant.20.clone.middle) | copy-start | bytes 82948
  27.6 1.3 %copy-start.12 = (bf16[32,144]{1,0:T(8,128)(2,1)S(1)}, bf16[32,144]{1,0:T(8,128)(2,1)}, u32[]{:S(2)}) copy-start(bf16[32,144]{1,0:T(8,128)(2,1)} %constant.25.clone.basis_y) | copy-start | bytes 27652
  30.3 7.0 %collective-permute-start.11 = (f32[2,32,128]{2,1,0:T(8,128)S(1)}, f32[2,32,128]{2,1,0:T(8,128)S(1)}, u32[]{:S(2)}, u32[]{:S(2)}) collective-permute-start(f32[2,32,128]{2,1,0:T(8,128)S(1)} %get-tuple-element.125), channel_id=1, source_target_pairs={{0,8},{8,0},{16,24},{24,16},{1,9},{9,1},{17,25},{25,17},{2,10},{10... | collective-permute-start | bytes 98312 | tf_op jit(solution)/shard_map/ppermute | solution.py:908
  31.2 6.1 %collective-permute-start.12 = (f32[2,32,128]{2,1,0:T(8,128)S(1)}, f32[2,32,128]{2,1,0:T(8,128)S(1)}, u32[]{:S(2)}, u32[]{:S(2)}) collective-permute-start(f32[2,32,128]{2,1,0:T(8,128)S(1)} %get-tuple-element.126), channel_id=1, source_target_pairs={{8,16},{16,8},{24,0},{0,24},{9,17},{17,9},{25,1},{1,25},{10,18},{1... | collective-permute-start | bytes 98312 | tf_op jit(solution)/shard_map/ppermute | solution.py:908
  33.7 3.7 %collective-permute-start.13 = (f32[32,128]{1,0:T(8,128)S(1)}, f32[32,128]{1,0:T(8,128)S(1)}, u32[]{:S(2)}, u32[]{:S(2)}) collective-permute-start(f32[32,128]{1,0:T(8,128)S(1)} %get-tuple-element.127), channel_id=1, source_target_pairs={{0,2},{2,0},{4,6},{6,4},{1,3},{3,1},{5,7},{7,5},{8,10},{10,8},{12,... | collective-permute-start | bytes 49160 | tf_op jit(solution)/shard_map/ppermute | solution.py:908
  33.7 3.7 %collective-permute-start.14 = (f32[32,128]{1,0:T(8,128)S(1)}, f32[32,128]{1,0:T(8,128)S(1)}, u32[]{:S(2)}, u32[]{:S(2)}) collective-permute-start(f32[32,128]{1,0:T(8,128)S(1)} %get-tuple-element.128), channel_id=1, source_target_pairs={{2,4},{4,2},{6,0},{0,6},{3,5},{5,3},{7,1},{1,7},{10,12},{12,10},{1... | collective-permute-start | bytes 49160 | tf_op jit(solution)/shard_map/ppermute | solution.py:908
  33.7 3.6 %collective-permute-start.15 = (f32[8,128]{1,0:T(8,128)S(1)}, f32[8,128]{1,0:T(8,128)S(1)}, u32[]{:S(2)}, u32[]{:S(2)}) collective-permute-start(f32[8,128]{1,0:T(8,128)S(1)} %get-tuple-element.129), channel_id=1, source_target_pairs={{0,1},{1,0},{2,3},{3,2},{4,5},{5,4},{6,7},{7,6},{8,9},{9,8},{10,11... | collective-permute-start | bytes 12296 | tf_op jit(solution)/shard_map/ppermute | solution.py:908
  51.0 6.3 %collective-permute-start.16 = (f32[32,128]{1,0:T(8,128)S(1)}, f32[32,128]{1,0:T(8,128)S(1)}, u32[]{:S(2)}, u32[]{:S(2)}) collective-permute-start(f32[32,128]{1,0:T(8,128)S(1)} %get-tuple-element.158), channel_id=1, source_target_pairs={{0,8},{8,0},{16,24},{24,16},{1,9},{9,1},{17,25},{25,17},{2,10},{10... | collective-permute-start | bytes 49160 | tf_op jit(solution)/shard_map/ppermute | solution.py:908
  51.5 5.8 %collective-permute-start.17 = (f32[32,128]{1,0:T(8,128)S(1)}, f32[32,128]{1,0:T(8,128)S(1)}, u32[]{:S(2)}, u32[]{:S(2)}) collective-permute-start(f32[32,128]{1,0:T(8,128)S(1)} %get-tuple-element.159), channel_id=1, source_target_pairs={{8,16},{16,8},{24,0},{0,24},{9,17},{17,9},{25,1},{1,25},{10,18},{1... | collective-permute-start | bytes 49160 | tf_op jit(solution)/shard_map/ppermute | solution.py:908
  53.0 4.4 %collective-permute-start.18 = (f32[32,128]{1,0:T(8,128)S(1)}, f32[32,128]{1,0:T(8,128)S(1)}, u32[]{:S(2)}, u32[]{:S(2)}) collective-permute-start(f32[32,128]{1,0:T(8,128)S(1)} %get-tuple-element.160), channel_id=1, source_target_pairs={{0,2},{2,0},{4,6},{6,4},{1,3},{3,1},{5,7},{7,5},{8,10},{10,8},{12,... | collective-permute-start | bytes 49160 | tf_op jit(solution)/shard_map/ppermute | solution.py:908
  53.0 4.4 %collective-permute-start.19 = (f32[32,128]{1,0:T(8,128)S(1)}, f32[32,128]{1,0:T(8,128)S(1)}, u32[]{:S(2)}, u32[]{:S(2)}) collective-permute-start(f32[32,128]{1,0:T(8,128)S(1)} %get-tuple-element.161), channel_id=1, source_target_pairs={{2,4},{4,2},{6,0},{0,6},{3,5},{5,3},{7,1},{1,7},{10,12},{12,10},{1... | collective-permute-start | bytes 49160 | tf_op jit(solution)/shard_map/ppermute | solution.py:908
  53.7 3.6 %collective-permute-start.20 = (f32[8,128]{1,0:T(8,128)S(1)}, f32[8,128]{1,0:T(8,128)S(1)}, u32[]{:S(2)}, u32[]{:S(2)}) collective-permute-start(f32[8,128]{1,0:T(8,128)S(1)} %get-tuple-element.162), channel_id=1, source_target_pairs={{0,1},{1,0},{2,3},{3,2},{4,5},{5,4},{6,7},{7,6},{8,9},{9,8},{10,11... | collective-permute-start | bytes 12296 | tf_op jit(solution)/shard_map/ppermute | solution.py:908
  58.8 8.2 %collective-permute-start.21 = (f32[32,128]{1,0:T(8,128)S(1)}, f32[32,128]{1,0:T(8,128)S(1)}, u32[]{:S(2)}, u32[]{:S(2)}) collective-permute-start(f32[32,128]{1,0:T(8,128)S(1)} %get-tuple-element.166), channel_id=1, source_target_pairs={{0,8},{8,0},{16,24},{24,16},{1,9},{9,1},{17,25},{25,17},{2,10},{10... | collective-permute-start | bytes 49160 | tf_op jit(solution)/shard_map/ppermute | solution.py:908
  58.9 8.1 %collective-permute-start.22 = (f32[32,128]{1,0:T(8,128)S(1)}, f32[32,128]{1,0:T(8,128)S(1)}, u32[]{:S(2)}, u32[]{:S(2)}) collective-permute-start(f32[32,128]{1,0:T(8,128)S(1)} %get-tuple-element.167), channel_id=1, source_target_pairs={{8,16},{16,8},{24,0},{0,24},{9,17},{17,9},{25,1},{1,25},{10,18},{1... | collective-permute-start | bytes 49160 | tf_op jit(solution)/shard_map/ppermute | solution.py:908
  61.8 5.3 %collective-permute-start.23 = (f32[32,128]{1,0:T(8,128)S(1)}, f32[32,128]{1,0:T(8,128)S(1)}, u32[]{:S(2)}, u32[]{:S(2)}) collective-permute-start(f32[32,128]{1,0:T(8,128)S(1)} %get-tuple-element.168), channel_id=1, source_target_pairs={{0,2},{2,0},{4,6},{6,4},{1,3},{3,1},{5,7},{7,5},{8,10},{10,8},{12,... | collective-permute-start | bytes 49160 | tf_op jit(solution)/shard_map/ppermute | solution.py:908
  61.8 5.3 %collective-permute-start.24 = (f32[32,128]{1,0:T(8,128)S(1)}, f32[32,128]{1,0:T(8,128)S(1)}, u32[]{:S(2)}, u32[]{:S(2)}) collective-permute-start(f32[32,128]{1,0:T(8,128)S(1)} %get-tuple-element.169), channel_id=1, source_target_pairs={{2,4},{4,2},{6,0},{0,6},{3,5},{5,3},{7,1},{1,7},{10,12},{12,10},{1... | collective-permute-start | bytes 49160 | tf_op jit(solution)/shard_map/ppermute | solution.py:908
  63.4 3.6 %collective-permute-start.25 = (f32[8,128]{1,0:T(8,128)S(1)}, f32[8,128]{1,0:T(8,128)S(1)}, u32[]{:S(2)}, u32[]{:S(2)}) collective-permute-start(f32[8,128]{1,0:T(8,128)S(1)} %get-tuple-element.170), channel_id=1, source_target_pairs={{0,1},{1,0},{2,3},{3,2},{4,5},{5,4},{6,7},{7,6},{8,9},{9,8},{10,11... | collective-permute-start | bytes 12296 | tf_op jit(solution)/shard_map/ppermute | solution.py:908
